TPU v7x, 32 devices: a whole 2x2x4 slice. The times are simulated.
32 devices in a mesh: seq: 16 (over z, y, core), chan: 2 (over x).
Axes of the slice: x: 2, y: 2, z: 4, core: 2. Of those that a mesh axis runs over, the one named last changes fastest.
Arguments:
- v_stream: bfloat16 [4096, 8192], P('chan', 'seq'), may hold values from -6 to 6
- gate_one: bfloat16 [4096, 8192], P('chan', 'seq'), may hold values from -6 to 6
- gate_two: bfloat16 [4096, 8192], P('chan', 'seq'), may hold values from -6 to 6
- short_filter: float32 [4096, 128], P('chan'), may hold values from -0.5 to 0.5
- decay_rates: float32 [4096, 16], P('chan'), may hold values from 6.1035157e-06 to 0.03
- residues: float32 [4096, 16], P('chan'), may hold values from -1.5 to 1.5
- skip_bias: float32 [4096], P('chan'), may hold values from -3 to 3
Outputs:
- hyena_out: bfloat16 [4096, 8192], P('chan', 'seq')
All inputs are finite; a program needn't handle non-finite values.
Results may differ from a plain program's by a relative error of at most 0.005.
Values may be sent and summed in bfloat16 or wider, within the bound.
No kernel may reach another device: no remote copies, remote signals or barrier semaphores. Data moves between devices by JAX's collectives and lax.ppermute only.
A program may use at most 192 MiB of HBM per device.

v0:
```python
import math

import jax
import jax.numpy as jnp
from jax import lax
from jax.sharding import PartitionSpec as P

SPLIT3 = lax.Precision.HIGH


def passed_along(block, axis, distance):
    devices = range(lax.axis_size(axis))
    route = [(i - distance, i) for i in devices if i - distance in devices]
    return lax.ppermute(block, axis, route)


def dft_table(row_count, col_count, period):
    row_index = lax.broadcasted_iota(jnp.int32, (row_count, col_count), 0)
    col_index = lax.broadcasted_iota(jnp.int32, (row_count, col_count), 1)
    phase = (row_index * col_index % period).astype(jnp.float32) * (2.0 * math.pi / period)
    return (jnp.cos(phase), -jnp.sin(phase))


def split_table(table):
    high_part = table.astype(jnp.bfloat16)
    back_wide = lax.optimization_barrier(high_part).astype(jnp.float32)
    low_part = (table - back_wide).astype(jnp.bfloat16)
    return (high_part, low_part)


def narrow_einsum(form, table, data):
    high_part, low_part = split_table(table)
    return jnp.einsum(form, high_part, data, preferred_element_type=jnp.float32) + jnp.einsum(
        form, low_part, data, preferred_element_type=jnp.float32
    )


def split_factor(length_total):
    factor = 2
    for candidate in range(2, math.isqrt(length_total) + 1, 2):
        if length_total % candidate == 0:
            factor = candidate
    return factor


def forward_dft(signal, rows_a, rows_b):
    width_here = signal.shape[0]
    grid = signal.reshape(width_here, rows_a // 2, rows_b)
    left_re, left_im = dft_table(rows_a, rows_a // 2, rows_a)
    if signal.dtype == jnp.bfloat16:
        first_re = narrow_einsum("kn,cnm->ckm", left_re, grid)
        first_im = narrow_einsum("kn,cnm->ckm", left_im, grid)
    else:
        first_re = jnp.einsum("kn,cnm->ckm", left_re, grid, precision=SPLIT3)
        first_im = jnp.einsum("kn,cnm->ckm", left_im, grid, precision=SPLIT3)
    twist_re, twist_im = dft_table(rows_a, rows_b, rows_a * rows_b)
    middle_re = first_re * twist_re - first_im * twist_im
    middle_im = first_re * twist_im + first_im * twist_re
    right_re, right_im = dft_table(rows_b, rows_b, rows_b)
    out_re = jnp.einsum("ckm,mj->ckj", middle_re, right_re, precision=SPLIT3) - jnp.einsum(
        "ckm,mj->ckj", middle_im, right_im, precision=SPLIT3
    )
    out_im = jnp.einsum("ckm,mj->ckj", middle_re, right_im, precision=SPLIT3) + jnp.einsum(
        "ckm,mj->ckj", middle_im, right_re, precision=SPLIT3
    )
    return (out_re, out_im)


def inverse_dft(spec_re, spec_im, rows_a, rows_b):
    width_here = spec_re.shape[0]
    right_re, right_im = dft_table(rows_b, rows_b, rows_b)
    back_re = jnp.einsum("ckj,jm->ckm", spec_re, right_re, precision=SPLIT3) + jnp.einsum(
        "ckj,jm->ckm", spec_im, right_im, precision=SPLIT3
    )
    back_im = jnp.einsum("ckj,jm->ckm", spec_im, right_re, precision=SPLIT3) - jnp.einsum(
        "ckj,jm->ckm", spec_re, right_im, precision=SPLIT3
    )
    twist_re, twist_im = dft_table(rows_a, rows_b, rows_a * rows_b)
    turned_re = back_re * twist_re + back_im * twist_im
    turned_im = back_im * twist_re - back_re * twist_im
    left_re, left_im = dft_table(rows_a, rows_a // 2, rows_a)
    signal = jnp.einsum("kn,ckm->cnm", left_re, turned_re, precision=SPLIT3) + jnp.einsum(
        "kn,ckm->cnm", left_im, turned_im, precision=SPLIT3
    )
    return signal.reshape(width_here, rows_a // 2 * rows_b) / float(rows_a * rows_b)


def causal_conv(signal, kernel_values):
    length_here = signal.shape[1]
    rows_a = split_factor(2 * length_here)
    rows_b = 2 * length_here // rows_a
    signal_re, signal_im = forward_dft(signal, rows_a, rows_b)
    kernel_re, kernel_im = forward_dft(kernel_values, rows_a, rows_b)
    product_re = signal_re * kernel_re - signal_im * kernel_im
    product_im = signal_re * kernel_im + signal_im * kernel_re
    return inverse_dft(product_re, product_im, rows_a, rows_b)


def causal_taps(extended, filter_taps):
    channel_count = extended.shape[0]
    high_taps, low_taps = split_table(jnp.flip(filter_taps, axis=1))
    lhs = extended[None]

    def apply_taps(taps):
        return lax.conv_general_dilated(
            lhs,
            taps[:, None, :],
            (1,),
            "VALID",
            feature_group_count=channel_count,
            dimension_numbers=("NCH", "OIH", "NCH"),
            preferred_element_type=jnp.float32,
        )[0]

    return apply_taps(high_taps) + apply_taps(low_taps)


def rim_mixed(v_stream, gate_one, short_filter):
    tokens_here = v_stream.shape[1]
    filter_len = short_filter.shape[1]
    tail_rows = v_stream[:, tokens_here - (filter_len - 1) :]
    before = passed_along(tail_rows, "seq", 1)
    extended = jnp.concatenate([before, v_stream], axis=1)
    return (gate_one.astype(jnp.float32) * causal_taps(extended, short_filter)).astype(jnp.bfloat16)


def on_device(v_stream, gate_one, gate_two, short_filter, decay_rates, residues, skip_bias):
    channels, tokens_here = v_stream.shape
    shards = lax.axis_size("seq")
    chan_width = channels // shards
    seq_total = tokens_here * shards
    first_chan = lax.axis_index("seq") * chan_width
    mixed_here = rim_mixed(v_stream, gate_one, short_filter)
    moved = lax.all_to_all(
        mixed_here.reshape(shards, chan_width, tokens_here),
        "seq",
        split_axis=0,
        concat_axis=2,
        tiled=True,
    )
    mixed = moved.reshape(chan_width, seq_total)
    local_rates = lax.dynamic_slice_in_dim(decay_rates, first_chan, chan_width, 0)
    local_weights = lax.dynamic_slice_in_dim(residues, first_chan, chan_width, 0)
    local_bias = lax.dynamic_slice_in_dim(skip_bias, first_chan, chan_width, 0)
    positions = jnp.arange(seq_total, dtype=jnp.float32)
    scaled_full = local_weights * jnp.sqrt(2.0 * local_rates + 2.0 / seq_total)
    decay = jnp.exp(-local_rates[:, :, None] * positions[None, None, :])
    filter_values = jnp.einsum("cm,cmt->ct", scaled_full, decay, precision=SPLIT3)
    long_conv = causal_conv(mixed, filter_values)
    skipped = long_conv + local_bias[:, None] * mixed.astype(jnp.float32)
    returned = lax.all_to_all(
        skipped.reshape(1, chan_width, seq_total), "seq", split_axis=2, concat_axis=0, tiled=True
    )
    skipped_back = returned.reshape(channels, tokens_here)
    return (gate_two.astype(jnp.float32) * skipped_back).astype(jnp.bfloat16)


def solution(mesh):
    in_specs = (
        P("chan", "seq"),
        P("chan", "seq"),
        P("chan", "seq"),
        P("chan", None),
        P("chan", None),
        P("chan", None),
        P("chan"),
    )
    out_specs = P("chan", "seq")
    return jax.shard_map(
        on_device, mesh=mesh, in_specs=in_specs, out_specs=out_specs, check_vma=False
    )
```

profile of v0, /device:TPU:0, one launch (start us, length us, event | category | flops | bytes accessed | tf_op | source)
XLA Modules:
  0.0 549.2 jit_solution(9074071362469505081)
XLA Ops:
  3.6 7.5 %rev.4 = f32[2048,128]{1,0:T(8,128)S(1)} reverse(f32[2048,128]{1,0:T(8,128)} %param.10), dimensions={1} | reverse | bytes 2097152 | tf_op jit(solution)/shard_map/jit(_flip)/rev | solution.py:101
  14.3 24.6 %fusion = f32[128,1,8192]{2,1,0:T(1,128)} fusion(f32[128,16,1]{1,2,0:T(1,128)S(1)} %copy.87, f32[128,16]{1,0:T(8,128)S(1)} %copy.69), kind=kOutput, calls=%fused_computation | convolution fusion | flops 117440512 | bytes 4210688 | tf_op jit(solution)/shard_map/cm,cmt->ct/dot_general | solution.py:148
  48.8 8.3 %copy.59 = bf16[1,2048,639]{1,0,2:T(2,128)(2,1)} copy(bf16[1,2048,639]{2,1,0:T(8,128)(2,1)S(1)} %maximum_bitcast_fusion) | data formatting | bytes 5234688 | tf_op jit(solution)/shard_map/broadcast_in_dim | solution.py:102
  57.1 66.5 %fusion.192 = f32[1,2048,512]{1,0,2:T(1,128)S(1)} fusion(bf16[1,2048,639]{1,0,2:T(2,128)(2,1)} %copy.59, bf16[2048,1,128]{0,1,2:T(2,128)(2,1)} %copy.62), kind=kOutput, calls=%fused_computation.205 | convolution fusion | flops 268435456 | bytes 7335936 | tf_op jit(solution)/shard_map/conv_general_dilated | solution.py:105
  123.6 82.4 %convolution_add_fusion = f32[1,2048,512]{1,0,2:T(1,128)S(1)} fusion(f32[1,2048,512]{1,0,2:T(1,128)S(1)} %fusion.192, bf16[1,2048,639]{1,0,2:T(2,128)(2,1)S(1)} %copy-done.8, bf16[2048,1,128]{0,1,2:T(2,128)(2,1)S(1)} %copy-done.10), kind=kOutput, calls=%fused_computation.27 | convolution fusion | flops 269484032 | bytes 11530240 | tf_op jit(solution)/shard_map/conv_general_dilated | solution.py:105
  208.7 7.6 %all-to-all-start = ((bf16[16,128,512]{1,2,0:T(8,128)(2,1)}), bf16[16,128,512]{1,2,0:T(8,128)(2,1)S(1)}, u32[]{:S(2)}, u32[]{:S(2)}) async-start(bf16[16,128,512]{1,2,0:T(8,128)(2,1)} %copy_bitcast_fusion.1), calls=%async_computation | async-start | bytes 4194304 | tf_op jit(solution)/shard_map/all_to_all | solution.py:134
  224.2 6.7 %fusion.75 = f32[128,128,128]{2,1,0:T(8,128)S(1)} fusion(f32[128,64,128]{2,1,0:T(8,128)S(1)} %bitcast.160), kind=kOutput, calls=%fused_computation.99 | convolution fusion | flops 805429248 | bytes 12582912 | tf_op jit(solution)/shard_map/kn,cnm->ckm/dot_general | solution.py:55
  230.9 6.9 %fusion.78 = f32[128,128,128]{2,1,0:T(8,128)S(1)} fusion(f32[128,64,128]{2,1,0:T(8,128)S(1)} %bitcast.161), kind=kOutput, calls=%fused_computation.102 | convolution fusion | flops 805421056 | bytes 12582912 | tf_op jit(solution)/shard_map/kn,cnm->ckm/dot_general | solution.py:54
  237.8 9.3 %fusion.30 = f32[128,128,128]{2,1,0:T(8,128)} fusion(f32[128,128,128]{2,1,0:T(8,128)S(1)} %fusion.75, f32[128,128,128]{2,1,0:T(8,128)S(1)} %fusion.78, f32[128,128]{0,1:T(8,128)S(1)} %copy.66, f32[128,128]{0,1:T(8,128)S(1)} %copy.65), kind=kOutput, calls=%fused_computation.45 | convolution fusion | flops 1617149952 | bytes 25296896 | tf_op jit(solution)/shard_map/ckm,mj->ckj/dot_general | solution.py:60
  247.1 9.5 %fusion.34 = f32[128,128,128]{2,1,0:T(8,128)} fusion(f32[128,128,128]{2,1,0:T(8,128)S(1)} %fusion.75, f32[128,128,128]{2,1,0:T(8,128)S(1)} %fusion.78, f32[128,128]{0,1:T(8,128)S(1)} %copy.66, f32[128,128]{0,1:T(8,128)S(1)} %copy.65), kind=kOutput, calls=%fused_computation.47 | convolution fusion | flops 1617133568 | bytes 25296896 | tf_op jit(solution)/shard_map/ckm,mj->ckj/dot_general | solution.py:60
  256.6 9.3 %fusion.28 = f32[128,128,128]{2,1,0:T(8,128)} fusion(f32[128,128,128]{2,1,0:T(8,128)S(1)} %fusion.75, f32[128,128,128]{2,1,0:T(8,128)S(1)} %fusion.78, f32[128,128]{0,1:T(8,128)S(1)} %copy.66, f32[128,128]{0,1:T(8,128)S(1)} %copy.65), kind=kOutput, calls=%fused_computation.44 | convolution fusion | flops 1617133568 | bytes 25296896 | tf_op jit(solution)/shard_map/ckm,mj->ckj/dot_general | solution.py:63
  284.4 13.8 %fusion.8 = (f32[128,128,128]{1,2,0:T(8,128)}, f32[128,128,128]{1,2,0:T(8,128)S(1)}) fusion(f32[128,128]{0,1:T(8,128)S(1)} %copy.66, f32[128,128]{0,1:T(8,128)S(1)} %copy.65, f32[128,128,128]{2,1,0:T(8,128)} %fusion.96, f32[128,128,128]{2,1,0:T(8,128)} %fusion.100, f32[128,128,128]{2,1,0:T(8,128)} %fusion.93, bf16[128,64,128]{2,1,0:T(8,128)(2,1)S(1)} %copy.101), kind=kOutput, calls=%fused_computation.14 | convolution fusion | flops 285343744 | bytes 44171264 | tf_op jit(solution)/shard_map/kn,cnm->ckm/dot_general | solution.py:33
  298.2 12.1 %fusion.52 = f32[128,128,128]{2,1,0:T(8,128)} fusion(f32[128,128,128]{1,2,0:T(8,128)} %get-tuple-element.7), kind=kOutput, calls=%fused_computation.70 | convolution fusion | flops 1610858496 | bytes 16777216 | tf_op jit(solution)/shard_map/ckm,mj->ckj/dot_general | solution.py:60
  310.3 9.3 %fusion.59 = f32[128,128,128]{2,1,0:T(8,128)} fusion(f32[128,128,128]{1,2,0:T(8,128)S(1)} %copy-done.3), kind=kOutput, calls=%fused_computation.77 | convolution fusion | flops 1610842112 | bytes 16777216 | tf_op jit(solution)/shard_map/ckm,mj->ckj/dot_general | solution.py:63
  319.7 9.5 %fusion.49 = f32[128,128,128]{2,1,0:T(8,128)} fusion(f32[128,128,128]{1,2,0:T(8,128)S(1)} %get-tuple-element.8), kind=kOutput, calls=%fused_computation.67 | convolution fusion | flops 1610858496 | bytes 16777216 | tf_op jit(solution)/shard_map/ckm,mj->ckj/dot_general | solution.py:63
  329.1 9.3 %fusion.62 = f32[128,128,128]{2,1,0:T(8,128)} fusion(f32[128,128,128]{1,2,0:T(8,128)S(1)} %get-tuple-element.8), kind=kOutput, calls=%fused_computation.80 | convolution fusion | flops 1610842112 | bytes 16777216 | tf_op jit(solution)/shard_map/ckm,mj->ckj/dot_general | solution.py:60
  338.5 31.7 %multiply_subtract_fusion = (f32[128,128,128]{2,1,0:T(8,128)}, f32[128,128,128]{2,1,0:T(8,128)}) fusion(f32[128,128,128]{2,1,0:T(8,128)} %fusion.28, f32[128,128,128]{2,1,0:T(8,128)} %fusion.49, f32[128,128,128]{2,1,0:T(8,128)} %fusion.59, f32[128,128,128]{2,1,0:T(8,128)} %fusion.34, f32[128,128,128]{2,1,0:T(8,128)} %fusion.30, ...), kind=kOutput, calls=%fused_computation.26 | convolution fusion | flops 1638121472 | bytes 92405760 | tf_op jit(solution)/shard_map/ckm,mj->ckj/dot_general | solution.py:63
  370.2 7.8 %fusion.46 = f32[128,128,128]{1,2,0:T(8,128)S(1)} fusion(f32[128,128,128]{2,1,0:T(8,128)} %get-tuple-element.6), kind=kOutput, calls=%fused_computation.64 | convolution fusion | flops 1610858496 | bytes 16777216 | tf_op jit(solution)/shard_map/ckj,jm->ckm/dot_general | solution.py:72
  378.0 6.2 %fusion.54 = f32[128,128,128]{1,2,0:T(8,128)} fusion(f32[128,128,128]{2,1,0:T(8,128)S(1)} %copy-done.4), kind=kOutput, calls=%fused_computation.72 | convolution fusion | flops 1610842112 | bytes 16777216 | tf_op jit(solution)/shard_map/ckj,jm->ckm/dot_general | solution.py:75
  384.2 6.2 %fusion.44 = f32[128,128,128]{1,2,0:T(8,128)} fusion(f32[128,128,128]{2,1,0:T(8,128)S(1)} %bitcast.159), kind=kOutput, calls=%fused_computation.62 | convolution fusion | flops 1610858496 | bytes 16777216 | tf_op jit(solution)/shard_map/ckj,jm->ckm/dot_general | solution.py:75
  390.4 6.3 %fusion.56 = f32[128,128,128]{1,2,0:T(8,128)} fusion(f32[128,128,128]{2,1,0:T(8,128)S(1)} %bitcast.159), kind=kOutput, calls=%fused_computation.74 | convolution fusion | flops 1610842112 | bytes 16777216 | tf_op jit(solution)/shard_map/ckj,jm->ckm/dot_general | solution.py:72
  396.7 16.3 %fusion.9 = f32[128,128,64]{1,2,0:T(8,128)} fusion(f32[128,128]{0,1:T(8,128)S(1)} %copy.66, f32[128,128]{0,1:T(8,128)S(1)} %copy.65, f32[128,128,128]{1,2,0:T(8,128)} %fusion.54, f32[128,128,128]{1,2,0:T(8,128)} %fusion.44, f32[128,128,128]{1,2,0:T(8,128)} %fusion.56, f32[128,128,128]{1,2,0:T(8,128)S(1)} %fusion.46), kind=kOutput, calls=%fused_computation.17 | convolution fusion | flops 815915008 | bytes 37879808 | tf_op jit(solution)/shard_map/kn,ckm->cnm/dot_general | solution.py:82
  413.0 19.6 %multiply_bitcast_fusion = f32[128,64,128]{2,1,0:T(8,128)} fusion(f32[128,128,64]{1,2,0:T(8,128)} %fusion.9, f32[128,128]{0,1:T(8,128)S(1)} %copy.66, f32[128,128]{0,1:T(8,128)S(1)} %copy.65, f32[128,128,128]{1,2,0:T(8,128)} %fusion.54, f32[128,128,128]{1,2,0:T(8,128)} %fusion.44, f32[128,128,128]{1,2,0:T(8,128)} %fusion.56, f32[128,128,128]{1,2,0:T(8,128)} %copy-done.2), kind=kOutput, calls=%fused_computation.35 | convolution fusion | flops 818003968 | bytes 42074112 | tf_op jit(solution)/shard_map/kn,ckm->cnm/dot_general | solution.py:82
  440.8 98.3 %all_to_all.30 = f32[1,128,8192]{1,0,2:T(1,128)} all-to-all(f32[1,128,8192]{1,0,2:T(1,128)S(1)} %bitcast.164), channel_id=1, replica_groups=mesh['seq'=16,'chan'=2] {'seq'}, dimensions={2} | all-to-all | bytes 8388608 | tf_op jit(solution)/shard_map/all_to_all | solution.py:151
  (61 shorter events, 63.4 us)
Async XLA Ops:
  1.2 44.5 %collective-permute-start = (bf16[2048,127]{1,0:T(8,128)(2,1)S(1)}, bf16[2048,127]{1,0:T(8,128)(2,1)S(1)}, u32[]{:S(2)}, u32[]{:S(2)}) collective-permute-start(bf16[2048,127]{1,0:T(8,128)(2,1)S(1)} %slice.3), channel_id=1, source_target_pairs={{0,2},{2,4},{4,6},{6,8},{8,10},{10,12},{12,14},{14,16},{16,18},{18... | collective-permute-start | bytes 1560584 | tf_op jit(solution)/shard_map/ppermute | solution.py:14
  57.1 66.5 %copy-start.8 = (bf16[1,2048,639]{1,0,2:T(2,128)(2,1)S(1)}, bf16[1,2048,639]{1,0,2:T(2,128)(2,1)}, u32[]{:S(2)}) copy-start(bf16[1,2048,639]{1,0,2:T(2,128)(2,1)} %copy.59) | copy-start | bytes 7852036
  57.1 66.5 %copy-start.10 = (bf16[2048,1,128]{0,1,2:T(2,128)(2,1)S(1)}, bf16[2048,1,128]{0,1,2:T(2,128)(2,1)}, u32[]{:S(2)}) copy-start(bf16[2048,1,128]{0,1,2:T(2,128)(2,1)} %copy.60) | copy-start | bytes 1572868
  123.6 82.4 %copy-start.7 = (bf16[2048,512]{0,1:T(8,128)(2,1)S(1)}, bf16[2048,512]{0,1:T(8,128)(2,1)}, u32[]{:S(2)}) copy-start(bf16[2048,512]{0,1:T(8,128)(2,1)} %copy.58) | copy-start | bytes 6291460
  208.7 57.2 %all-to-all-start = ((bf16[16,128,512]{1,2,0:T(8,128)(2,1)}), bf16[16,128,512]{1,2,0:T(8,128)(2,1)S(1)}, u32[]{:S(2)}, u32[]{:S(2)}) async-start(bf16[16,128,512]{1,2,0:T(8,128)(2,1)} %copy_bitcast_fusion.1), calls=%async_computation | async-start | bytes 4194304 | tf_op jit(solution)/shard_map/all_to_all | solution.py:134
  230.9 25.7 %copy-start = (f32[128,128,128]{2,1,0:T(8,128)}, f32[128,128,128]{2,1,0:T(8,128)S(1)}, u32[]{:S(2)}) copy-start(f32[128,128,128]{2,1,0:T(8,128)S(1)} %fusion.75) | copy-start | bytes 25165828
  237.8 18.8 %copy-start.1 = (f32[128,128,128]{2,1,0:T(8,128)}, f32[128,128,128]{2,1,0:T(8,128)S(1)}, u32[]{:S(2)}) copy-start(f32[128,128,128]{2,1,0:T(8,128)S(1)} %fusion.78) | copy-start | bytes 25165828
  265.9 9.2 %copy-start.11 = (bf16[128,64]{0,1:T(8,128)(2,1)S(1)}, bf16[128,64]{0,1:T(8,128)(2,1)}, u32[]{:S(2)}) copy-start(bf16[128,64]{0,1:T(8,128)(2,1)} %fusion.109) | copy-start | bytes 49156
  265.9 1.3 copy-start.5
  298.2 12.1 %copy-start.3 = (f32[128,128,128]{1,2,0:T(8,128)S(1)}, f32[128,128,128]{1,2,0:T(8,128)}, u32[]{:S(2)}) copy-start(f32[128,128,128]{1,2,0:T(8,128)} %get-tuple-element.7) | copy-start | bytes 25165828
  370.1 7.8 %copy-start.4 = (f32[128,128,128]{2,1,0:T(8,128)S(1)}, f32[128,128,128]{2,1,0:T(8,128)}, u32[]{:S(2)}) copy-start(f32[128,128,128]{2,1,0:T(8,128)} %get-tuple-element.6) | copy-start | bytes 25165828
  370.1 14.0 %slice-start = ((s8[8388608]{0:T(1024)(128)(4,1)}), s8[4194304]{0:T(1024)(128)(4,1)S(1)}, s32[]{:S(2)}) async-start(s8[8388608]{0:T(1024)(128)(4,1)} %bitcast.158), calls=%async_computation.2 | async-start | bytes 8388608
  378.0 18.7 %copy-start.2 = (f32[128,128,128]{1,2,0:T(8,128)}, f32[128,128,128]{1,2,0:T(8,128)S(1)}, u32[]{:S(2)}) copy-start(f32[128,128,128]{1,2,0:T(8,128)S(1)} %fusion.46) | copy-start | bytes 25165828
  378.0 6.2 %slice-start.1 = ((s8[8388608]{0:T(1024)(128)(4,1)}), s8[4194304]{0:T(1024)(128)(4,1)S(1)}, s32[]{:S(2)}) async-start(s8[8388608]{0:T(1024)(128)(4,1)} %bitcast.158), calls=%async_computation.3 | async-start | bytes 8388608
  432.6 5.6 %copy-start.6 = (bf16[16,128,512]{1,2,0:T(8,128)(2,1)S(1)}, bf16[16,128,512]{1,2,0:T(8,128)(2,1)}, u32[]{:S(2)}) copy-start(bf16[16,128,512]{1,2,0:T(8,128)(2,1)} %copy-done.5) | copy-start | bytes 6291460
  440.8 103.7 %copy-start.9 = (bf16[2048,512]{1,0:T(8,128)(2,1)S(1)}, bf16[2048,512]{1,0:T(8,128)(2,1)}, u32[]{:S(2)}) copy-start(bf16[2048,512]{1,0:T(8,128)(2,1)} %param.9) | copy-start | bytes 6291460
where the time goes:
time: 557 us; the launch traced here: 549 us
  matrix products  377 us (68%)
  blocking collectives  98.3 us (18%)
  local copies, waits for them, and re-layouts  48.1 us (9%)
  other arithmetic  14.9 us (3%)
  starting transfers between devices  9.98 us (2%)
    conv_general_dilated x2, matrix products, apply_taps(): lax.conv_general_dilated(lhs, taps[:, None, :], (1,), 'VALID', feature_gr...  149 us
    all_to_all x1, blocking collectives, on_device(): lax.all_to_all(skipped.reshape(1, chan_width, seq_total), 'seq', split_ax...  98.3 us
    dot_general x2, matrix products, forward_dft(): jnp.einsum('ckm,mj->ckj', middle_re, right_im, precision=SPLIT3)  41.1 us
    dot_general x1, matrix products, on_device(): jnp.einsum('cm,cmt->ct', scaled_full, decay, precision=SPLIT3)  24.6 us
    dot_general x2, matrix products, forward_dft(): jnp.einsum('ckm,mj->ckj', middle_im, right_im, precision=SPLIT3)  21.4 us
    dot_general x1, matrix products, inverse_dft(): jnp.einsum('kn,ckm->cnm', left_re, turned_re, precision=SPLIT3)  19.6 us
    dot_general x2, matrix products, forward_dft(): jnp.einsum('ckm,mj->ckj', middle_re, right_re, precision=SPLIT3)  18.8 us
    dot_general x2, matrix products, forward_dft(): jnp.einsum('ckm,mj->ckj', middle_im, right_re, precision=SPLIT3)  18.7 us
  transfers between devices with their start and end apart: 2, of which 0 were waited for; matrix products, arithmetic and copies ran while one was open for 17% of the time, Pallas kernels for 0%

commit v1 on v0

v1 whole, which is shorter than its diff:
```python
import functools
import math

import jax
import jax.numpy as jnp
import numpy as np
from jax import lax
from jax.experimental import pallas as pl
from jax.experimental.pallas import tpu as pltpu
from jax.sharding import PartitionSpec as P

LANES = 128
SUBS = 8
TILE = LANES * SUBS
BLOCK = 128
ROWS = 256
STEPS = 8
F32, BF16 = jnp.float32, jnp.bfloat16


def halves(table):
    high = table.astype(jnp.bfloat16)
    low = (table - high.astype(np.float64)).astype(jnp.bfloat16)
    return high, low


def window_tables():
    size = 2 * BLOCK
    phase = 2.0 * math.pi / size * np.outer(np.arange(size), np.arange(BLOCK) + 0.5)
    forward = np.concatenate([np.cos(phase), -np.sin(phase)], axis=1)
    inverse = forward[BLOCK:].T / BLOCK
    return halves(forward), halves(inverse)


def mm(left, right):
    return jnp.dot(left, right, preferred_element_type=F32)


def split(value):
    high = value.astype(BF16)
    return high, (value - high.astype(F32)).astype(BF16)


def apply_window(window, spectrum, fwd_hi, fwd_lo, inv_hi, inv_lo):
    image = mm(window, fwd_hi[...]) + mm(window, fwd_lo[...])
    re, im = image[:, :BLOCK], image[:, BLOCK:]
    h_re, h_im = spectrum[:, :BLOCK], spectrum[:, BLOCK:]
    product = jnp.concatenate([re * h_re - im * h_im, re * h_im + im * h_re], axis=1)
    high, low = split(product)
    return mm(high, inv_hi[...]) + mm(low, inv_hi[...]) + mm(high, inv_lo[...])


def put_mixed(store, first_row, block_at, short, gate):
    mixed = (gate.astype(F32) * short).astype(BF16).astype(F32)
    for piece in range(ROWS // LANES):
        group = first_row // LANES + piece
        turned = mixed[piece * LANES : (piece + 1) * LANES].T
        store[pl.ds(block_at * BLOCK * SUBS + group, BLOCK, stride=SUBS), :] = turned


def end_states(store, mixed_ref, rates_ref, start):
    modes = rates_ref.shape[0]
    steps = store.shape[0] // SUBS
    decay = [jnp.exp(-rates_ref[mode]) for mode in range(modes)]

    def turn(index, states):
        at = pl.multiple_of(index * STEPS * SUBS, STEPS * SUBS)
        values = store[pl.ds(at, STEPS * SUBS), :]
        mixed_ref[pl.ds(at, STEPS * SUBS), :] = values.astype(BF16)
        for step in range(STEPS):
            value = values[step * SUBS : (step + 1) * SUBS]
            states = tuple(d * s + value for d, s in zip(decay, states))
        return states

    return lax.fori_loop(0, steps // STEPS, turn, start)


def inner_kernel(v_ref, gate_ref, taps_ref, rates_ref, fwd_hi, fwd_lo, inv_hi, inv_lo, spec_ref, mixed_ref, state_ref, store):
    windows = v_ref.shape[1] // BLOCK - 1
    for first in range(0, TILE, ROWS):
        rows = slice(first, first + ROWS)
        tap_hi, tap_lo = split(taps_ref[rows])
        head_hi, head_lo = fwd_hi[:BLOCK], fwd_lo[:BLOCK]
        spectrum = mm(tap_hi, head_hi) + mm(tap_lo, head_hi) + mm(tap_hi, head_lo)
        spec_ref[rows] = spectrum
        for window in range(windows):
            at = window * BLOCK
            short = apply_window(v_ref[rows, at : at + 2 * BLOCK], spectrum, fwd_hi, fwd_lo, inv_hi, inv_lo)
            put_mixed(store, first, window, short, gate_ref[rows, at + BLOCK : at + 2 * BLOCK])
    zeros = tuple(jnp.zeros((SUBS, LANES), F32) for _ in range(rates_ref.shape[0]))
    for mode, state in enumerate(end_states(store, mixed_ref, rates_ref, zeros)):
        state_ref[mode] = state


def rim_kernel(inner, before_ref, v_ref, gate_ref, spec_ref, rates_ref, inner_ref, fwd_hi, fwd_lo, inv_hi, inv_lo, mixed_ref, state_ref, store):
    for first in range(0, TILE, ROWS):
        rows = slice(first, first + ROWS)
        window = jnp.concatenate([before_ref[rows], v_ref[rows]], axis=1)
        short = apply_window(window, spec_ref[rows], fwd_hi, fwd_lo, inv_hi, inv_lo)
        put_mixed(store, first, 0, short, gate_ref[rows])
    zeros = tuple(jnp.zeros((SUBS, LANES), F32) for _ in range(rates_ref.shape[0]))
    for mode, state in enumerate(end_states(store, mixed_ref, rates_ref, zeros)):
        state_ref[mode] = jnp.exp(-float(inner) * rates_ref[mode]) * state + inner_ref[mode]


def outer_kernel(seq_total, rim_ref, inner_ref, gate_ref, rates_ref, weights_ref, bias_ref, start_ref, out_ref, store):
    modes = rates_ref.shape[0]
    decay = [jnp.exp(-rates_ref[mode]) for mode in range(modes)]
    scaled = [weights_ref[mode] * jnp.sqrt(2.0 * rates_ref[mode] + 2.0 / seq_total) for mode in range(modes)]
    bias = bias_ref[...]
    states = tuple(start_ref[mode] for mode in range(modes))
    first = 0
    for source in (rim_ref, inner_ref):

        def turn(index, states, source=source, first=first):
            at = pl.multiple_of(index * STEPS * SUBS, STEPS * SUBS)
            values = source[pl.ds(at, STEPS * SUBS), :].astype(F32)
            sums = []
            for step in range(STEPS):
                value = values[step * SUBS : (step + 1) * SUBS]
                states = tuple(d * s + value for d, s in zip(decay, states))
                parts = [c * s for c, s in zip(scaled, states)] + [bias * value]
                while len(parts) > 1:
                    parts = [sum(parts[i : i + 2][1:], parts[i]) for i in range(0, len(parts), 2)]
                sums.append(parts[0])
            store[pl.ds(first * SUBS + at, STEPS * SUBS), :] = jnp.concatenate(sums, axis=0)
            return states

        count = source.shape[0] // SUBS
        states = lax.fori_loop(0, count // STEPS, turn, states)
        first += count
    for group in range(SUBS):
        rows = slice(group * LANES, (group + 1) * LANES)
        for block in range(first // BLOCK):
            cols = slice(block * BLOCK, (block + 1) * BLOCK)
            turned = store[pl.ds(block * BLOCK * SUBS + group, BLOCK, stride=SUBS), :].T
            out_ref[rows, cols] = (gate_ref[rows, cols].astype(F32) * turned).astype(BF16)


def call(kernel, tiles, in_specs, out_specs, out_shape, steps, flops, moved):
    return pl.pallas_call(
        kernel,
        grid=(tiles,),
        in_specs=in_specs,
        out_specs=out_specs,
        out_shape=out_shape,
        scratch_shapes=[pltpu.VMEM((steps * SUBS, LANES), F32)],
        compiler_params=pltpu.CompilerParams(vmem_limit_bytes=48 << 20),
        cost_estimate=pl.CostEstimate(flops=flops, bytes_accessed=moved, transcendentals=0),
    )


def rows_spec(width, column=0):
    return pl.BlockSpec((TILE, width), lambda i: (i, column))


def modes_spec(modes):
    return pl.BlockSpec((modes, SUBS, LANES), lambda i: (0, i, 0))


def steps_spec(steps):
    return pl.BlockSpec((None, steps * SUBS, LANES), lambda i: (i, 0, 0))


def whole_spec(table):
    return pl.BlockSpec(table.shape, lambda i: (0, 0))


def on_device(v_stream, gate_one, gate_two, short_filter, decay_rates, residues, skip_bias):
    real_channels, tokens = v_stream.shape
    modes = decay_rates.shape[1]
    shards = lax.axis_size("seq")
    tail = v_stream[:, tokens - BLOCK :]
    before = lax.ppermute(tail, "seq", [(i, i + 1) for i in range(shards - 1)])
    extra = -real_channels % TILE

    def padded(array):
        return jnp.pad(array, ((0, extra),) + ((0, 0),) * (array.ndim - 1)) if extra else array

    v_stream, gate_one, gate_two, short_filter = map(padded, (v_stream, gate_one, gate_two, short_filter))
    decay_rates, residues, skip_bias, before = map(padded, (decay_rates, residues, skip_bias, before))
    channels = real_channels + extra
    tiles, groups = channels // TILE, channels // LANES
    rates = decay_rates.T.reshape(modes, groups, LANES)
    weights = residues.T.reshape(modes, groups, LANES)
    bias = skip_bias.reshape(groups, LANES)
    (fwd_hi, fwd_lo), (inv_hi, inv_lo) = window_tables()
    tables = [jnp.asarray(t) for t in (fwd_hi, fwd_lo, inv_hi, inv_lo)]
    table_specs = [whole_spec(t) for t in tables]
    inner = tokens - BLOCK
    shape = jax.ShapeDtypeStruct
    spectrum, inner_mixed, inner_state = call(
        inner_kernel,
        tiles,
        [rows_spec(tokens), rows_spec(tokens), rows_spec(BLOCK), modes_spec(modes)] + table_specs,
        [rows_spec(2 * BLOCK), steps_spec(inner), modes_spec(modes)],
        [
            shape((channels, 2 * BLOCK), F32),
            shape((tiles, inner * SUBS, LANES), BF16),
            shape((modes, groups, LANES), F32),
        ],
        inner,
        channels * inner * 2600,
        channels * tokens * 8,
    )(v_stream, gate_one, short_filter, rates, *tables)
    rim_mixed, end_state = call(
        functools.partial(rim_kernel, inner),
        tiles,
        [rows_spec(BLOCK), rows_spec(BLOCK), rows_spec(BLOCK), rows_spec(2 * BLOCK), modes_spec(modes), modes_spec(modes)]
        + table_specs,
        [steps_spec(BLOCK), modes_spec(modes)],
        [shape((tiles, BLOCK * SUBS, LANES), BF16), shape((modes, groups, LANES), F32)],
        BLOCK,
        channels * BLOCK * 2600,
        channels * BLOCK * 16,
    )(before, v_stream, gate_one, spectrum, rates, inner_state, *tables)

    me = lax.axis_index("seq")
    pieces = end_state.reshape(shards, -1, LANES)
    moved = lax.all_to_all(pieces, "seq", split_axis=0, concat_axis=0, tiled=True)
    own_rates = lax.dynamic_index_in_dim(rates.reshape(shards, -1, LANES), me, 0, keepdims=False)
    reach = jnp.exp(-float(tokens) * own_rates)
    carried = [jnp.zeros_like(reach)]
    for shard in range(shards - 1):
        carried.append(reach * carried[-1] + moved[shard])
    start = lax.all_to_all(jnp.stack(carried), "seq", split_axis=0, concat_axis=0, tiled=True)
    start = start.reshape(modes, groups, LANES)

    hyena_out = call(
        functools.partial(outer_kernel, tokens * shards),
        tiles,
        [
            steps_spec(BLOCK),
            steps_spec(inner),
            rows_spec(tokens),
            modes_spec(modes),
            modes_spec(modes),
            pl.BlockSpec((SUBS, LANES), lambda i: (i, 0)),
            modes_spec(modes),
        ],
        rows_spec(tokens),
        shape((channels, tokens), BF16),
        tokens,
        channels * tokens * 70,
        channels * tokens * 6,
    )(rim_mixed, inner_mixed, gate_two, rates, weights, bias, start)
    return hyena_out[:real_channels]


def solution(mesh):
    in_specs = (
        P("chan", "seq"),
        P("chan", "seq"),
        P("chan", "seq"),
        P("chan", None),
        P("chan", None),
        P("chan", None),
        P("chan"),
    )
    out_specs = P("chan", "seq")
    return jax.shard_map(
        on_device, mesh=mesh, in_specs=in_specs, out_specs=out_specs, check_vma=False
    )
```

time: 557 us -> 82.2 us (0.15); the launches traced: 549 us -> 81.7 us
  matrix products: 377 us -> 0 us
  blocking collectives: 98.3 us -> 0 us
  local copies, waits for them, and re-layouts: 48.1 us -> 11.2 us
  Pallas kernels: 0 us -> 32.8 us
  waiting for transfers between devices: 0.01 us -> 15.2 us
  other arithmetic: 14.9 us -> 9.18 us
    dot_general x21 -> x0, matrix products: 228 us -> none  [the longest x2 41.1 us: forward_dft(): jnp.einsum('ckm,mj->ckj', middle_re, right_im, precision=SPLIT3)]
    conv_general_dilated x2 -> x0, matrix products: 149 us -> none  [apply_taps(): lax.conv_general_dilated(lhs, taps[:, None, :], (1,), 'VALID', feature_gr...]
    all_to_all x1 -> x0, blocking collectives: 98.3 us -> none  [on_device(): lax.all_to_all(skipped.reshape(1, chan_width, seq_total), 'seq', split_ax...]
    pallas_call x0 -> x3, Pallas kernels: none -> 32.8 us  [the longest x1 14.4 us: on_device(): call(inner_kernel, tiles, [rows_spec(tokens), rows_spec(tokens), rows_spe...]
    all_to_all x1 -> x2, waiting for transfers between devices: 0.01 us -> 15.2 us  [the longest x1 7.85 us: on_device(): lax.all_to_all(jnp.stack(carried), 'seq', split_axis=0, concat_axis=0, ti...]
    broadcast_in_dim x3 -> x0, local copies, waits for them, and re-layouts: 12.4 us -> none  [the longest x1 8.3 us: causal_taps(): lhs = extended[None]]
    unnamed x1 -> x14, other arithmetic: 0.01 us -> 8.57 us
    rev x1 -> x0, local copies, waits for them, and re-layouts: 7.5 us -> none  [causal_taps(): high_taps, low_taps = split_table(jnp.flip(filter_taps, axis=1))]
  transfers between devices with their start and end apart: 2 -> 3, of which waited for: 0 -> 2; matrix products, arithmetic and copies ran while one was open for 17% -> 2% of each run, Pallas kernels for 0% -> 18%
where the time goes in v1:
time: 82.2 us; the launch traced here: 81.7 us
  Pallas kernels  32.8 us (40%)
  waiting for transfers between devices  15.2 us (18%)
  starting transfers between devices  13.1 us (16%)
  local copies, waits for them, and re-layouts  11.2 us (14%)
  other arithmetic  9.18 us (11%)
    pallas_call x1, Pallas kernels, on_device(): call(inner_kernel, tiles, [rows_spec(tokens), rows_spec(tokens), rows_spe...  14.4 us
    pallas_call x1, Pallas kernels, on_device(): call(functools.partial(outer_kernel, tokens * shards), tiles, [steps_spec...  12 us
    unnamed x29, local copies, waits for them, and re-layouts  10.2 us
    unnamed x14, other arithmetic  8.57 us
    all_to_all x1, waiting for transfers between devices, on_device(): lax.all_to_all(jnp.stack(carried), 'seq', split_axis=0, concat_axis=0, ti...  7.85 us
    all_to_all x1, waiting for transfers between devices, on_device(): lax.all_to_all(pieces, 'seq', split_axis=0, concat_axis=0, tiled=True)  7.33 us
    all_to_all x1, starting transfers between devices, on_device(): lax.all_to_all(pieces, 'seq', split_axis=0, concat_axis=0, tiled=True)  7.19 us
    pallas_call x1, Pallas kernels, on_device(): call(functools.partial(rim_kernel, inner), tiles, [rows_spec(BLOCK), rows...  6.41 us
  transfers between devices with their start and end apart: 3, of which 2 were waited for; matrix products, arithmetic and copies ran while one was open for 2% of the time, Pallas kernels for 18%

profile of v1, /device:TPU:0, one launch (start us, length us, event | category | flops | bytes accessed | tf_op | source)
XLA Modules:
  0.0 81.7 jit_solution(13019412420791108762)
XLA Ops:
  0.0 1.1 %slice.48 = bf16[2048,128]{1,0:T(8,128)(2,1)S(1)} slice(bf16[2048,512]{1,0:T(8,128)(2,1)} %v_ref.3), slice={[0:2048], [384:512]} | slice | bytes 1048576 | tf_op jit(solution)/shard_map/slice | solution.py:173
  1.1 2.4 %collective-permute-start = (bf16[2048,128]{1,0:T(8,128)(2,1)S(1)}, bf16[2048,128]{1,0:T(8,128)(2,1)S(1)}, u32[]{:S(2)}, u32[]{:S(2)}) collective-permute-start(bf16[2048,128]{1,0:T(8,128)(2,1)S(1)} %slice.48), channel_id=1, source_target_pairs={{0,2},{2,4},{4,6},{6,8},{8,10},{10,12},{12,14},{14,16},{16,18},{18... | collective-permute-start | bytes 1572872 | tf_op jit(solution)/shard_map/ppermute | solution.py:174
  3.5 0.9 %copy.12 = f32[2,8,16,128]{3,2,1,0:T(8,128)S(1)} copy(f32[2,8,16,128]{3,1,2,0:T(8,128)} %bitcast.27) | data formatting | bytes 262144
  4.4 0.9 %copy-done.6 = bf16[256,256]{1,0:T(8,128)(2,1)S(1)} copy-done((bf16[256,256]{1,0:T(8,128)(2,1)S(1)}, bf16[256,256]{1,0:T(8,128)(2,1)}, u32[]{:S(2)}) %copy-start.6) | copy-done | bytes 131096
  5.3 0.9 %copy-done.7 = bf16[256,256]{1,0:T(8,128)(2,1)S(1)} copy-done((bf16[256,256]{1,0:T(8,128)(2,1)S(1)}, bf16[256,256]{1,0:T(8,128)(2,1)}, u32[]{:S(2)}) %copy-start.7) | copy-done | bytes 131096
  6.2 0.8 %copy-done.8 = bf16[256,128]{1,0:T(8,128)(2,1)S(1)} copy-done((bf16[256,128]{1,0:T(8,128)(2,1)S(1)}, bf16[256,128]{1,0:T(8,128)(2,1)}, u32[]{:S(2)}) %copy-start.8) | copy-done | bytes 65560
  7.1 0.8 %copy-done.9 = bf16[256,128]{1,0:T(8,128)(2,1)S(1)} copy-done((bf16[256,128]{1,0:T(8,128)(2,1)S(1)}, bf16[256,128]{1,0:T(8,128)(2,1)}, u32[]{:S(2)}) %copy-start.9) | copy-done | bytes 65560
  7.9 1.2 %copy-done.11 = f32[2048,128]{1,0:T(8,128)S(1)} copy-done((f32[2048,128]{1,0:T(8,128)S(1)}, f32[2048,128]{1,0:T(8,128)}, u32[]{:S(2)}) %copy-start.11) | copy-done | bytes 1048600
  9.1 14.4 %shard_map.109 = (f32[2048,256]{1,0:T(8,128)S(1)}, bf16[2,3072,128]{2,1,0:T(8,128)(2,1)S(1)}, f32[16,16,128]{2,1,0:T(8,128)S(1)}) custom-call(bf16[2048,512]{1,0:T(8,128)(2,1)} %v_ref.3, bf16[2048,512]{1,0:T(8,128)(2,1)} %gate_ref.4, f32[2048,128]{1,0:T(8,128)S(1)} %copy-done.11, f32[16,16,128]{2,1,0:T(8,128)S(1)} %bitcast.7, ...), custom_call_target="tpu_custom_call" | custom-call | flops 2044723200 | bytes 8388608 | tf_op jit(solution)/shard_map/pallas_call | solution.py:192
  23.5 1.3 %copy-done.2 = f32[2048,256]{1,0:T(8,128)} copy-done((f32[2048,256]{1,0:T(8,128)}, f32[2048,256]{1,0:T(8,128)S(1)}, u32[]{:S(2)}) %copy-start.2) | copy-done | bytes 2097176
  24.9 1.2 %copy-done.4 = bf16[2,3072,128]{2,1,0:T(8,128)(2,1)} copy-done((bf16[2,3072,128]{2,1,0:T(8,128)(2,1)}, bf16[2,3072,128]{2,1,0:T(8,128)(2,1)S(1)}, u32[]{:S(2)}) %copy-start.4) | copy-done | bytes 1572888
  26.1 6.4 %shard_map.110 = (bf16[2,1024,128]{2,1,0:T(8,128)(2,1)S(1)}, f32[16,16,128]{2,1,0:T(8,128)}) custom-call(bf16[2048,128]{1,0:T(8,128)(2,1)S(1)} %collective-permute-done.before_ref, bf16[2048,512]{1,0:T(8,128)(2,1)S(1)} %copy-done, bf16[2048,512]{1,0:T(8,128)(2,1)S(1)} %copy-done.1, f32[2048,256]{1,0:T(8,128)} %copy-done.2, f32[16,16,128]{2,1,0:T(8,128)S(1)} %bitcast.8, ...), custom_call_target="tpu_custom_call" | custom-call | flops 681574400 | bytes 4194304 | tf_op jit(solution)/shard_map/pallas_call | solution.py:206
  32.5 7.2 %all-to-all-start = ((f32[16,16,128]{2,1,0:T(8,128)}), f32[16,16,128]{2,1,0:T(8,128)S(1)}, u32[]{:S(2)}, u32[]{:S(2)}) async-start(f32[16,16,128]{2,1,0:T(8,128)} %get-tuple-element.14), calls=%async_computation | async-start | bytes 262144 | tf_op jit(solution)/shard_map/all_to_all | solution.py:220
  40.3 7.3 %all-to-all-done = f32[16,16,128]{2,1,0:T(8,128)S(1)} async-done(((f32[16,16,128]{2,1,0:T(8,128)}), f32[16,16,128]{2,1,0:T(8,128)S(1)}, u32[]{:S(2)}, u32[]{:S(2)}) %all-to-all-start) | async-done | bytes 131104 | tf_op jit(solution)/shard_map/all_to_all | solution.py:220
  48.8 0.6 constant_dynamic-update-slice_fusion.12
  49.4 0.6 constant_dynamic-update-slice_fusion.11
  50.7 0.6 constant_dynamic-update-slice_fusion.9
  54.3 0.6 constant_dynamic-update-slice_fusion.3
  55.6 0.6 constant_dynamic-update-slice_fusion.1
  56.2 0.6 constant_dynamic-update-slice_fusion
  56.8 3.5 %all-to-all-start.1 = ((f32[16,16,128]{2,1,0:T(8,128)}), f32[16,16,128]{2,1,0:T(8,128)S(1)}, u32[]{:S(2)}, u32[]{:S(2)}) async-start(f32[16,16,128]{2,1,0:T(8,128)} %constant_dynamic-update-slice_fusion), calls=%async_computation.1 | async-start | bytes 262144 | tf_op jit(solution)/shard_map/all_to_all | solution.py:226
  60.3 7.9 %all-to-all-done.1.start_ref = f32[16,16,128]{2,1,0:T(8,128)S(1)} async-done(((f32[16,16,128]{2,1,0:T(8,128)}), f32[16,16,128]{2,1,0:T(8,128)S(1)}, u32[]{:S(2)}, u32[]{:S(2)}) %all-to-all-start.1) | async-done | bytes 131104 | tf_op jit(solution)/shard_map/all_to_all | solution.py:226
  68.2 1.4 %copy-done.5 = bf16[2,3072,128]{2,1,0:T(8,128)(2,1)S(1)} copy-done((bf16[2,3072,128]{2,1,0:T(8,128)(2,1)S(1)}, bf16[2,3072,128]{2,1,0:T(8,128)(2,1)}, u32[]{:S(2)}) %copy-start.5) | copy-done | bytes 1572888
  69.6 12.0 %shard_map.111 = bf16[2048,512]{1,0:T(8,128)(2,1)} custom-call(bf16[2,1024,128]{2,1,0:T(8,128)(2,1)S(1)} %get-tuple-element.12.rim_ref, bf16[2,3072,128]{2,1,0:T(8,128)(2,1)S(1)} %copy-done.5, bf16[2048,512]{1,0:T(8,128)(2,1)S(1)} %copy-done.3, f32[16,16,128]{2,1,0:T(8,128)S(1)} %bitcast.24, f32[16,16,128]{2,1,0:T(8,128)S(1)} %bitcast.25, ...), custom_call_target="tpu_custom_call" | custom-call | flops 73400320 | bytes 6291456 | tf_op jit(solution)/shard_map/pallas_call | solution.py:229
  (30 shorter events, 6.2 us)
Async XLA Ops:
  1.1 24.9 %collective-permute-start = (bf16[2048,128]{1,0:T(8,128)(2,1)S(1)}, bf16[2048,128]{1,0:T(8,128)(2,1)S(1)}, u32[]{:S(2)}, u32[]{:S(2)}) collective-permute-start(bf16[2048,128]{1,0:T(8,128)(2,1)S(1)} %slice.48), channel_id=1, source_target_pairs={{0,2},{2,4},{4,6},{6,8},{8,10},{10,12},{12,14},{14,16},{16,18},{18... | collective-permute-start | bytes 1572872 | tf_op jit(solution)/shard_map/ppermute | solution.py:174
  4.4 0.9 %copy-start.6 = (bf16[256,256]{1,0:T(8,128)(2,1)S(1)}, bf16[256,256]{1,0:T(8,128)(2,1)}, u32[]{:S(2)}) copy-start(bf16[256,256]{1,0:T(8,128)(2,1)} %constant.25.clone.fwd_hi) | copy-start | bytes 393220
  5.3 0.9 %copy-start.7 = (bf16[256,256]{1,0:T(8,128)(2,1)S(1)}, bf16[256,256]{1,0:T(8,128)(2,1)}, u32[]{:S(2)}) copy-start(bf16[256,256]{1,0:T(8,128)(2,1)} %constant.26.clone.fwd_lo) | copy-start | bytes 393220
  6.2 0.8 %copy-start.8 = (bf16[256,128]{1,0:T(8,128)(2,1)S(1)}, bf16[256,128]{1,0:T(8,128)(2,1)}, u32[]{:S(2)}) copy-start(bf16[256,128]{1,0:T(8,128)(2,1)} %constant.27.clone.inv_hi) | copy-start | bytes 196612
  7.1 0.8 %copy-start.9 = (bf16[256,128]{1,0:T(8,128)(2,1)S(1)}, bf16[256,128]{1,0:T(8,128)(2,1)}, u32[]{:S(2)}) copy-start(bf16[256,128]{1,0:T(8,128)(2,1)} %constant.28.clone.inv_lo) | copy-start | bytes 196612
  7.9 1.2 %copy-start.11 = (f32[2048,128]{1,0:T(8,128)S(1)}, f32[2048,128]{1,0:T(8,128)}, u32[]{:S(2)}) copy-start(f32[2048,128]{1,0:T(8,128)} %taps_ref.1) | copy-start | bytes 3145732
  9.1 16.9 %copy-start = (bf16[2048,512]{1,0:T(8,128)(2,1)S(1)}, bf16[2048,512]{1,0:T(8,128)(2,1)}, u32[]{:S(2)}) copy-start(bf16[2048,512]{1,0:T(8,128)(2,1)} %v_ref.3) | copy-start | bytes 6291460
  9.1 16.9 %copy-start.1 = (bf16[2048,512]{1,0:T(8,128)(2,1)S(1)}, bf16[2048,512]{1,0:T(8,128)(2,1)}, u32[]{:S(2)}) copy-start(bf16[2048,512]{1,0:T(8,128)(2,1)} %gate_ref.4) | copy-start | bytes 6291460
  23.5 1.3 %copy-start.2 = (f32[2048,256]{1,0:T(8,128)}, f32[2048,256]{1,0:T(8,128)S(1)}, u32[]{:S(2)}) copy-start(f32[2048,256]{1,0:T(8,128)S(1)} %get-tuple-element.10.spec_ref) | copy-start | bytes 6291460
  24.8 1.2 %copy-start.4 = (bf16[2,3072,128]{2,1,0:T(8,128)(2,1)}, bf16[2,3072,128]{2,1,0:T(8,128)(2,1)S(1)}, u32[]{:S(2)}) copy-start(bf16[2,3072,128]{2,1,0:T(8,128)(2,1)S(1)} %get-tuple-element.13.inner_ref) | copy-start | bytes 4718596
  26.0 34.3 %copy-start.12 = (f32[2048,16]{0,1:T(8,128)S(1)}, f32[2048,16]{0,1:T(8,128)}, u32[]{:S(2)}) copy-start(f32[2048,16]{0,1:T(8,128)} %param.16) | copy-start | bytes 393220
  26.0 42.2 %copy-start.3 = (bf16[2048,512]{1,0:T(8,128)(2,1)S(1)}, bf16[2048,512]{1,0:T(8,128)(2,1)}, u32[]{:S(2)}) copy-start(bf16[2048,512]{1,0:T(8,128)(2,1)} %gate_ref.5) | copy-start | bytes 6291460
  26.0 42.2 %copy-start.10 = (f32[2048]{0:T(1024)S(1)}, f32[2048]{0:T(1024)}, u32[]{:S(2)}) copy-start(f32[2048]{0:T(1024)} %param.17) | copy-start | bytes 24580
  32.5 15.1 %all-to-all-start = ((f32[16,16,128]{2,1,0:T(8,128)}), f32[16,16,128]{2,1,0:T(8,128)S(1)}, u32[]{:S(2)}, u32[]{:S(2)}) async-start(f32[16,16,128]{2,1,0:T(8,128)} %get-tuple-element.14), calls=%async_computation | async-start | bytes 262144 | tf_op jit(solution)/shard_map/all_to_all | solution.py:220
  56.8 11.4 %all-to-all-start.1 = ((f32[16,16,128]{2,1,0:T(8,128)}), f32[16,16,128]{2,1,0:T(8,128)S(1)}, u32[]{:S(2)}, u32[]{:S(2)}) async-start(f32[16,16,128]{2,1,0:T(8,128)} %constant_dynamic-update-slice_fusion), calls=%async_computation.1 | async-start | bytes 262144 | tf_op jit(solution)/shard_map/all_to_all | solution.py:226
  68.2 1.4 %copy-start.5 = (bf16[2,3072,128]{2,1,0:T(8,128)(2,1)S(1)}, bf16[2,3072,128]{2,1,0:T(8,128)(2,1)}, u32[]{:S(2)}) copy-start(bf16[2,3072,128]{2,1,0:T(8,128)(2,1)} %copy-done.4) | copy-start | bytes 4718596

commit v2 on v1

v2 whole, which is shorter than its diff:
```python
import functools
import math

import jax
import jax.numpy as jnp
import numpy as np
from jax import lax
from jax.experimental import pallas as pl
from jax.experimental.pallas import tpu as pltpu
from jax.sharding import PartitionSpec as P

LANES = 128
SUBS = 8
TILE = LANES * SUBS
BLOCK = 128
ROWS = 256
STEPS = 8
F32, BF16 = jnp.float32, jnp.bfloat16


def halves(table):
    high = table.astype(jnp.bfloat16)
    low = (table - high.astype(np.float64)).astype(jnp.bfloat16)
    return high, low


def window_tables():
    size = 2 * BLOCK
    phase = 2.0 * math.pi / size * np.outer(np.arange(size), np.arange(BLOCK) + 0.5)
    forward = np.concatenate([np.cos(phase), -np.sin(phase)], axis=1)
    signs = np.tile((-1.0) ** np.arange(BLOCK), 2)
    inverse = forward[BLOCK:].T / BLOCK
    even = np.concatenate(halves(forward[:BLOCK]), axis=0)
    odd = np.concatenate(halves(forward[:BLOCK] * signs), axis=0)
    back = np.concatenate(halves(inverse), axis=1)
    return np.concatenate([even, odd, back], axis=1)


EVEN, ODD, BACK = (slice(i * 2 * BLOCK, (i + 1) * 2 * BLOCK) for i in range(3))


def mm(left, right):
    return jnp.dot(left, right, preferred_element_type=F32)


def split(value):
    high = value.astype(BF16)
    return high, (value - high.astype(F32)).astype(BF16)


def twice(block):
    return jnp.concatenate([block, block], axis=1)


def parts(image):
    return image[:, :BLOCK], image[:, BLOCK:]


def apply_window(earlier, later, spectrum, tables):
    (e_re, e_im), (l_re, l_im), (h_re, h_im) = parts(earlier), parts(later), parts(spectrum)
    re, im = e_re + l_im, e_im - l_re
    high, low = split(jnp.concatenate([re * h_re - im * h_im, re * h_im + im * h_re], axis=1))
    both = mm(high, tables[:, BACK])
    return both[:, :BLOCK] + both[:, BLOCK:] + mm(low, tables[:, BACK][:, :BLOCK])


def put_mixed(store, first_row, block_at, short, gate):
    mixed = (gate.astype(F32) * short).astype(BF16).astype(F32)
    for piece in range(ROWS // LANES):
        group = first_row // LANES + piece
        turned = mixed[piece * LANES : (piece + 1) * LANES].T
        store[pl.ds(block_at * BLOCK * SUBS + group, BLOCK, stride=SUBS), :] = turned


def end_states(store, mixed_ref, rates_ref):
    modes = rates_ref.shape[0]
    steps = store.shape[0] // SUBS
    decay = [jnp.exp(-rates_ref[mode]) for mode in range(modes)]

    def turn(index, states):
        at = pl.multiple_of(index * STEPS * SUBS, STEPS * SUBS)
        values = store[pl.ds(at, STEPS * SUBS), :]
        mixed_ref[pl.ds(at, STEPS * SUBS), :] = values.astype(BF16)
        for step in range(STEPS):
            value = values[step * SUBS : (step + 1) * SUBS]
            states = tuple(d * s + value for d, s in zip(decay, states))
        return states

    zeros = tuple(jnp.zeros((SUBS, LANES), F32) for _ in range(modes))
    return lax.fori_loop(0, steps // STEPS, turn, zeros)


def inner_kernel(v_ref, gate_ref, taps_ref, rates_ref, tables, spec_ref, mixed_ref, state_ref, store):
    blocks = v_ref.shape[1] // BLOCK
    sign = 1.0 - 2.0 * (lax.broadcasted_iota(jnp.int32, (1, 2 * BLOCK), 1) % 2).astype(F32)
    for first in range(0, TILE, ROWS):
        rows = slice(first, first + ROWS)
        tap_hi, tap_lo = split(taps_ref[rows])
        spectrum = mm(twice(tap_hi), tables[:, EVEN]) + mm(tap_lo, tables[:BLOCK, EVEN])
        turned = spectrum * sign
        spec_ref[rows] = turned
        earlier = mm(twice(v_ref[rows, :BLOCK]), tables[:, EVEN])
        for block in range(1, blocks):
            at = slice(block * BLOCK, (block + 1) * BLOCK)
            later = mm(twice(v_ref[rows, at]), tables[:, ODD if block % 2 else EVEN])
            short = apply_window(earlier, later, spectrum if block % 2 else turned, tables)
            put_mixed(store, first, block - 1, short, gate_ref[rows, at])
            earlier = later
    for mode, state in enumerate(end_states(store, mixed_ref, rates_ref)):
        state_ref[mode] = state


def rim_kernel(inner, place_ref, before_ref, v_ref, gate_ref, spec_ref, rates_ref, inner_ref, tables, *rest):
    mixed_ref, *piece_refs, store, ends = rest
    for first in range(0, TILE, ROWS):
        rows = slice(first, first + ROWS)
        earlier = mm(twice(before_ref[rows]), tables[:, ODD])
        later = mm(twice(v_ref[rows]), tables[:, EVEN])
        short = apply_window(earlier, later, spec_ref[rows], tables)
        put_mixed(store, first, 0, short, gate_ref[rows])
    for mode, state in enumerate(end_states(store, mixed_ref, rates_ref)):
        ends[mode] = jnp.exp(-float(inner) * rates_ref[mode]) * state + inner_ref[mode]
    plane = len(piece_refs)
    share = ends.shape[0] // plane
    for ahead, piece in enumerate(piece_refs):
        piece[...] = ends[pl.ds(lax.rem(place_ref[0] + ahead, plane) * share, share)]


def decayed(rates, positions):
    return jnp.exp(-lax.convert_element_type(positions, F32) * rates)


def total_kernel(tokens, place_ref, rates_ref, *rest):
    *ends, total_ref = rest
    plane, share = len(ends), total_ref.shape[0]
    place = place_ref[0]
    for mode in range(share):
        rates = rates_ref[place * share + mode]
        total = None
        for behind, end in enumerate(ends):
            owner = lax.rem(place - behind + plane, plane)
            term = decayed(rates, tokens * (plane - 1 - owner)) * end[mode]
            total = term if total is None else total + term
        total_ref[mode] = total


def start_kernel(tokens, planes, place_ref, rates_ref, *rest):
    plane = (len(rest) - (planes - 1)) // 2
    ends, totals, starts = rest[:plane], rest[plane : plane + planes - 1], rest[plane + planes - 1 :]
    share = starts[0].shape[0]
    place = place_ref[0]
    for mode in range(share):
        rates = rates_ref[place * share + mode]
        base = totals[0][mode]
        for behind in range(1, planes - 1):
            base = base + jnp.exp(-float(tokens * plane * behind) * rates) * totals[behind][mode]
        for ahead in range(plane):
            target = lax.rem(place + ahead, plane)
            start = decayed(rates, tokens * target) * base
            for behind, end in enumerate(ends):
                owner = lax.rem(place - behind + plane, plane)
                gap = target - 1 - owner
                term = decayed(rates, tokens * jnp.maximum(gap, 0)) * end[mode]
                start = start + jnp.where(gap >= 0, term, 0.0)
            starts[ahead][mode] = start


def outer_kernel(seq_total, place_ref, rim_ref, inner_ref, gate_ref, rates_ref, weights_ref, bias_ref, *rest):
    *start_refs, out_ref, store, begin = rest
    modes, plane = rates_ref.shape[0], len(start_refs)
    share = modes // plane
    for behind, ref in enumerate(start_refs):
        begin[pl.ds(lax.rem(place_ref[0] - behind + plane, plane) * share, share)] = ref[...]
    decay = [jnp.exp(-rates_ref[mode]) for mode in range(modes)]
    scaled = [weights_ref[mode] * jnp.sqrt(2.0 * rates_ref[mode] + 2.0 / seq_total) for mode in range(modes)]
    bias = bias_ref[...]
    states = tuple(begin[mode] for mode in range(modes))
    first = 0
    for source in (rim_ref, inner_ref):

        def turn(index, states, source=source, first=first):
            at = pl.multiple_of(index * STEPS * SUBS, STEPS * SUBS)
            values = source[pl.ds(at, STEPS * SUBS), :].astype(F32)
            sums = []
            for step in range(STEPS):
                value = values[step * SUBS : (step + 1) * SUBS]
                states = tuple(d * s + value for d, s in zip(decay, states))
                terms = [c * s for c, s in zip(scaled, states)] + [bias * value]
                while len(terms) > 1:
                    terms = [sum(terms[i : i + 2][1:], terms[i]) for i in range(0, len(terms), 2)]
                sums.append(terms[0])
            store[pl.ds(first * SUBS + at, STEPS * SUBS), :] = jnp.concatenate(sums, axis=0)
            return states

        count = source.shape[0] // SUBS
        states = lax.fori_loop(0, count // STEPS, turn, states)
        first += count
    for group in range(SUBS):
        rows = slice(group * LANES, (group + 1) * LANES)
        for block in range(first // BLOCK):
            cols = slice(block * BLOCK, (block + 1) * BLOCK)
            turned = store[pl.ds(block * BLOCK * SUBS + group, BLOCK, stride=SUBS), :].T
            out_ref[rows, cols] = (gate_ref[rows, cols].astype(F32) * turned).astype(BF16)


SCALAR = pl.BlockSpec(memory_space=pltpu.SMEM)


def call(kernel, tiles, in_specs, out_specs, out_shape, scratch, flops, moved, room):
    return pl.pallas_call(
        kernel,
        grid=(tiles,),
        in_specs=in_specs,
        out_specs=out_specs,
        out_shape=out_shape,
        scratch_shapes=scratch,
        compiler_params=pltpu.CompilerParams(vmem_limit_bytes=room << 20),
        cost_estimate=pl.CostEstimate(flops=flops, bytes_accessed=moved, transcendentals=0),
    )


def rows_spec(width, column=0):
    return pl.BlockSpec((TILE, width), lambda i: (i, column))


def modes_spec(modes):
    return pl.BlockSpec((modes, SUBS, LANES), lambda i: (0, i, 0))


def steps_spec(steps):
    return pl.BlockSpec((None, steps * SUBS, LANES), lambda i: (i, 0, 0))


def steps_scratch(steps):
    return pltpu.VMEM((steps * SUBS, LANES), F32)


def on_device(v_stream, gate_one, gate_two, short_filter, decay_rates, residues, skip_bias):
    real_channels, tokens = v_stream.shape
    modes = decay_rates.shape[1]
    shards = lax.axis_size("seq")
    before = lax.ppermute(v_stream[:, tokens - BLOCK :], "seq", [(i, i + 1) for i in range(shards - 1)])
    extra = -real_channels % TILE

    def padded(array):
        return jnp.pad(array, ((0, extra),) + ((0, 0),) * (array.ndim - 1)) if extra else array

    v_stream, gate_one, gate_two, short_filter = map(padded, (v_stream, gate_one, gate_two, short_filter))
    decay_rates, residues, skip_bias, before = map(padded, (decay_rates, residues, skip_bias, before))
    channels = real_channels + extra
    tiles, groups = channels // TILE, channels // LANES
    rates = decay_rates.T.reshape(modes, groups, LANES)
    weights = residues.T.reshape(modes, groups, LANES)
    bias = skip_bias.reshape(groups, LANES)
    tables = jnp.asarray(window_tables())
    tables_spec = pl.BlockSpec(tables.shape, lambda i: (0, 0))
    planes = 4 if shards % 4 == 0 else 1
    plane = shards // planes
    share = modes // plane
    place = (lax.axis_index("seq") % plane).astype(jnp.int32).reshape(1)
    inner = tokens - BLOCK
    shape = jax.ShapeDtypeStruct
    per_mode = shape((modes, groups, LANES), F32)
    piece = shape((share, groups, LANES), F32)
    spectrum, inner_mixed, inner_state = call(
        inner_kernel,
        tiles,
        [rows_spec(tokens), rows_spec(tokens), rows_spec(BLOCK), modes_spec(modes), tables_spec],
        [rows_spec(2 * BLOCK), steps_spec(inner), modes_spec(modes)],
        [shape((channels, 2 * BLOCK), F32), shape((tiles, inner * SUBS, LANES), BF16), per_mode],
        [steps_scratch(inner)],
        channels * inner * 2600,
        channels * tokens * 8,
        56,
    )(v_stream, gate_one, short_filter, rates, tables)
    rim_mixed, *ends = call(
        functools.partial(rim_kernel, inner),
        tiles,
        [SCALAR, rows_spec(BLOCK), rows_spec(BLOCK), rows_spec(BLOCK), rows_spec(2 * BLOCK)]
        + [modes_spec(modes), modes_spec(modes), tables_spec],
        [steps_spec(BLOCK)] + [modes_spec(share)] * plane,
        [shape((tiles, BLOCK * SUBS, LANES), BF16)] + [piece] * plane,
        [steps_scratch(BLOCK), pltpu.VMEM((modes, SUBS, LANES), F32)],
        channels * BLOCK * 2600,
        channels * BLOCK * 16,
        40,
    )(place, before, v_stream, gate_one, spectrum, rates, inner_state, tables)

    def round_plane(pieces):
        turned = [pieces[0]]
        for ahead in range(1, plane):
            route = [(g * plane + i, g * plane + (i + ahead) % plane) for g in range(planes) for i in range(plane)]
            turned.append(lax.ppermute(pieces[ahead], "seq", route))
        return turned

    arrived = round_plane(ends)
    pieces_spec, rates_spec = modes_spec(share), modes_spec(modes)
    total = call(
        functools.partial(total_kernel, tokens),
        tiles,
        [SCALAR, rates_spec] + [pieces_spec] * plane,
        pieces_spec,
        piece,
        [],
        1 << 20,
        1 << 18,
        4,
    )(place, rates, *arrived)
    totals = [
        lax.ppermute(total, "seq", [(i, i + step * plane) for i in range(shards - step * plane)])
        for step in range(1, planes)
    ]
    starts = call(
        functools.partial(start_kernel, tokens, planes),
        tiles,
        [SCALAR, rates_spec] + [pieces_spec] * (plane + planes - 1),
        [pieces_spec] * plane,
        [piece] * plane,
        [],
        1 << 20,
        1 << 18,
        4,
    )(place, rates, *arrived, *totals)
    starts = round_plane(starts)

    hyena_out = call(
        functools.partial(outer_kernel, tokens * shards),
        tiles,
        [SCALAR, steps_spec(BLOCK), steps_spec(inner), rows_spec(tokens), rates_spec, rates_spec]
        + [pl.BlockSpec((SUBS, LANES), lambda i: (i, 0))]
        + [pieces_spec] * plane,
        rows_spec(tokens),
        shape((channels, tokens), BF16),
        [steps_scratch(tokens), pltpu.VMEM((modes, SUBS, LANES), F32)],
        channels * tokens * 70,
        channels * tokens * 6,
        40,
    )(place, rim_mixed, inner_mixed, gate_two, rates, weights, bias, *starts)
    return hyena_out[:real_channels]


def solution(mesh):
    in_specs = (
        P("chan", "seq"),
        P("chan", "seq"),
        P("chan", "seq"),
        P("chan", None),
        P("chan", None),
        P("chan", None),
        P("chan"),
    )
    out_specs = P("chan", "seq")
    return jax.shard_map(
        on_device, mesh=mesh, in_specs=in_specs, out_specs=out_specs, check_vma=False
    )
```

time: 82.2 us -> 60.1 us (0.73)
  other arithmetic: 9.18 us -> 0 us
  waiting for transfers between devices: 15.2 us -> 6.19 us
  local copies, waits for them, and re-layouts: 11.2 us -> 5.22 us
  starting transfers between devices: 13.1 us -> 17.7 us
  Pallas kernels: 32.8 us -> 29.9 us
    ppermute x1 -> x10, starting transfers between devices: 2.39 us -> 17.7 us  [the longest x3 9.27 us: on_device(): lax.ppermute(total, 'seq', [(i, i + step * plane) for i in range(shards -...]
    all_to_all x2 -> x0, waiting for transfers between devices: 15.2 us -> none  [the longest x1 7.85 us: on_device(): lax.all_to_all(jnp.stack(carried), 'seq', split_axis=0, concat_axis=0, ti...]
    all_to_all x2 -> x0, starting transfers between devices: 10.7 us -> none  [the longest x1 7.19 us: on_device(): lax.all_to_all(pieces, 'seq', split_axis=0, concat_axis=0, tiled=True)]
    unnamed x14 -> x0, other arithmetic: 8.57 us -> none
    ppermute x1 -> x10, waiting for transfers between devices: 0.01 us -> 6.19 us  [the longest x6 4.61 us: round_plane(): turned.append(lax.ppermute(pieces[ahead], 'seq', route))]
    unnamed x29 -> x22, local copies, waits for them, and re-layouts: 10.2 us -> 4.15 us
    pallas_call x2 -> x4, Pallas kernels: 18.4 us -> 16.4 us  [the longest x1 12.1 us: on_device(): call(functools.partial(outer_kernel, tokens * shards), tiles, [SCALAR, st...]
    pallas_call x1, Pallas kernels: 14.4 us -> 13.5 us  [on_device(): call(inner_kernel, tiles, [rows_spec(tokens), rows_spec(tokens), rows_spe...]
  transfers between devices with their start and end apart: 3 -> 10, of which waited for: 2 -> 6; matrix products, arithmetic and copies ran while one was open for 2% -> 3% of each run, Pallas kernels for 18% -> 23%
where the time goes in v2:
time: 60.1 us; the launch traced here: 59.1 us
  Pallas kernels  29.9 us (50%)
  starting transfers between devices  17.7 us (29%)
  waiting for transfers between devices  6.19 us (10%)
  local copies, waits for them, and re-layouts  5.22 us (9%)
    pallas_call x1, Pallas kernels, on_device(): call(inner_kernel, tiles, [rows_spec(tokens), rows_spec(tokens), rows_spe...  13.5 us
    pallas_call x1, Pallas kernels, on_device(): call(functools.partial(outer_kernel, tokens * shards), tiles, [SCALAR, st...  12.1 us
    ppermute x3, starting transfers between devices, on_device(): lax.ppermute(total, 'seq', [(i, i + step * plane) for i in range(shards -...  9.27 us
    ppermute x6, starting transfers between devices, round_plane(): turned.append(lax.ppermute(pieces[ahead], 'seq', route))  6 us
    ppermute x6, waiting for transfers between devices, round_plane(): turned.append(lax.ppermute(pieces[ahead], 'seq', route))  4.61 us
    unnamed x22, local copies, waits for them, and re-layouts  4.15 us
    pallas_call x1, Pallas kernels, on_device(): call(functools.partial(rim_kernel, inner), tiles, [SCALAR, rows_spec(BLOC...  3.79 us
    ppermute x1, starting transfers between devices, on_device(): lax.ppermute(v_stream[:, tokens - BLOCK:], 'seq', [(i, i + 1) for i in ra...  2.39 us
  transfers between devices with their start and end apart: 10, of which 6 were waited for; matrix products, arithmetic and copies ran while one was open for 3% of the time, Pallas kernels for 23%

profile of v2, /device:TPU:0, one launch (start us, length us, event | category | flops | bytes accessed | tf_op | source)
XLA Modules:
  0.0 59.1 jit_solution(4968367640476522028)
XLA Ops:
  0.0 1.1 %slice.3 = bf16[2048,128]{1,0:T(8,128)(2,1)S(1)} slice(bf16[2048,512]{1,0:T(8,128)(2,1)} %v_ref.3), slice={[0:2048], [384:512]} | slice | bytes 1048576 | tf_op jit(solution)/shard_map/slice | solution.py:242
  1.1 2.4 %collective-permute-start = (bf16[2048,128]{1,0:T(8,128)(2,1)S(1)}, bf16[2048,128]{1,0:T(8,128)(2,1)S(1)}, u32[]{:S(2)}, u32[]{:S(2)}) collective-permute-start(bf16[2048,128]{1,0:T(8,128)(2,1)S(1)} %slice.3), channel_id=1, source_target_pairs={{0,2},{2,4},{4,6},{6,8},{8,10},{10,12},{12,14},{14,16},{16,18},{18... | collective-permute-start | bytes 1572872 | tf_op jit(solution)/shard_map/ppermute | solution.py:242
  3.5 1.6 %copy.9 = f32[2,8,16,128]{3,2,1,0:T(8,128)} copy(f32[2,8,16,128]{3,1,2,0:T(8,128)} %bitcast.15) | data formatting | bytes 262144
  5.1 13.5 %shard_map.82 = (f32[2048,256]{1,0:T(8,128)}, bf16[2,3072,128]{2,1,0:T(8,128)(2,1)}, f32[16,16,128]{2,1,0:T(8,128)}) custom-call(bf16[2048,512]{1,0:T(8,128)(2,1)} %v_ref.3, bf16[2048,512]{1,0:T(8,128)(2,1)} %gate_ref.4, f32[2048,128]{1,0:T(8,128)} %taps_ref.1, f32[16,16,128]{2,1,0:T(8,128)} %bitcast.8, bf16[256,768]{1,0:T(8,128)(2,1)} %constant.21.clone.tables), custom_call_target="tpu_custom_call" | custom-call | flops 2044723200 | bytes 8388608 | tf_op jit(solution)/shard_map/pallas_call | solution.py:265
  18.7 1.6 %copy-done.4 = f32[2048,256]{1,0:T(8,128)S(1)} copy-done((f32[2048,256]{1,0:T(8,128)S(1)}, f32[2048,256]{1,0:T(8,128)}, u32[]{:S(2)}) %copy-start.4) | copy-done | bytes 2097176
  20.3 0.9 %copy-done.7 = f32[16,16,128]{2,1,0:T(8,128)S(1)} copy-done((f32[16,16,128]{2,1,0:T(8,128)S(1)}, f32[16,16,128]{2,1,0:T(8,128)}, u32[]{:S(2)}) %copy-start.7) | copy-done | bytes 131096
  21.2 3.8 %shard_map.83 = (bf16[2,1024,128]{2,1,0:T(8,128)(2,1)S(1)}, f32[4,16,128]{2,1,0:T(8,128)S(1)}, f32[4,16,128]{2,1,0:T(8,128)S(1)}, f32[4,16,128]{2,1,0:T(8,128)S(1)}, f32[4,16,128]{2,1,0:T(8,128)S(1)}) custom-call(s32[1]{0:T(128)} %bitcast.place_ref, bf16[2048,128]{1,0:T(8,128)(2,1)S(1)} %collective-permute-done.before_ref, bf16[2048,512]{1,0:T(8,128)(2,1)S(1)} %copy-done.1, ...), custom_call_target="tpu_custom_call" | custom-call | flops 681574400 | bytes 4194304 | tf_op jit(solution)/shard_map/pallas_call | solution.py:276
  25.0 2.6 %collective-permute-start.1 = (f32[4,16,128]{2,1,0:T(8,128)S(1)}, f32[4,16,128]{2,1,0:T(8,128)S(1)}, u32[]{:S(2)}, u32[]{:S(2)}) collective-permute-start(f32[4,16,128]{2,1,0:T(8,128)S(1)} %get-tuple-element.22), channel_id=1, source_target_pairs={{0,2},{2,4},{4,6},{6,0},{8,10},{10,12},{12,14},{14,8},{16,18},{18,... | collective-permute-start | bytes 98312 | tf_op jit(solution)/shard_map/ppermute | solution.py:293
  27.6 1.5 %collective-permute-start.2 = (f32[4,16,128]{2,1,0:T(8,128)S(1)}, f32[4,16,128]{2,1,0:T(8,128)S(1)}, u32[]{:S(2)}, u32[]{:S(2)}) collective-permute-start(f32[4,16,128]{2,1,0:T(8,128)S(1)} %get-tuple-element.23), channel_id=1, source_target_pairs={{0,4},{2,6},{4,0},{6,2},{8,12},{10,14},{12,8},{14,10},{16,20},{18,... | collective-permute-start | bytes 98312 | tf_op jit(solution)/shard_map/ppermute | solution.py:293
  29.2 1.2 %collective-permute-done.1.rest_1_ = f32[4,16,128]{2,1,0:T(8,128)S(1)} collective-permute-done((f32[4,16,128]{2,1,0:T(8,128)S(1)}, f32[4,16,128]{2,1,0:T(8,128)S(1)}, u32[]{:S(2)}, u32[]{:S(2)}) %collective-permute-start.1) | collective-permute-done | bytes 32800 | tf_op jit(solution)/shard_map/ppermute | solution.py:293
  30.4 1.2 %collective-permute-done.2.rest_2_ = f32[4,16,128]{2,1,0:T(8,128)S(1)} collective-permute-done((f32[4,16,128]{2,1,0:T(8,128)S(1)}, f32[4,16,128]{2,1,0:T(8,128)S(1)}, u32[]{:S(2)}, u32[]{:S(2)}) %collective-permute-start.2) | collective-permute-done | bytes 32800 | tf_op jit(solution)/shard_map/ppermute | solution.py:293
  31.6 0.2 shard_map.84
  31.7 3.5 %collective-permute-start.4 = (f32[4,16,128]{2,1,0:T(8,128)S(1)}, f32[4,16,128]{2,1,0:T(8,128)S(1)}, u32[]{:S(2)}, u32[]{:S(2)}) collective-permute-start(f32[4,16,128]{2,1,0:T(8,128)S(1)} %shard_map.84), channel_id=1, source_target_pairs={{0,8},{2,10},{4,12},{6,14},{8,16},{10,18},{12,20},{14,22},{16,24},... | collective-permute-start | bytes 98312 | tf_op jit(solution)/shard_map/ppermute | solution.py:310
  35.2 4.5 %collective-permute-start.5 = (f32[4,16,128]{2,1,0:T(8,128)S(1)}, f32[4,16,128]{2,1,0:T(8,128)S(1)}, u32[]{:S(2)}, u32[]{:S(2)}) collective-permute-start(f32[4,16,128]{2,1,0:T(8,128)S(1)} %shard_map.84), channel_id=1, source_target_pairs={{0,16},{2,18},{4,20},{6,22},{8,24},{10,26},{12,28},{14,30},{1,17},... | collective-permute-start | bytes 98312 | tf_op jit(solution)/shard_map/ppermute | solution.py:310
  39.7 1.3 %collective-permute-start.6 = (f32[4,16,128]{2,1,0:T(8,128)S(1)}, f32[4,16,128]{2,1,0:T(8,128)S(1)}, u32[]{:S(2)}, u32[]{:S(2)}) collective-permute-start(f32[4,16,128]{2,1,0:T(8,128)S(1)} %shard_map.84), channel_id=1, source_target_pairs={{0,24},{2,26},{4,28},{6,30},{1,25},{3,27},{5,29},{7,31}} | collective-permute-start | bytes 98312 | tf_op jit(solution)/shard_map/ppermute | solution.py:310
  41.0 0.3 collective-permute-done.5.rest_5_
  41.3 1.3 %collective-permute-done.6.rest_6_ = f32[4,16,128]{2,1,0:T(8,128)S(1)} collective-permute-done((f32[4,16,128]{2,1,0:T(8,128)S(1)}, f32[4,16,128]{2,1,0:T(8,128)S(1)}, u32[]{:S(2)}, u32[]{:S(2)}) %collective-permute-start.6) | collective-permute-done | bytes 32800 | tf_op jit(solution)/shard_map/ppermute | solution.py:310
  42.6 0.3 shard_map.85
  42.9 0.1 collective-permute-start.7
  43.0 0.3 collective-permute-start.8
  43.2 1.5 %collective-permute-start.9 = (f32[4,16,128]{2,1,0:T(8,128)S(1)}, f32[4,16,128]{2,1,0:T(8,128)S(1)}, u32[]{:S(2)}, u32[]{:S(2)}) collective-permute-start(f32[4,16,128]{2,1,0:T(8,128)S(1)} %get-tuple-element.28), channel_id=1, source_target_pairs={{0,6},{2,0},{4,2},{6,4},{8,14},{10,8},{12,10},{14,12},{16,22},{18,... | collective-permute-start | bytes 98312 | tf_op jit(solution)/shard_map/ppermute | solution.py:293
  44.8 1.5 %collective-permute-done.7.rest_1_ = f32[4,16,128]{2,1,0:T(8,128)S(1)} collective-permute-done((f32[4,16,128]{2,1,0:T(8,128)S(1)}, f32[4,16,128]{2,1,0:T(8,128)S(1)}, u32[]{:S(2)}, u32[]{:S(2)}) %collective-permute-start.7) | collective-permute-done | bytes 32800 | tf_op jit(solution)/shard_map/ppermute | solution.py:293
  46.3 0.7 %collective-permute-done.8.rest_2_ = f32[4,16,128]{2,1,0:T(8,128)S(1)} collective-permute-done((f32[4,16,128]{2,1,0:T(8,128)S(1)}, f32[4,16,128]{2,1,0:T(8,128)S(1)}, u32[]{:S(2)}, u32[]{:S(2)}) %collective-permute-start.8) | collective-permute-done | bytes 32800 | tf_op jit(solution)/shard_map/ppermute | solution.py:293
  47.0 12.1 %shard_map.86 = bf16[2048,512]{1,0:T(8,128)(2,1)} custom-call(s32[1]{0:T(128)} %bitcast.place_ref, bf16[2,1024,128]{2,1,0:T(8,128)(2,1)S(1)} %get-tuple-element.19.rim_ref, bf16[2,3072,128]{2,1,0:T(8,128)(2,1)S(1)} %copy-done.5, bf16[2048,512]{1,0:T(8,128)(2,1)S(1)} %copy-done.3, f32[16,16,128]{2,1,0:T(8,128)S(1)} %bitcast.12, f32[16,16,128]{2,1,0:T(8,128)S(1)} %bitcast.13, ...), custom_call_target="tpu_custom_call" | custom-call | flops 73400320 | bytes 6291456 | tf_op jit(solution)/shard_map/pallas_call | solution.py:326
  (24 shorter events, 0.1 us)
Async XLA Ops:
  1.1 17.6 %collective-permute-start = (bf16[2048,128]{1,0:T(8,128)(2,1)S(1)}, bf16[2048,128]{1,0:T(8,128)(2,1)S(1)}, u32[]{:S(2)}, u32[]{:S(2)}) collective-permute-start(bf16[2048,128]{1,0:T(8,128)(2,1)S(1)} %slice.3), channel_id=1, source_target_pairs={{0,2},{2,4},{4,6},{6,8},{8,10},{10,12},{12,14},{14,16},{16,18},{18... | collective-permute-start | bytes 1572872 | tf_op jit(solution)/shard_map/ppermute | solution.py:242
  5.1 13.5 %copy-start = (f32[2,8,16,128]{3,2,1,0:T(8,128)S(1)}, f32[2,8,16,128]{3,2,1,0:T(8,128)}, u32[]{:S(2)}) copy-start(f32[2,8,16,128]{3,2,1,0:T(8,128)} %copy.9) | copy-start | bytes 393220
  5.1 13.6 %copy-start.1 = (bf16[2048,512]{1,0:T(8,128)(2,1)S(1)}, bf16[2048,512]{1,0:T(8,128)(2,1)}, u32[]{:S(2)}) copy-start(bf16[2048,512]{1,0:T(8,128)(2,1)} %v_ref.3) | copy-start | bytes 6291460
  5.1 13.6 %copy-start.2 = (bf16[2048,512]{1,0:T(8,128)(2,1)S(1)}, bf16[2048,512]{1,0:T(8,128)(2,1)}, u32[]{:S(2)}) copy-start(bf16[2048,512]{1,0:T(8,128)(2,1)} %gate_ref.4) | copy-start | bytes 6291460
  5.1 13.6 %copy-start.6 = (bf16[256,768]{1,0:T(8,128)(2,1)S(1)}, bf16[256,768]{1,0:T(8,128)(2,1)}, u32[]{:S(2)}) copy-start(bf16[256,768]{1,0:T(8,128)(2,1)} %constant.21.clone.tables) | copy-start | bytes 1179652
  18.7 1.6 %copy-start.4 = (f32[2048,256]{1,0:T(8,128)S(1)}, f32[2048,256]{1,0:T(8,128)}, u32[]{:S(2)}) copy-start(f32[2048,256]{1,0:T(8,128)} %get-tuple-element.17.spec_ref) | copy-start | bytes 6291460
  20.3 0.9 %copy-start.7 = (f32[16,16,128]{2,1,0:T(8,128)S(1)}, f32[16,16,128]{2,1,0:T(8,128)}, u32[]{:S(2)}) copy-start(f32[16,16,128]{2,1,0:T(8,128)} %get-tuple-element.18.inner_ref) | copy-start | bytes 393220
  21.2 23.6 %copy-start.9 = (f32[2048,16]{0,1:T(8,128)S(1)}, f32[2048,16]{0,1:T(8,128)}, u32[]{:S(2)}) copy-start(f32[2048,16]{0,1:T(8,128)} %param.13) | copy-start | bytes 393220
  21.2 25.8 %copy-start.3 = (bf16[2048,512]{1,0:T(8,128)(2,1)S(1)}, bf16[2048,512]{1,0:T(8,128)(2,1)}, u32[]{:S(2)}) copy-start(bf16[2048,512]{1,0:T(8,128)(2,1)} %gate_ref.5) | copy-start | bytes 6291460
  21.2 25.8 %copy-start.5 = (bf16[2,3072,128]{2,1,0:T(8,128)(2,1)S(1)}, bf16[2,3072,128]{2,1,0:T(8,128)(2,1)}, u32[]{:S(2)}) copy-start(bf16[2,3072,128]{2,1,0:T(8,128)(2,1)} %get-tuple-element.20.inner_ref) | copy-start | bytes 4718596
  21.2 25.8 %copy-start.8 = (f32[2048]{0:T(1024)S(1)}, f32[2048]{0:T(1024)}, u32[]{:S(2)}) copy-start(f32[2048]{0:T(1024)} %param.14) | copy-start | bytes 24580
  25.0 5.4 %collective-permute-start.1 = (f32[4,16,128]{2,1,0:T(8,128)S(1)}, f32[4,16,128]{2,1,0:T(8,128)S(1)}, u32[]{:S(2)}, u32[]{:S(2)}) collective-permute-start(f32[4,16,128]{2,1,0:T(8,128)S(1)} %get-tuple-element.22), channel_id=1, source_target_pairs={{0,2},{2,4},{4,6},{6,0},{8,10},{10,12},{12,14},{14,8},{16,18},{18,... | collective-permute-start | bytes 98312 | tf_op jit(solution)/shard_map/ppermute | solution.py:293
  27.6 3.9 %collective-permute-start.2 = (f32[4,16,128]{2,1,0:T(8,128)S(1)}, f32[4,16,128]{2,1,0:T(8,128)S(1)}, u32[]{:S(2)}, u32[]{:S(2)}) collective-permute-start(f32[4,16,128]{2,1,0:T(8,128)S(1)} %get-tuple-element.23), channel_id=1, source_target_pairs={{0,4},{2,6},{4,0},{6,2},{8,12},{10,14},{12,8},{14,10},{16,20},{18,... | collective-permute-start | bytes 98312 | tf_op jit(solution)/shard_map/ppermute | solution.py:293
  29.2 2.4 %collective-permute-start.3 = (f32[4,16,128]{2,1,0:T(8,128)S(1)}, f32[4,16,128]{2,1,0:T(8,128)S(1)}, u32[]{:S(2)}, u32[]{:S(2)}) collective-permute-start(f32[4,16,128]{2,1,0:T(8,128)S(1)} %get-tuple-element.24), channel_id=1, source_target_pairs={{0,6},{2,0},{4,2},{6,4},{8,14},{10,8},{12,10},{14,12},{16,22},{18,... | collective-permute-start | bytes 98312 | tf_op jit(solution)/shard_map/ppermute | solution.py:293
  31.7 9.3 %collective-permute-start.4 = (f32[4,16,128]{2,1,0:T(8,128)S(1)}, f32[4,16,128]{2,1,0:T(8,128)S(1)}, u32[]{:S(2)}, u32[]{:S(2)}) collective-permute-start(f32[4,16,128]{2,1,0:T(8,128)S(1)} %shard_map.84), channel_id=1, source_target_pairs={{0,8},{2,10},{4,12},{6,14},{8,16},{10,18},{12,20},{14,22},{16,24},... | collective-permute-start | bytes 98312 | tf_op jit(solution)/shard_map/ppermute | solution.py:310
  35.2 6.1 %collective-permute-start.5 = (f32[4,16,128]{2,1,0:T(8,128)S(1)}, f32[4,16,128]{2,1,0:T(8,128)S(1)}, u32[]{:S(2)}, u32[]{:S(2)}) collective-permute-start(f32[4,16,128]{2,1,0:T(8,128)S(1)} %shard_map.84), channel_id=1, source_target_pairs={{0,16},{2,18},{4,20},{6,22},{8,24},{10,26},{12,28},{14,30},{1,17},... | collective-permute-start | bytes 98312 | tf_op jit(solution)/shard_map/ppermute | solution.py:310
  39.7 2.9 %collective-permute-start.6 = (f32[4,16,128]{2,1,0:T(8,128)S(1)}, f32[4,16,128]{2,1,0:T(8,128)S(1)}, u32[]{:S(2)}, u32[]{:S(2)}) collective-permute-start(f32[4,16,128]{2,1,0:T(8,128)S(1)} %shard_map.84), channel_id=1, source_target_pairs={{0,24},{2,26},{4,28},{6,30},{1,25},{3,27},{5,29},{7,31}} | collective-permute-start | bytes 98312 | tf_op jit(solution)/shard_map/ppermute | solution.py:310
  42.9 3.4 %collective-permute-start.7 = (f32[4,16,128]{2,1,0:T(8,128)S(1)}, f32[4,16,128]{2,1,0:T(8,128)S(1)}, u32[]{:S(2)}, u32[]{:S(2)}) collective-permute-start(f32[4,16,128]{2,1,0:T(8,128)S(1)} %get-tuple-element.26), channel_id=1, source_target_pairs={{0,2},{2,4},{4,6},{6,0},{8,10},{10,12},{12,14},{14,8},{16,18},{18,... | collective-permute-start | bytes 98312 | tf_op jit(solution)/shard_map/ppermute | solution.py:293
  43.0 4.0 %collective-permute-start.8 = (f32[4,16,128]{2,1,0:T(8,128)S(1)}, f32[4,16,128]{2,1,0:T(8,128)S(1)}, u32[]{:S(2)}, u32[]{:S(2)}) collective-permute-start(f32[4,16,128]{2,1,0:T(8,128)S(1)} %get-tuple-element.27), channel_id=1, source_target_pairs={{0,4},{2,6},{4,0},{6,2},{8,12},{10,14},{12,8},{14,10},{16,20},{18,... | collective-permute-start | bytes 98312 | tf_op jit(solution)/shard_map/ppermute | solution.py:293
  43.2 3.8 %collective-permute-start.9 = (f32[4,16,128]{2,1,0:T(8,128)S(1)}, f32[4,16,128]{2,1,0:T(8,128)S(1)}, u32[]{:S(2)}, u32[]{:S(2)}) collective-permute-start(f32[4,16,128]{2,1,0:T(8,128)S(1)} %get-tuple-element.28), channel_id=1, source_target_pairs={{0,6},{2,0},{4,2},{6,4},{8,14},{10,8},{12,10},{14,12},{16,22},{18,... | collective-permute-start | bytes 98312 | tf_op jit(solution)/shard_map/ppermute | solution.py:293

commit v3 on v2

--- a/solution.py
+++ b/solution.py
@@ -13,7 +13,8 @@
 SUBS = 8
 TILE = LANES * SUBS
 BLOCK = 128
-ROWS = 256
+ROWS = 512
+ROOM = 56
 STEPS = 8
 F32, BF16 = jnp.float32, jnp.bfloat16
 
@@ -110,8 +111,7 @@
         state_ref[mode] = state
 
 
-def rim_kernel(inner, place_ref, before_ref, v_ref, gate_ref, spec_ref, rates_ref, inner_ref, tables, *rest):
-    mixed_ref, *piece_refs, store, ends = rest
+def rim_kernel(inner, before_ref, v_ref, gate_ref, spec_ref, rates_ref, inner_ref, tables, mixed_ref, ends_ref, store):
     for first in range(0, TILE, ROWS):
         rows = slice(first, first + ROWS)
         earlier = mm(twice(before_ref[rows]), tables[:, ODD])
@@ -119,91 +119,86 @@
         short = apply_window(earlier, later, spec_ref[rows], tables)
         put_mixed(store, first, 0, short, gate_ref[rows])
     for mode, state in enumerate(end_states(store, mixed_ref, rates_ref)):
-        ends[mode] = jnp.exp(-float(inner) * rates_ref[mode]) * state + inner_ref[mode]
-    plane = len(piece_refs)
-    share = ends.shape[0] // plane
-    for ahead, piece in enumerate(piece_refs):
-        piece[...] = ends[pl.ds(lax.rem(place_ref[0] + ahead, plane) * share, share)]
-
-
-def decayed(rates, positions):
-    return jnp.exp(-lax.convert_element_type(positions, F32) * rates)
-
-
-def total_kernel(tokens, place_ref, rates_ref, *rest):
-    *ends, total_ref = rest
-    plane, share = len(ends), total_ref.shape[0]
-    place = place_ref[0]
-    for mode in range(share):
-        rates = rates_ref[place * share + mode]
-        total = None
-        for behind, end in enumerate(ends):
-            owner = lax.rem(place - behind + plane, plane)
-            term = decayed(rates, tokens * (plane - 1 - owner)) * end[mode]
-            total = term if total is None else total + term
-        total_ref[mode] = total
-
-
-def start_kernel(tokens, planes, place_ref, rates_ref, *rest):
-    plane = (len(rest) - (planes - 1)) // 2
-    ends, totals, starts = rest[:plane], rest[plane : plane + planes - 1], rest[plane + planes - 1 :]
-    share = starts[0].shape[0]
-    place = place_ref[0]
-    for mode in range(share):
-        rates = rates_ref[place * share + mode]
-        base = totals[0][mode]
-        for behind in range(1, planes - 1):
-            base = base + jnp.exp(-float(tokens * plane * behind) * rates) * totals[behind][mode]
-        for ahead in range(plane):
-            target = lax.rem(place + ahead, plane)
-            start = decayed(rates, tokens * target) * base
-            for behind, end in enumerate(ends):
-                owner = lax.rem(place - behind + plane, plane)
-                gap = target - 1 - owner
-                term = decayed(rates, tokens * jnp.maximum(gap, 0)) * end[mode]
-                start = start + jnp.where(gap >= 0, term, 0.0)
-            starts[ahead][mode] = start
-
-
-def outer_kernel(seq_total, place_ref, rim_ref, inner_ref, gate_ref, rates_ref, weights_ref, bias_ref, *rest):
-    *start_refs, out_ref, store, begin = rest
-    modes, plane = rates_ref.shape[0], len(start_refs)
-    share = modes // plane
-    for behind, ref in enumerate(start_refs):
-        begin[pl.ds(lax.rem(place_ref[0] - behind + plane, plane) * share, share)] = ref[...]
+        ends_ref[mode] = jnp.exp(-float(inner) * rates_ref[mode]) * state + inner_ref[mode]
+
+
+def scan_kernel(tokens, place_ref, rates_ref, ends_ref, starts_ref):
+    reach = jnp.exp(-float(tokens) * rates_ref[place_ref[0]])
+    start = jnp.zeros_like(reach)
+    starts_ref[0] = start
+    for shard in range(1, ends_ref.shape[0]):
+        start = reach * start + ends_ref[shard - 1]
+        starts_ref[shard] = start
+
+
+def added(terms):
+    while len(terms) > 1:
+        terms = [sum(terms[i : i + 2][1:], terms[i]) for i in range(0, len(terms), 2)]
+    return terms[0]
+
+
+def scales(rates_ref, weights_ref, seq_total):
+    modes = rates_ref.shape[0]
     decay = [jnp.exp(-rates_ref[mode]) for mode in range(modes)]
     scaled = [weights_ref[mode] * jnp.sqrt(2.0 * rates_ref[mode] + 2.0 / seq_total) for mode in range(modes)]
+    return decay, scaled
+
+
+def local_kernel(seq_total, rim_ref, inner_ref, rates_ref, weights_ref, bias_ref, *rest):
+    sums_ref = rest[-1]
+    decay, scaled = scales(rates_ref, weights_ref, seq_total)
     bias = bias_ref[...]
-    states = tuple(begin[mode] for mode in range(modes))
+    states = tuple(jnp.zeros((SUBS, LANES), F32) for _ in decay)
     first = 0
     for source in (rim_ref, inner_ref):
 
         def turn(index, states, source=source, first=first):
             at = pl.multiple_of(index * STEPS * SUBS, STEPS * SUBS)
             values = source[pl.ds(at, STEPS * SUBS), :].astype(F32)
-            sums = []
             for step in range(STEPS):
                 value = values[step * SUBS : (step + 1) * SUBS]
                 states = tuple(d * s + value for d, s in zip(decay, states))
-                terms = [c * s for c, s in zip(scaled, states)] + [bias * value]
-                while len(terms) > 1:
-                    terms = [sum(terms[i : i + 2][1:], terms[i]) for i in range(0, len(terms), 2)]
-                sums.append(terms[0])
-            store[pl.ds(first * SUBS + at, STEPS * SUBS), :] = jnp.concatenate(sums, axis=0)
+                total = added([c * s for c, s in zip(scaled, states)] + [bias * value])
+                sums_ref[pl.ds(first * SUBS + at + step * SUBS, SUBS), :] = total
             return states
 
         count = source.shape[0] // SUBS
         states = lax.fori_loop(0, count // STEPS, turn, states)
         first += count
+
+
+def outer_kernel(seq_total, sums_ref, gate_ref, rates_ref, weights_ref, start_ref, out_ref, store):
+    decay, scaled = scales(rates_ref, weights_ref, seq_total)
+    states = tuple(c * start_ref[mode] for mode, c in enumerate(scaled))
+    steps = BLOCK // SUBS
+
+    def carry(index, states):
+        at = pl.multiple_of(index * steps * SUBS, steps * SUBS)
+        for step in range(steps):
+            states = tuple(d * s for d, s in zip(decay, states))
+            where = pl.ds(at + step * SUBS, SUBS)
+            store[where, :] = sums_ref[where, :] + added(list(states))
+        return states
+
+    def finish(block, group):
+        rows = pl.ds(pl.multiple_of(group * LANES, LANES), LANES)
+        cols = pl.ds(pl.multiple_of(block * BLOCK, BLOCK), BLOCK)
+        turned = store[pl.ds(block * BLOCK * SUBS + group, BLOCK, stride=SUBS), :].T
+        out_ref[rows, cols] = (gate_ref[rows, cols].astype(F32) * turned).astype(BF16)
+
+    def both(index, states):
+        finish(index // SUBS - 1, index % SUBS)
+        return carry(index, states)
+
+    blocks = store.shape[0] // SUBS // BLOCK
+    states = lax.fori_loop(0, SUBS, carry, states)
+    lax.fori_loop(SUBS, blocks * SUBS, both, states)
     for group in range(SUBS):
-        rows = slice(group * LANES, (group + 1) * LANES)
-        for block in range(first // BLOCK):
-            cols = slice(block * BLOCK, (block + 1) * BLOCK)
-            turned = store[pl.ds(block * BLOCK * SUBS + group, BLOCK, stride=SUBS), :].T
-            out_ref[rows, cols] = (gate_ref[rows, cols].astype(F32) * turned).astype(BF16)
+        finish(blocks - 1, group)
 
 
 SCALAR = pl.BlockSpec(memory_space=pltpu.SMEM)
+WHOLE = pl.BlockSpec(memory_space=pltpu.VMEM)
 
 
 def call(kernel, tiles, in_specs, out_specs, out_shape, scratch, flops, moved, room):
@@ -254,14 +249,11 @@
     bias = skip_bias.reshape(groups, LANES)
     tables = jnp.asarray(window_tables())
     tables_spec = pl.BlockSpec(tables.shape, lambda i: (0, 0))
-    planes = 4 if shards % 4 == 0 else 1
-    plane = shards // planes
-    share = modes // plane
-    place = (lax.axis_index("seq") % plane).astype(jnp.int32).reshape(1)
+    place = lax.axis_index("seq").astype(jnp.int32).reshape(1)
     inner = tokens - BLOCK
+    seq_total = tokens * shards
     shape = jax.ShapeDtypeStruct
     per_mode = shape((modes, groups, LANES), F32)
-    piece = shape((share, groups, LANES), F32)
     spectrum, inner_mixed, inner_state = call(
         inner_kernel,
         tiles,
@@ -271,71 +263,73 @@
         [steps_scratch(inner)],
         channels * inner * 2600,
         channels * tokens * 8,
-        56,
+        ROOM,
     )(v_stream, gate_one, short_filter, rates, tables)
-    rim_mixed, *ends = call(
+    rim_mixed, end_state = call(
         functools.partial(rim_kernel, inner),
         tiles,
-        [SCALAR, rows_spec(BLOCK), rows_spec(BLOCK), rows_spec(BLOCK), rows_spec(2 * BLOCK)]
+        [rows_spec(BLOCK), rows_spec(BLOCK), rows_spec(BLOCK), rows_spec(2 * BLOCK)]
         + [modes_spec(modes), modes_spec(modes), tables_spec],
-        [steps_spec(BLOCK)] + [modes_spec(share)] * plane,
-        [shape((tiles, BLOCK * SUBS, LANES), BF16)] + [piece] * plane,
-        [steps_scratch(BLOCK), pltpu.VMEM((modes, SUBS, LANES), F32)],
+        [steps_spec(BLOCK), modes_spec(modes)],
+        [shape((tiles, BLOCK * SUBS, LANES), BF16), per_mode],
+        [steps_scratch(BLOCK)],
         channels * BLOCK * 2600,
         channels * BLOCK * 16,
-        40,
-    )(place, before, v_stream, gate_one, spectrum, rates, inner_state, tables)
-
-    def round_plane(pieces):
-        turned = [pieces[0]]
-        for ahead in range(1, plane):
-            route = [(g * plane + i, g * plane + (i + ahead) % plane) for g in range(planes) for i in range(plane)]
-            turned.append(lax.ppermute(pieces[ahead], "seq", route))
-        return turned
-
-    arrived = round_plane(ends)
-    pieces_spec, rates_spec = modes_spec(share), modes_spec(modes)
-    total = call(
-        functools.partial(total_kernel, tokens),
+        ROOM,
+    )(before, v_stream, gate_one, spectrum, rates, inner_state, tables)
+
+    def local(first, count, sums, rim_mixed, inner_mixed):
+        def shifted(spec):
+            return pl.BlockSpec(spec.block_shape, lambda i: spec.index_map(i + first))
+
+        return pl.pallas_call(
+            functools.partial(local_kernel, seq_total),
+            grid=(count,),
+            in_specs=[
+                shifted(steps_spec(BLOCK)),
+                shifted(steps_spec(inner)),
+                shifted(modes_spec(modes)),
+                shifted(modes_spec(modes)),
+                shifted(pl.BlockSpec((SUBS, LANES), lambda i: (i, 0))),
+            ]
+            + [pl.BlockSpec(memory_space=pl.ANY)] * len(sums),
+            out_specs=shifted(steps_spec(tokens)),
+            out_shape=shape((tiles, tokens * SUBS, LANES), F32),
+            input_output_aliases={5: 0} if sums else {},
+            compiler_params=pltpu.CompilerParams(vmem_limit_bytes=ROOM << 20),
+            cost_estimate=pl.CostEstimate(
+                flops=count * TILE * tokens * 70, bytes_accessed=count * TILE * tokens * 6, transcendentals=0
+            ),
+        )(rim_mixed, inner_mixed, rates, weights, bias, *sums)
+
+    moved = lax.all_to_all(end_state.reshape(shards, -1, LANES), "seq", split_axis=0, concat_axis=0, tiled=True)
+    early = (tiles + 1) // 2
+    sums = local(0, early, (), rim_mixed, inner_mixed)
+    moved, sums = lax.optimization_barrier((moved, sums))
+    carried = pl.pallas_call(
+        functools.partial(scan_kernel, tokens),
+        in_specs=[SCALAR, WHOLE, WHOLE],
+        out_specs=WHOLE,
+        out_shape=shape(moved.shape, F32),
+        compiler_params=pltpu.CompilerParams(vmem_limit_bytes=4 << 20),
+    )(place, rates.reshape(moved.shape), moved)
+    start = lax.all_to_all(carried, "seq", split_axis=0, concat_axis=0, tiled=True).reshape(per_mode.shape)
+
+    if early < tiles:
+        rim_later, inner_later, _ = lax.optimization_barrier((rim_mixed, inner_mixed, carried))
+        sums = local(early, tiles - early, (sums,), rim_later, inner_later)
+
+    hyena_out = call(
+        functools.partial(outer_kernel, seq_total),
         tiles,
-        [SCALAR, rates_spec] + [pieces_spec] * plane,
-        pieces_spec,
-        piece,
-        [],
-        1 << 20,
-        1 << 18,
-        4,
-    )(place, rates, *arrived)
-    totals = [
-        lax.ppermute(total, "seq", [(i, i + step * plane) for i in range(shards - step * plane)])
-        for step in range(1, planes)
-    ]
-    starts = call(
-        functools.partial(start_kernel, tokens, planes),
-        tiles,
-        [SCALAR, rates_spec] + [pieces_spec] * (plane + planes - 1),
-        [pieces_spec] * plane,
-        [piece] * plane,
-        [],
-        1 << 20,
-        1 << 18,
-        4,
-    )(place, rates, *arrived, *totals)
-    starts = round_plane(starts)
-
-    hyena_out = call(
-        functools.partial(outer_kernel, tokens * shards),
-        tiles,
-        [SCALAR, steps_spec(BLOCK), steps_spec(inner), rows_spec(tokens), rates_spec, rates_spec]
-        + [pl.BlockSpec((SUBS, LANES), lambda i: (i, 0))]
-        + [pieces_spec] * plane,
+        [steps_spec(tokens), rows_spec(tokens)] + [modes_spec(modes)] * 3,
         rows_spec(tokens),
         shape((channels, tokens), BF16),
-        [steps_scratch(tokens), pltpu.VMEM((modes, SUBS, LANES), F32)],
-        channels * tokens * 70,
-        channels * tokens * 6,
-        40,
-    )(place, rim_mixed, inner_mixed, gate_two, rates, weights, bias, *starts)
+        [steps_scratch(tokens)],
+        channels * tokens * 40,
+        channels * tokens * 8,
+        ROOM,
+    )(sums, gate_two, rates, weights, start)
     return hyena_out[:real_channels]
 
 

time: 60.1 us -> 67.1 us (1.12)
  Pallas kernels: 29.9 us -> 45.8 us
  waiting for transfers between devices: 6.19 us -> 0.51 us
  starting transfers between devices: 17.7 us -> 15.6 us
    pallas_call x4 -> x5, Pallas kernels: 16.4 us -> 34.4 us  [the longest x2 14.9 us: local(): pl.pallas_call(functools.partial(local_kernel, seq_total), grid=(count,),...]
    ppermute x9 -> x0, starting transfers between devices: 15.3 us -> none  [the longest x3 9.27 us: on_device(): lax.ppermute(total, 'seq', [(i, i + step * plane) for i in range(shards -...]
    all_to_all x0 -> x2, starting transfers between devices: none -> 13.2 us  [the longest x1 7.19 us: on_device(): lax.all_to_all(end_state.reshape(shards, -1, LANES), 'seq', split_axis=0,...]
    ppermute x9 -> x0, waiting for transfers between devices: 6.18 us -> none  [the longest x6 4.61 us: round_plane(): turned.append(lax.ppermute(pieces[ahead], 'seq', route))]
    pallas_call x1, Pallas kernels: 13.5 us -> 11.4 us  [on_device(): call(inner_kernel, tiles, [rows_spec(tokens), rows_spec(tokens), rows_spe...]
    unnamed x22 -> x10, local copies, waits for them, and re-layouts: 4.15 us -> 3.7 us
  transfers between devices with their start and end apart: 10 -> 3, of which waited for: 6 -> 1; matrix products, arithmetic and copies ran while one was open for 3% -> 3% of each run, Pallas kernels for 23% -> 39%
where the time goes in v3:
time: 67.1 us; the launch traced here: 66.7 us
  Pallas kernels  45.8 us (68%)
  starting transfers between devices  15.6 us (23%)
  local copies, waits for them, and re-layouts  4.77 us (7%)
    pallas_call x2, Pallas kernels, local(): pl.pallas_call(functools.partial(local_kernel, seq_total), grid=(count,),...  14.9 us
    pallas_call x1, Pallas kernels, on_device(): call(functools.partial(outer_kernel, seq_total), tiles, [steps_spec(token...  13.1 us
    pallas_call x1, Pallas kernels, on_device(): call(inner_kernel, tiles, [rows_spec(tokens), rows_spec(tokens), rows_spe...  11.4 us
    all_to_all x1, starting transfers between devices, on_device(): lax.all_to_all(end_state.reshape(shards, -1, LANES), 'seq', split_axis=0,...  7.19 us
    all_to_all x1, starting transfers between devices, on_device(): lax.all_to_all(carried, 'seq', split_axis=0, concat_axis=0, tiled=True)  6 us
    pallas_call x1, Pallas kernels, on_device(): call(functools.partial(rim_kernel, inner), tiles, [rows_spec(BLOCK), rows...  5.7 us
    unnamed x10, local copies, waits for them, and re-layouts  3.7 us
    ppermute x1, starting transfers between devices, on_device(): lax.ppermute(v_stream[:, tokens - BLOCK:], 'seq', [(i, i + 1) for i in ra...  2.39 us
  transfers between devices with their start and end apart: 3, of which 1 were waited for; matrix products, arithmetic and copies ran while one was open for 3% of the time, Pallas kernels for 39%

profile of v3, /device:TPU:0, one launch (start us, length us, event | category | flops | bytes accessed | tf_op | source)
XLA Modules:
  0.0 66.7 jit_solution(2259954259119629103)
XLA Ops:
  0.0 1.1 %slice.3 = bf16[2048,128]{1,0:T(8,128)(2,1)S(1)} slice(bf16[2048,512]{1,0:T(8,128)(2,1)} %v_ref.3), slice={[0:2048], [384:512]} | slice | bytes 1048576 | tf_op jit(solution)/shard_map/slice | solution.py:237
  1.1 2.4 %collective-permute-start = (bf16[2048,128]{1,0:T(8,128)(2,1)S(1)}, bf16[2048,128]{1,0:T(8,128)(2,1)S(1)}, u32[]{:S(2)}, u32[]{:S(2)}) collective-permute-start(bf16[2048,128]{1,0:T(8,128)(2,1)S(1)} %slice.3), channel_id=1, source_target_pairs={{0,2},{2,4},{4,6},{6,8},{8,10},{10,12},{12,14},{14,16},{16,18},{18... | collective-permute-start | bytes 1572872 | tf_op jit(solution)/shard_map/ppermute | solution.py:237
  3.5 1.6 %copy.10 = f32[2,8,16,128]{3,2,1,0:T(8,128)} copy(f32[2,8,16,128]{3,1,2,0:T(8,128)} %bitcast.17) | data formatting | bytes 262144
  5.1 11.4 %shard_map.82 = (f32[2048,256]{1,0:T(8,128)}, bf16[2,3072,128]{2,1,0:T(8,128)(2,1)}, f32[16,16,128]{2,1,0:T(8,128)}) custom-call(bf16[2048,512]{1,0:T(8,128)(2,1)} %v_ref.3, bf16[2048,512]{1,0:T(8,128)(2,1)} %gate_ref.4, f32[2048,128]{1,0:T(8,128)} %taps_ref.1, f32[16,16,128]{2,1,0:T(8,128)} %bitcast.8, bf16[256,768]{1,0:T(8,128)(2,1)} %constant.8.clone.tables), custom_call_target="tpu_custom_call" | custom-call | flops 2044723200 | bytes 8388608 | tf_op jit(solution)/shard_map/pallas_call | solution.py:257
  16.5 0.0 collective-permute-done.before_ref
  16.5 0.0 copy-start.1
  16.5 0.8 %copy-done.1 = bf16[2048,128]{1,0:T(8,128)(2,1)} copy-done((bf16[2048,128]{1,0:T(8,128)(2,1)}, bf16[2048,128]{1,0:T(8,128)(2,1)S(1)}, u32[]{:S(2)}) %copy-start.1) | copy-done | bytes 524312
  17.3 0.0 copy-start.3
  17.3 5.7 %shard_map.83 = (bf16[2,1024,128]{2,1,0:T(8,128)(2,1)}, f32[16,16,128]{2,1,0:T(8,128)}) custom-call(bf16[2048,128]{1,0:T(8,128)(2,1)} %copy-done.1, bf16[2048,512]{1,0:T(8,128)(2,1)} %v_ref.3, bf16[2048,512]{1,0:T(8,128)(2,1)} %gate_ref.4, f32[2048,256]{1,0:T(8,128)} %get-tuple-element.14.spec_ref, f32[16,16,128]{2,1,0:T(8,128)} %bitcast.9, ...), custom_call_target="tpu_custom_call" | custom-call | flops 681574400 | bytes 4194304 | tf_op jit(solution)/shard_map/pallas_call | solution.py:268
  23.0 7.2 %all-to-all-start = ((f32[16,16,128]{2,1,0:T(8,128)}), f32[16,16,128]{2,1,0:T(8,128)S(1)}, u32[]{:S(2)}, u32[]{:S(2)}) async-start(f32[16,16,128]{2,1,0:T(8,128)} %get-tuple-element.18), calls=%async_computation | async-start | bytes 262144 | tf_op jit(solution)/shard_map/all_to_all | solution.py:305
  30.2 0.0 copy-done.3
  30.2 0.7 %copy.11 = f32[2,8,16,128]{3,2,1,0:T(8,128)} copy(f32[2,8,16,128]{3,1,2,0:T(8,128)S(1)} %bitcast.18) | data formatting | bytes 262144
  30.9 0.0 copy-start
  30.9 7.5 %shard_map.84.rest_0_ = f32[2,4096,128]{2,1,0:T(8,128)} custom-call(bf16[2,1024,128]{2,1,0:T(8,128)(2,1)} %get-tuple-element.20.rim_ref, bf16[2,3072,128]{2,1,0:T(8,128)(2,1)} %get-tuple-element.21.inner_ref, f32[16,16,128]{2,1,0:T(8,128)} %bitcast.10, f32[16,16,128]{2,1,0:T(8,128)} %bitcast.14, f32[16,128]{1,0:T(8,128)} %bitcast.19), custom_call_target="tpu_custom_call" | custom-call | flops 36700160 | bytes 3145728 | tf_op jit(solution)/shard_map/pallas_call | solution.py:285
  38.3 0.0 all-to-all-done.ends_ref
  38.3 0.0 copy-done
  38.3 0.7 %shard_map.85 = f32[16,16,128]{2,1,0:T(8,128)} custom-call(s32[1]{0:T(128)} %bitcast.1.place_ref, f32[16,16,128]{2,1,0:T(8,128)S(1)} %bitcast.13, f32[16,16,128]{2,1,0:T(8,128)S(1)} %all-to-all-done.ends_ref), custom_call_target="tpu_custom_call" | custom-call | tf_op jit(solution)/shard_map/pallas_call | solution.py:309
  39.0 6.0 %all-to-all-start.1 = ((f32[16,16,128]{2,1,0:T(8,128)}), f32[16,16,128]{2,1,0:T(8,128)S(1)}, u32[]{:S(2)}, u32[]{:S(2)}) async-start(f32[16,16,128]{2,1,0:T(8,128)} %shard_map.85), calls=%async_computation.1 | async-start | bytes 262144 | tf_op jit(solution)/shard_map/all_to_all | solution.py:316
  45.0 7.4 %shard_map.86.sums_ref = f32[2,4096,128]{2,1,0:T(8,128)} custom-call(bf16[2,1024,128]{2,1,0:T(8,128)(2,1)} %get-tuple-element.20.rim_ref, bf16[2,3072,128]{2,1,0:T(8,128)(2,1)} %get-tuple-element.21.inner_ref, f32[16,16,128]{2,1,0:T(8,128)} %bitcast.11, f32[16,16,128]{2,1,0:T(8,128)} %bitcast.15, ...), custom_call_target="tpu_custom_call", output_to_operand_aliasing={{}: (5, {})} | custom-call | flops 36700160 | bytes 3145728 | tf_op jit(solution)/shard_map/pallas_call | solution.py:285
  52.5 0.5 all-to-all-done.1.start_ref
  53.0 0.0 copy-start.2
  53.0 0.6 copy-done.2
  53.6 13.1 %shard_map.87 = bf16[2048,512]{1,0:T(8,128)(2,1)} custom-call(f32[2,4096,128]{2,1,0:T(8,128)} %shard_map.86.sums_ref, bf16[2048,512]{1,0:T(8,128)(2,1)} %gate_ref.5, f32[16,16,128]{2,1,0:T(8,128)} %bitcast.12, f32[16,16,128]{2,1,0:T(8,128)} %bitcast.16, f32[16,16,128]{2,1,0:T(8,128)} %copy-done.2), custom_call_target="tpu_custom_call" | custom-call | flops 41943040 | bytes 8388608 | tf_op jit(solution)/shard_map/pallas_call | solution.py:322
Async XLA Ops:
  1.1 15.4 %collective-permute-start = (bf16[2048,128]{1,0:T(8,128)(2,1)S(1)}, bf16[2048,128]{1,0:T(8,128)(2,1)S(1)}, u32[]{:S(2)}, u32[]{:S(2)}) collective-permute-start(bf16[2048,128]{1,0:T(8,128)(2,1)S(1)} %slice.3), channel_id=1, source_target_pairs={{0,2},{2,4},{4,6},{6,8},{8,10},{10,12},{12,14},{14,16},{16,18},{18... | collective-permute-start | bytes 1572872 | tf_op jit(solution)/shard_map/ppermute | solution.py:237
  16.5 0.8 %copy-start.1 = (bf16[2048,128]{1,0:T(8,128)(2,1)}, bf16[2048,128]{1,0:T(8,128)(2,1)S(1)}, u32[]{:S(2)}) copy-start(bf16[2048,128]{1,0:T(8,128)(2,1)S(1)} %collective-permute-done.before_ref) | copy-start | bytes 1572868
  17.3 12.9 %copy-start.3 = (f32[2048,16]{0,1:T(8,128)S(1)}, f32[2048,16]{0,1:T(8,128)}, u32[]{:S(2)}) copy-start(f32[2048,16]{0,1:T(8,128)} %param.13) | copy-start | bytes 393220
  23.0 15.4 %all-to-all-start = ((f32[16,16,128]{2,1,0:T(8,128)}), f32[16,16,128]{2,1,0:T(8,128)S(1)}, u32[]{:S(2)}, u32[]{:S(2)}) async-start(f32[16,16,128]{2,1,0:T(8,128)} %get-tuple-element.18), calls=%async_computation | async-start | bytes 262144 | tf_op jit(solution)/shard_map/all_to_all | solution.py:305
  30.9 7.5 %copy-start = (f32[2,8,16,128]{3,2,1,0:T(8,128)S(1)}, f32[2,8,16,128]{3,2,1,0:T(8,128)}, u32[]{:S(2)}) copy-start(f32[2,8,16,128]{3,2,1,0:T(8,128)} %copy.10) | copy-start | bytes 393220
  39.0 13.9 %all-to-all-start.1 = ((f32[16,16,128]{2,1,0:T(8,128)}), f32[16,16,128]{2,1,0:T(8,128)S(1)}, u32[]{:S(2)}, u32[]{:S(2)}) async-start(f32[16,16,128]{2,1,0:T(8,128)} %shard_map.85), calls=%async_computation.1 | async-start | bytes 262144 | tf_op jit(solution)/shard_map/all_to_all | solution.py:316
  53.0 0.6 copy-start.2

commit v4 on v2

--- a/solution.py
+++ b/solution.py
@@ -13,7 +13,7 @@
 SUBS = 8
 TILE = LANES * SUBS
 BLOCK = 128
-ROWS = 256
+ROWS = 1024
 STEPS = 8
 F32, BF16 = jnp.float32, jnp.bfloat16
 
@@ -72,6 +72,12 @@
         store[pl.ds(block_at * BLOCK * SUBS + group, BLOCK, stride=SUBS), :] = turned
 
 
+def lay_out(rows_ref, store):
+    modes = rows_ref.shape[0]
+    for group in range(SUBS):
+        store[pl.ds(group, modes, stride=SUBS), :] = rows_ref[:, group * LANES : (group + 1) * LANES]
+
+
 def end_states(store, mixed_ref, rates_ref):
     modes = rates_ref.shape[0]
     steps = store.shape[0] // SUBS
@@ -90,7 +96,9 @@
     return lax.fori_loop(0, steps // STEPS, turn, zeros)
 
 
-def inner_kernel(v_ref, gate_ref, taps_ref, rates_ref, tables, spec_ref, mixed_ref, state_ref, store):
+def inner_kernel(v_ref, gate_ref, taps_ref, raw_ref, tables, spec_ref, mixed_ref, state_ref, rates_ref, store, laid):
+    lay_out(raw_ref, laid)
+    rates_ref[...] = laid[...].reshape(rates_ref.shape)
     blocks = v_ref.shape[1] // BLOCK
     sign = 1.0 - 2.0 * (lax.broadcasted_iota(jnp.int32, (1, 2 * BLOCK), 1) % 2).astype(F32)
     for first in range(0, TILE, ROWS):
@@ -123,56 +131,56 @@
     plane = len(piece_refs)
     share = ends.shape[0] // plane
     for ahead, piece in enumerate(piece_refs):
-        piece[...] = ends[pl.ds(lax.rem(place_ref[0] + ahead, plane) * share, share)]
+        piece[...] = ends[pl.ds((place_ref[0] + ahead) % plane * share, share)]
 
 
 def decayed(rates, positions):
     return jnp.exp(-lax.convert_element_type(positions, F32) * rates)
 
 
-def total_kernel(tokens, place_ref, rates_ref, *rest):
-    *ends, total_ref = rest
-    plane, share = len(ends), total_ref.shape[0]
+def chip_kernel(tokens, place_ref, rates_ref, mine_ref, other_ref, total_ref):
+    half = total_ref.shape[0]
+    core = place_ref[0] % 2
+    rates = rates_ref[pl.ds(core * half, half)]
+    total_ref[...] = decayed(rates, tokens * (1 - core)) * mine_ref[...] + decayed(rates, tokens * core) * other_ref[...]
+
+
+def level_kernel(tokens, size, place_ref, rates_ref, total_ref, other_ref, before_ref, joined_ref, after_ref):
+    half = total_ref.shape[0]
     place = place_ref[0]
-    for mode in range(share):
-        rates = rates_ref[place * share + mode]
-        total = None
-        for behind, end in enumerate(ends):
-            owner = lax.rem(place - behind + plane, plane)
-            term = decayed(rates, tokens * (plane - 1 - owner)) * end[mode]
-            total = term if total is None else total + term
-        total_ref[mode] = total
-
-
-def start_kernel(tokens, planes, place_ref, rates_ref, *rest):
-    plane = (len(rest) - (planes - 1)) // 2
-    ends, totals, starts = rest[:plane], rest[plane : plane + planes - 1], rest[plane + planes - 1 :]
-    share = starts[0].shape[0]
+    upper = place // size % 2
+    rates = rates_ref[pl.ds(place % 2 * half, half)]
+    joined_ref[...] = (
+        decayed(rates, tokens * size * (1 - upper)) * total_ref[...]
+        + decayed(rates, tokens * size * upper) * other_ref[...]
+    )
+    reach = decayed(rates, tokens * (place % size // 2 * 2)) * other_ref[...]
+    after_ref[...] = before_ref[...] + jnp.where(upper == 1, reach, 0.0)
+
+
+def start_kernel(tokens, size, place_ref, rates_ref, other_ref, before_ref, own_ref, twin_ref, mine_ref, twins_ref):
+    half = own_ref.shape[0]
     place = place_ref[0]
-    for mode in range(share):
-        rates = rates_ref[place * share + mode]
-        base = totals[0][mode]
-        for behind in range(1, planes - 1):
-            base = base + jnp.exp(-float(tokens * plane * behind) * rates) * totals[behind][mode]
-        for ahead in range(plane):
-            target = lax.rem(place + ahead, plane)
-            start = decayed(rates, tokens * target) * base
-            for behind, end in enumerate(ends):
-                owner = lax.rem(place - behind + plane, plane)
-                gap = target - 1 - owner
-                term = decayed(rates, tokens * jnp.maximum(gap, 0)) * end[mode]
-                start = start + jnp.where(gap >= 0, term, 0.0)
-            starts[ahead][mode] = start
-
-
-def outer_kernel(seq_total, place_ref, rim_ref, inner_ref, gate_ref, rates_ref, weights_ref, bias_ref, *rest):
-    *start_refs, out_ref, store, begin = rest
+    core = place % 2
+    upper = place // size % 2
+    rates = rates_ref[pl.ds(core * half, half)]
+    reach = decayed(rates, tokens * (place % size // 2 * 2)) * other_ref[...]
+    first = before_ref[...] + jnp.where(upper == 1, reach, 0.0)
+    second = decayed(rates, tokens) * first + jnp.where(core == 0, own_ref[...], twin_ref[...])
+    mine_ref[...] = jnp.where(core == 0, first, second)
+    twins_ref[...] = jnp.where(core == 0, second, first)
+
+
+def outer_kernel(seq_total, place_ref, rim_ref, inner_ref, gate_ref, rates_ref, raw_ref, bias_ref, *rest):
+    *start_refs, out_ref, store, begin, laid = rest
+    lay_out(raw_ref, laid)
     modes, plane = rates_ref.shape[0], len(start_refs)
     share = modes // plane
     for behind, ref in enumerate(start_refs):
-        begin[pl.ds(lax.rem(place_ref[0] - behind + plane, plane) * share, share)] = ref[...]
+        begin[pl.ds((place_ref[0] + behind) % plane * share, share)] = ref[...]
     decay = [jnp.exp(-rates_ref[mode]) for mode in range(modes)]
-    scaled = [weights_ref[mode] * jnp.sqrt(2.0 * rates_ref[mode] + 2.0 / seq_total) for mode in range(modes)]
+    weights = [laid[mode * SUBS : (mode + 1) * SUBS] for mode in range(modes)]
+    scaled = [weights[mode] * jnp.sqrt(2.0 * rates_ref[mode] + 2.0 / seq_total) for mode in range(modes)]
     bias = bias_ref[...]
     states = tuple(begin[mode] for mode in range(modes))
     first = 0
@@ -204,6 +212,8 @@
 
 
 SCALAR = pl.BlockSpec(memory_space=pltpu.SMEM)
+WHOLE = pl.BlockSpec(memory_space=pltpu.VMEM)
+RIM_ROOM = 40
 
 
 def call(kernel, tiles, in_specs, out_specs, out_shape, scratch, flops, moved, room):
@@ -249,93 +259,79 @@
     decay_rates, residues, skip_bias, before = map(padded, (decay_rates, residues, skip_bias, before))
     channels = real_channels + extra
     tiles, groups = channels // TILE, channels // LANES
-    rates = decay_rates.T.reshape(modes, groups, LANES)
-    weights = residues.T.reshape(modes, groups, LANES)
+    raw_rates, raw_weights = decay_rates.T, residues.T
     bias = skip_bias.reshape(groups, LANES)
     tables = jnp.asarray(window_tables())
     tables_spec = pl.BlockSpec(tables.shape, lambda i: (0, 0))
-    planes = 4 if shards % 4 == 0 else 1
-    plane = shards // planes
-    share = modes // plane
-    place = (lax.axis_index("seq") % plane).astype(jnp.int32).reshape(1)
+    place = lax.axis_index("seq").astype(jnp.int32).reshape(1)
     inner = tokens - BLOCK
     shape = jax.ShapeDtypeStruct
     per_mode = shape((modes, groups, LANES), F32)
-    piece = shape((share, groups, LANES), F32)
-    spectrum, inner_mixed, inner_state = call(
+    half = shape((modes // 2, groups, LANES), F32)
+    raw_spec = pl.BlockSpec((modes, TILE), lambda i: (0, i))
+    rates_spec, half_spec = modes_spec(modes), modes_spec(modes // 2)
+    laid = pltpu.VMEM((modes * SUBS, LANES), F32)
+    spectrum, inner_mixed, inner_state, rates = call(
         inner_kernel,
         tiles,
-        [rows_spec(tokens), rows_spec(tokens), rows_spec(BLOCK), modes_spec(modes), tables_spec],
-        [rows_spec(2 * BLOCK), steps_spec(inner), modes_spec(modes)],
-        [shape((channels, 2 * BLOCK), F32), shape((tiles, inner * SUBS, LANES), BF16), per_mode],
-        [steps_scratch(inner)],
+        [rows_spec(tokens), rows_spec(tokens), rows_spec(BLOCK), raw_spec, tables_spec],
+        [rows_spec(2 * BLOCK), steps_spec(inner), rates_spec, rates_spec],
+        [shape((channels, 2 * BLOCK), F32), shape((tiles, inner * SUBS, LANES), BF16), per_mode, per_mode],
+        [steps_scratch(inner), laid],
         channels * inner * 2600,
         channels * tokens * 8,
         56,
-    )(v_stream, gate_one, short_filter, rates, tables)
-    rim_mixed, *ends = call(
+    )(v_stream, gate_one, short_filter, raw_rates, tables)
+    rim_mixed, own_end, twin_half = call(
         functools.partial(rim_kernel, inner),
         tiles,
         [SCALAR, rows_spec(BLOCK), rows_spec(BLOCK), rows_spec(BLOCK), rows_spec(2 * BLOCK)]
-        + [modes_spec(modes), modes_spec(modes), tables_spec],
-        [steps_spec(BLOCK)] + [modes_spec(share)] * plane,
-        [shape((tiles, BLOCK * SUBS, LANES), BF16)] + [piece] * plane,
+        + [rates_spec, rates_spec, tables_spec],
+        [steps_spec(BLOCK), half_spec, half_spec],
+        [shape((tiles, BLOCK * SUBS, LANES), BF16), half, half],
         [steps_scratch(BLOCK), pltpu.VMEM((modes, SUBS, LANES), F32)],
         channels * BLOCK * 2600,
         channels * BLOCK * 16,
-        40,
+        RIM_ROOM,
     )(place, before, v_stream, gate_one, spectrum, rates, inner_state, tables)
 
-    def round_plane(pieces):
-        turned = [pieces[0]]
-        for ahead in range(1, plane):
-            route = [(g * plane + i, g * plane + (i + ahead) % plane) for g in range(planes) for i in range(plane)]
-            turned.append(lax.ppermute(pieces[ahead], "seq", route))
-        return turned
-
-    arrived = round_plane(ends)
-    pieces_spec, rates_spec = modes_spec(share), modes_spec(modes)
-    total = call(
-        functools.partial(total_kernel, tokens),
-        tiles,
-        [SCALAR, rates_spec] + [pieces_spec] * plane,
-        pieces_spec,
-        piece,
-        [],
-        1 << 20,
-        1 << 18,
-        4,
-    )(place, rates, *arrived)
-    totals = [
-        lax.ppermute(total, "seq", [(i, i + step * plane) for i in range(shards - step * plane)])
-        for step in range(1, planes)
-    ]
-    starts = call(
-        functools.partial(start_kernel, tokens, planes),
-        tiles,
-        [SCALAR, rates_spec] + [pieces_spec] * (plane + planes - 1),
-        [pieces_spec] * plane,
-        [piece] * plane,
-        [],
-        1 << 20,
-        1 << 18,
-        4,
-    )(place, rates, *arrived, *totals)
-    starts = round_plane(starts)
+    def swap(array, distance):
+        return lax.ppermute(array, "seq", [(i, i ^ distance) for i in range(shards)])
+
+    def small(kernel, outputs, *arrays):
+        return pl.pallas_call(
+            kernel,
+            in_specs=[SCALAR] + [WHOLE] * (len(arrays) + 1),
+            out_specs=[WHOLE] * outputs,
+            out_shape=[half] * outputs,
+            compiler_params=pltpu.CompilerParams(vmem_limit_bytes=8 << 20),
+        )(place, rates, *arrays)
+
+    twin_end = swap(twin_half, 1)
+    (total,) = small(functools.partial(chip_kernel, tokens), 1, own_end, twin_end)
+    ahead = jnp.zeros(half.shape, F32)
+    size = 2
+    while 2 * size < shards:
+        total, ahead = small(functools.partial(level_kernel, tokens, size), 2, total, swap(total, size), ahead)
+        size *= 2
+    mine, twins = small(
+        functools.partial(start_kernel, tokens, size), 2, swap(total, size), ahead, own_end, twin_end
+    )
+    starts = [mine, swap(twins, 1)]
 
     hyena_out = call(
         functools.partial(outer_kernel, tokens * shards),
         tiles,
-        [SCALAR, steps_spec(BLOCK), steps_spec(inner), rows_spec(tokens), rates_spec, rates_spec]
+        [SCALAR, steps_spec(BLOCK), steps_spec(inner), rows_spec(tokens), rates_spec, raw_spec]
         + [pl.BlockSpec((SUBS, LANES), lambda i: (i, 0))]
-        + [pieces_spec] * plane,
+        + [half_spec] * 2,
         rows_spec(tokens),
         shape((channels, tokens), BF16),
-        [steps_scratch(tokens), pltpu.VMEM((modes, SUBS, LANES), F32)],
+        [steps_scratch(tokens), pltpu.VMEM((modes, SUBS, LANES), F32), laid],
         channels * tokens * 70,
         channels * tokens * 6,
         40,
-    )(place, rim_mixed, inner_mixed, gate_two, rates, weights, bias, *starts)
+    )(place, rim_mixed, inner_mixed, gate_two, rates, raw_weights, bias, *starts)
     return hyena_out[:real_channels]
 
 

time: 60.1 us -> 52.9 us (0.88); the launches traced: 59.1 us -> 52.7 us
  starting transfers between devices: 17.7 us -> 11 us
  waiting for transfers between devices: 6.19 us -> 10.2 us
  Pallas kernels: 29.9 us -> 26.8 us
  local copies, waits for them, and re-layouts: 5.22 us -> 4.51 us
    ppermute x9 -> x5, starting transfers between devices: 15.3 us -> 8.62 us  [swap(): lax.ppermute(array, 'seq', [(i, i ^ distance) for i in range(shards)])]
    ppermute x9 -> x5, waiting for transfers between devices: 6.18 us -> 10.2 us  [swap(): lax.ppermute(array, 'seq', [(i, i ^ distance) for i in range(shards)])]
    pallas_call x1, Pallas kernels: 13.5 us -> 11.3 us  [on_device(): call(inner_kernel, tiles, [rows_spec(tokens), rows_spec(tokens), rows_spe...]
    unnamed x22 -> x20, local copies, waits for them, and re-layouts: 4.15 us -> 3.43 us
    pallas_call x1, Pallas kernels: 3.79 us -> 3.17 us  [on_device(): call(functools.partial(rim_kernel, inner), tiles, [SCALAR, rows_spec(BLOC...]
  transfers between devices with their start and end apart: 10 -> 6, of which waited for: 6 -> 5; matrix products, arithmetic and copies ran while one was open for 3% -> 0% of each run, Pallas kernels for 23% -> 22%
where the time goes in v4:
time: 52.9 us; the launch traced here: 52.7 us
  Pallas kernels  26.8 us (51%)
  starting transfers between devices  11 us (21%)
  waiting for transfers between devices  10.2 us (19%)
  local copies, waits for them, and re-layouts  4.51 us (9%)
    pallas_call x1, Pallas kernels, on_device(): call(functools.partial(outer_kernel, tokens * shards), tiles, [SCALAR, st...  12.1 us
    pallas_call x1, Pallas kernels, on_device(): call(inner_kernel, tiles, [rows_spec(tokens), rows_spec(tokens), rows_spe...  11.3 us
    ppermute x5, waiting for transfers between devices, swap(): lax.ppermute(array, 'seq', [(i, i ^ distance) for i in range(shards)])  10.2 us
    ppermute x5, starting transfers between devices, swap(): lax.ppermute(array, 'seq', [(i, i ^ distance) for i in range(shards)])  8.62 us
    unnamed x20, local copies, waits for them, and re-layouts  3.43 us
    pallas_call x1, Pallas kernels, on_device(): call(functools.partial(rim_kernel, inner), tiles, [SCALAR, rows_spec(BLOC...  3.17 us
    ppermute x1, starting transfers between devices, on_device(): lax.ppermute(v_stream[:, tokens - BLOCK:], 'seq', [(i, i + 1) for i in ra...  2.39 us
    slice x1, local copies, waits for them, and re-layouts, on_device(): v_stream[:, tokens - BLOCK:]  1.08 us
  transfers between devices with their start and end apart: 6, of which 5 were waited for; matrix products, arithmetic and copies ran while one was open for 0% of the time, Pallas kernels for 22%

profile of v4, /device:TPU:0, one launch (start us, length us, event | category | flops | bytes accessed | tf_op | source)
XLA Modules:
  0.0 52.7 jit_solution(10055649694215539618)
XLA Ops:
  0.0 1.1 %slice.3 = bf16[2048,128]{1,0:T(8,128)(2,1)S(1)} slice(bf16[2048,512]{1,0:T(8,128)(2,1)} %v_ref.3), slice={[0:2048], [384:512]} | slice | bytes 1048576 | tf_op jit(solution)/shard_map/slice | solution.py:252
  1.1 2.4 %collective-permute-start = (bf16[2048,128]{1,0:T(8,128)(2,1)S(1)}, bf16[2048,128]{1,0:T(8,128)(2,1)S(1)}, u32[]{:S(2)}, u32[]{:S(2)}) collective-permute-start(bf16[2048,128]{1,0:T(8,128)(2,1)S(1)} %slice.3), channel_id=1, source_target_pairs={{0,2},{2,4},{4,6},{6,8},{8,10},{10,12},{12,14},{14,16},{16,18},{18... | collective-permute-start | bytes 1572872 | tf_op jit(solution)/shard_map/ppermute | solution.py:252
  3.5 0.0 copy-start.1
  3.5 0.0 copy-start.2
  3.5 0.0 copy-start.6
  3.5 11.3 %shard_map.82 = (f32[2048,256]{1,0:T(8,128)}, bf16[2,3072,128]{2,1,0:T(8,128)(2,1)}, f32[16,16,128]{2,1,0:T(8,128)}, f32[16,16,128]{2,1,0:T(8,128)}) custom-call(bf16[2048,512]{1,0:T(8,128)(2,1)} %v_ref.3, bf16[2048,512]{1,0:T(8,128)(2,1)} %gate_ref.4, f32[2048,128]{1,0:T(8,128)} %taps_ref.1, f32[16,2048]{1,0:T(8,128)} %bitcast.6, ...), custom_call_target="tpu_custom_call" | custom-call | flops 2044723200 | bytes 8388608 | tf_op jit(solution)/shard_map/pallas_call | solution.py:274
  14.9 0.0 collective-permute-done.before_ref
  14.9 0.0 copy-done.1
  14.9 0.0 copy-done.2
  14.9 0.9 %copy-done = f32[16,16,128]{2,1,0:T(8,128)S(1)} copy-done((f32[16,16,128]{2,1,0:T(8,128)S(1)}, f32[16,16,128]{2,1,0:T(8,128)}, u32[]{:S(2)}) %copy-start) | copy-done | bytes 131096
  15.8 1.6 %copy-done.4 = f32[2048,256]{1,0:T(8,128)S(1)} copy-done((f32[2048,256]{1,0:T(8,128)S(1)}, f32[2048,256]{1,0:T(8,128)}, u32[]{:S(2)}) %copy-start.4) | copy-done | bytes 2097176
  17.4 0.9 %copy-done.7 = f32[16,16,128]{2,1,0:T(8,128)S(1)} copy-done((f32[16,16,128]{2,1,0:T(8,128)S(1)}, f32[16,16,128]{2,1,0:T(8,128)}, u32[]{:S(2)}) %copy-start.7) | copy-done | bytes 131096
  18.3 3.2 %shard_map.83 = (bf16[2,1024,128]{2,1,0:T(8,128)(2,1)S(1)}, f32[8,16,128]{2,1,0:T(8,128)S(1)}, f32[8,16,128]{2,1,0:T(8,128)S(1)}) custom-call(s32[1]{0:T(128)} %bitcast.place_ref, bf16[2048,128]{1,0:T(8,128)(2,1)S(1)} %collective-permute-done.before_ref, bf16[2048,512]{1,0:T(8,128)(2,1)S(1)} %copy-done.1, bf16[2048,512]{1,0:T(8,128)(2,1)S(1)} %copy-done.2, ...), custom_call_target="tpu_custom_call" | custom-call | flops 681574400 | bytes 4194304 | tf_op jit(solution)/shard_map/pallas_call | solution.py:285
  21.5 2.7 %collective-permute-start.1 = (f32[8,16,128]{2,1,0:T(8,128)S(1)}, f32[8,16,128]{2,1,0:T(8,128)S(1)}, u32[]{:S(2)}, u32[]{:S(2)}) collective-permute-start(f32[8,16,128]{2,1,0:T(8,128)S(1)} %get-tuple-element.24), channel_id=1, source_target_pairs={{0,2},{2,0},{4,6},{6,4},{8,10},{10,8},{12,14},{14,12},{16,18},{18,... | collective-permute-start | bytes 196616 | tf_op jit(solution)/shard_map/ppermute | solution.py:299
  24.2 0.9 %collective-permute-done.1.other_ref.twin_ref = f32[8,16,128]{2,1,0:T(8,128)S(1)} collective-permute-done((f32[8,16,128]{2,1,0:T(8,128)S(1)}, f32[8,16,128]{2,1,0:T(8,128)S(1)}, u32[]{:S(2)}, u32[]{:S(2)}) %collective-permute-start.1) | collective-permute-done | bytes 65568 | tf_op jit(solution)/shard_map/ppermute | solution.py:299
  25.1 1.6 %collective-permute-start.2 = (f32[8,16,128]{2,1,0:T(8,128)S(1)}, f32[8,16,128]{2,1,0:T(8,128)S(1)}, u32[]{:S(2)}, u32[]{:S(2)}) collective-permute-start(f32[8,16,128]{2,1,0:T(8,128)S(1)} %shard_map.84.total_ref), channel_id=1, source_target_pairs={{0,4},{2,6},{4,0},{6,2},{8,12},{10,14},{12,8},{14,10},{16,20},{18,... | collective-permute-start | bytes 196616 | tf_op jit(solution)/shard_map/ppermute | solution.py:299
  26.7 2.8 %collective-permute-done.2.other_ref = f32[8,16,128]{2,1,0:T(8,128)S(1)} collective-permute-done((f32[8,16,128]{2,1,0:T(8,128)S(1)}, f32[8,16,128]{2,1,0:T(8,128)S(1)}, u32[]{:S(2)}, u32[]{:S(2)}) %collective-permute-start.2) | collective-permute-done | bytes 65568 | tf_op jit(solution)/shard_map/ppermute | solution.py:299
  29.6 1.6 %collective-permute-start.3 = (f32[8,16,128]{2,1,0:T(8,128)S(1)}, f32[8,16,128]{2,1,0:T(8,128)S(1)}, u32[]{:S(2)}, u32[]{:S(2)}) collective-permute-start(f32[8,16,128]{2,1,0:T(8,128)S(1)} %get-tuple-element.25.total_ref), channel_id=1, source_target_pairs={{0,8},{2,10},{4,12},{6,14},{8,0},{10,2},{12,4},{14,6},{16,24},{18,... | collective-permute-start | bytes 196616 | tf_op jit(solution)/shard_map/ppermute | solution.py:299
  31.2 2.7 %collective-permute-done.3.other_ref = f32[8,16,128]{2,1,0:T(8,128)S(1)} collective-permute-done((f32[8,16,128]{2,1,0:T(8,128)S(1)}, f32[8,16,128]{2,1,0:T(8,128)S(1)}, u32[]{:S(2)}, u32[]{:S(2)}) %collective-permute-start.3) | collective-permute-done | bytes 65568 | tf_op jit(solution)/shard_map/ppermute | solution.py:299
  33.9 2.7 %collective-permute-start.4 = (f32[8,16,128]{2,1,0:T(8,128)S(1)}, f32[8,16,128]{2,1,0:T(8,128)S(1)}, u32[]{:S(2)}, u32[]{:S(2)}) collective-permute-start(f32[8,16,128]{2,1,0:T(8,128)S(1)} %get-tuple-element.27), channel_id=1, source_target_pairs={{0,16},{2,18},{4,20},{6,22},{8,24},{10,26},{12,28},{14,30},{16,0},... | collective-permute-start | bytes 196616 | tf_op jit(solution)/shard_map/ppermute | solution.py:299
  36.6 2.6 %collective-permute-done.4.other_ref = f32[8,16,128]{2,1,0:T(8,128)S(1)} collective-permute-done((f32[8,16,128]{2,1,0:T(8,128)S(1)}, f32[8,16,128]{2,1,0:T(8,128)S(1)}, u32[]{:S(2)}, u32[]{:S(2)}) %collective-permute-start.4) | collective-permute-done | bytes 65568 | tf_op jit(solution)/shard_map/ppermute | solution.py:299
  39.2 0.1 collective-permute-start.5
  39.3 1.2 %collective-permute-done.5.rest_1_ = f32[8,16,128]{2,1,0:T(8,128)S(1)} collective-permute-done((f32[8,16,128]{2,1,0:T(8,128)S(1)}, f32[8,16,128]{2,1,0:T(8,128)S(1)}, u32[]{:S(2)}, u32[]{:S(2)}) %collective-permute-start.5) | collective-permute-done | bytes 65568 | tf_op jit(solution)/shard_map/ppermute | solution.py:299
  40.6 12.1 %shard_map.88 = bf16[2048,512]{1,0:T(8,128)(2,1)} custom-call(s32[1]{0:T(128)} %bitcast.place_ref, bf16[2,1024,128]{2,1,0:T(8,128)(2,1)S(1)} %get-tuple-element.21.rim_ref, bf16[2,3072,128]{2,1,0:T(8,128)(2,1)S(1)} %copy-done.5, bf16[2048,512]{1,0:T(8,128)(2,1)S(1)} %copy-done.3, f32[16,16,128]{2,1,0:T(8,128)S(1)} %copy-done, f32[16,2048]{1,0:T(8,128)S(1)} %bitcast.4, ...), custom_call_target="tpu_custom_call" | custom-call | flops 73400320 | bytes 6291456 | tf_op jit(solution)/shard_map/pallas_call | solution.py:322
  (17 shorter events, 0.2 us)
Async XLA Ops:
  1.1 13.8 %collective-permute-start = (bf16[2048,128]{1,0:T(8,128)(2,1)S(1)}, bf16[2048,128]{1,0:T(8,128)(2,1)S(1)}, u32[]{:S(2)}, u32[]{:S(2)}) collective-permute-start(bf16[2048,128]{1,0:T(8,128)(2,1)S(1)} %slice.3), channel_id=1, source_target_pairs={{0,2},{2,4},{4,6},{6,8},{8,10},{10,12},{12,14},{14,16},{16,18},{18... | collective-permute-start | bytes 1572872 | tf_op jit(solution)/shard_map/ppermute | solution.py:252
  3.5 11.4 %copy-start.1 = (bf16[2048,512]{1,0:T(8,128)(2,1)S(1)}, bf16[2048,512]{1,0:T(8,128)(2,1)}, u32[]{:S(2)}) copy-start(bf16[2048,512]{1,0:T(8,128)(2,1)} %v_ref.3) | copy-start | bytes 6291460
  3.5 11.4 %copy-start.2 = (bf16[2048,512]{1,0:T(8,128)(2,1)S(1)}, bf16[2048,512]{1,0:T(8,128)(2,1)}, u32[]{:S(2)}) copy-start(bf16[2048,512]{1,0:T(8,128)(2,1)} %gate_ref.4) | copy-start | bytes 6291460
  3.5 11.4 %copy-start.6 = (bf16[256,768]{1,0:T(8,128)(2,1)S(1)}, bf16[256,768]{1,0:T(8,128)(2,1)}, u32[]{:S(2)}) copy-start(bf16[256,768]{1,0:T(8,128)(2,1)} %constant.10.clone.tables) | copy-start | bytes 1179652
  14.9 0.9 %copy-start = (f32[16,16,128]{2,1,0:T(8,128)S(1)}, f32[16,16,128]{2,1,0:T(8,128)}, u32[]{:S(2)}) copy-start(f32[16,16,128]{2,1,0:T(8,128)} %get-tuple-element.19.rates_ref) | copy-start | bytes 393220
  15.8 1.6 %copy-start.4 = (f32[2048,256]{1,0:T(8,128)S(1)}, f32[2048,256]{1,0:T(8,128)}, u32[]{:S(2)}) copy-start(f32[2048,256]{1,0:T(8,128)} %get-tuple-element.18.spec_ref) | copy-start | bytes 6291460
  17.4 0.9 %copy-start.7 = (f32[16,16,128]{2,1,0:T(8,128)S(1)}, f32[16,16,128]{2,1,0:T(8,128)}, u32[]{:S(2)}) copy-start(f32[16,16,128]{2,1,0:T(8,128)} %get-tuple-element.20.inner_ref) | copy-start | bytes 393220
  18.3 22.2 %copy-start.3 = (bf16[2048,512]{1,0:T(8,128)(2,1)S(1)}, bf16[2048,512]{1,0:T(8,128)(2,1)}, u32[]{:S(2)}) copy-start(bf16[2048,512]{1,0:T(8,128)(2,1)} %gate_ref.5) | copy-start | bytes 6291460
  18.3 22.2 %copy-start.5 = (bf16[2,3072,128]{2,1,0:T(8,128)(2,1)S(1)}, bf16[2,3072,128]{2,1,0:T(8,128)(2,1)}, u32[]{:S(2)}) copy-start(bf16[2,3072,128]{2,1,0:T(8,128)(2,1)} %get-tuple-element.22.inner_ref) | copy-start | bytes 4718596
  18.3 22.2 %copy-start.8 = (f32[2048,16]{0,1:T(8,128)S(1)}, f32[2048,16]{0,1:T(8,128)}, u32[]{:S(2)}) copy-start(f32[2048,16]{0,1:T(8,128)} %param.13) | copy-start | bytes 393220
  18.3 22.2 %copy-start.9 = (f32[2048]{0:T(1024)S(1)}, f32[2048]{0:T(1024)}, u32[]{:S(2)}) copy-start(f32[2048]{0:T(1024)} %param.14) | copy-start | bytes 24580
  21.5 3.6 %collective-permute-start.1 = (f32[8,16,128]{2,1,0:T(8,128)S(1)}, f32[8,16,128]{2,1,0:T(8,128)S(1)}, u32[]{:S(2)}, u32[]{:S(2)}) collective-permute-start(f32[8,16,128]{2,1,0:T(8,128)S(1)} %get-tuple-element.24), channel_id=1, source_target_pairs={{0,2},{2,0},{4,6},{6,4},{8,10},{10,8},{12,14},{14,12},{16,18},{18,... | collective-permute-start | bytes 196616 | tf_op jit(solution)/shard_map/ppermute | solution.py:299
  25.1 4.4 %collective-permute-start.2 = (f32[8,16,128]{2,1,0:T(8,128)S(1)}, f32[8,16,128]{2,1,0:T(8,128)S(1)}, u32[]{:S(2)}, u32[]{:S(2)}) collective-permute-start(f32[8,16,128]{2,1,0:T(8,128)S(1)} %shard_map.84.total_ref), channel_id=1, source_target_pairs={{0,4},{2,6},{4,0},{6,2},{8,12},{10,14},{12,8},{14,10},{16,20},{18,... | collective-permute-start | bytes 196616 | tf_op jit(solution)/shard_map/ppermute | solution.py:299
  29.6 4.3 %collective-permute-start.3 = (f32[8,16,128]{2,1,0:T(8,128)S(1)}, f32[8,16,128]{2,1,0:T(8,128)S(1)}, u32[]{:S(2)}, u32[]{:S(2)}) collective-permute-start(f32[8,16,128]{2,1,0:T(8,128)S(1)} %get-tuple-element.25.total_ref), channel_id=1, source_target_pairs={{0,8},{2,10},{4,12},{6,14},{8,0},{10,2},{12,4},{14,6},{16,24},{18,... | collective-permute-start | bytes 196616 | tf_op jit(solution)/shard_map/ppermute | solution.py:299
  33.9 5.2 %collective-permute-start.4 = (f32[8,16,128]{2,1,0:T(8,128)S(1)}, f32[8,16,128]{2,1,0:T(8,128)S(1)}, u32[]{:S(2)}, u32[]{:S(2)}) collective-permute-start(f32[8,16,128]{2,1,0:T(8,128)S(1)} %get-tuple-element.27), channel_id=1, source_target_pairs={{0,16},{2,18},{4,20},{6,22},{8,24},{10,26},{12,28},{14,30},{16,0},... | collective-permute-start | bytes 196616 | tf_op jit(solution)/shard_map/ppermute | solution.py:299
  39.2 1.3 %collective-permute-start.5 = (f32[8,16,128]{2,1,0:T(8,128)S(1)}, f32[8,16,128]{2,1,0:T(8,128)S(1)}, u32[]{:S(2)}, u32[]{:S(2)}) collective-permute-start(f32[8,16,128]{2,1,0:T(8,128)S(1)} %get-tuple-element.30), channel_id=1, source_target_pairs={{0,2},{2,0},{4,6},{6,4},{8,10},{10,8},{12,14},{14,12},{16,18},{18,... | collective-permute-start | bytes 196616 | tf_op jit(solution)/shard_map/ppermute | solution.py:299

commit v5 on v4

--- a/solution.py
+++ b/solution.py
@@ -96,42 +96,72 @@
     return lax.fori_loop(0, steps // STEPS, turn, zeros)
 
 
-def inner_kernel(v_ref, gate_ref, taps_ref, raw_ref, tables, spec_ref, mixed_ref, state_ref, rates_ref, store, laid):
-    lay_out(raw_ref, laid)
-    rates_ref[...] = laid[...].reshape(rates_ref.shape)
-    blocks = v_ref.shape[1] // BLOCK
+def inner_kernel(
+    v_hbm, gate_hbm, taps_hbm, raw_hbm, tables_hbm,
+    spec_ref, mixed_ref, state_ref, rates_ref, v_first, gate_first, tables,
+    v_rest, gate_rest, taps, raw, store, laid, sems,
+):
+    tiles, inner = mixed_ref.shape[0], v_rest.shape[1]
+
+    def copies(tile):
+        rows = pl.ds(tile * TILE, TILE)
+        pairs = [(taps_hbm.at[rows], taps.at[rows])]
+        for whole, head, rest in ((v_hbm, v_first, v_rest), (gate_hbm, gate_first, gate_rest)):
+            pairs.append((whole.at[rows, pl.ds(0, BLOCK)], head.at[rows]))
+            pairs.append((whole.at[rows, pl.ds(BLOCK, inner)], rest.at[rows]))
+        return [pltpu.make_async_copy(*pair, sems.at[tile * 5 + i]) for i, pair in enumerate(pairs)]
+
+    small = [
+        pltpu.make_async_copy(tables_hbm, tables, sems.at[tiles * 5]),
+        pltpu.make_async_copy(raw_hbm, raw, sems.at[tiles * 5 + 1]),
+    ]
+    large = [copies(tile) for tile in range(tiles)]
+    for copy in small + sum(large, []):
+        copy.start()
+    small[0].wait()
     sign = 1.0 - 2.0 * (lax.broadcasted_iota(jnp.int32, (1, 2 * BLOCK), 1) % 2).astype(F32)
-    for first in range(0, TILE, ROWS):
-        rows = slice(first, first + ROWS)
-        tap_hi, tap_lo = split(taps_ref[rows])
+    for tile in range(tiles):
+        rows = slice(tile * TILE, (tile + 1) * TILE)
+        groups = slice(tile * SUBS, (tile + 1) * SUBS)
+        large[tile][0].wait()
+        tap_hi, tap_lo = split(taps[rows])
         spectrum = mm(twice(tap_hi), tables[:, EVEN]) + mm(tap_lo, tables[:BLOCK, EVEN])
         turned = spectrum * sign
         spec_ref[rows] = turned
-        earlier = mm(twice(v_ref[rows, :BLOCK]), tables[:, EVEN])
-        for block in range(1, blocks):
-            at = slice(block * BLOCK, (block + 1) * BLOCK)
-            later = mm(twice(v_ref[rows, at]), tables[:, ODD if block % 2 else EVEN])
+        for copy in large[tile][1:]:
+            copy.wait()
+        earlier = mm(twice(v_first[rows]), tables[:, EVEN])
+        for block in range(1, inner // BLOCK + 1):
+            at = slice((block - 1) * BLOCK, block * BLOCK)
+            later = mm(twice(v_rest[rows, at]), tables[:, ODD if block % 2 else EVEN])
             short = apply_window(earlier, later, spectrum if block % 2 else turned, tables)
-            put_mixed(store, first, block - 1, short, gate_ref[rows, at])
+            put_mixed(store, 0, block - 1, short, gate_rest[rows, at])
             earlier = later
-    for mode, state in enumerate(end_states(store, mixed_ref, rates_ref)):
-        state_ref[mode] = state
+        if tile == 0:
+            small[1].wait()
+        lay_out(raw.at[:, pl.ds(tile * TILE, TILE)], laid)
+        modes = raw.shape[0]
+        rates_ref[:, groups] = laid[...].reshape(modes, SUBS, LANES)
+        for mode, state in enumerate(end_states(store, mixed_ref.at[tile], rates_ref.at[:, groups])):
+            state_ref[mode, groups] = state
 
 
 def rim_kernel(inner, place_ref, before_ref, v_ref, gate_ref, spec_ref, rates_ref, inner_ref, tables, *rest):
-    mixed_ref, *piece_refs, store, ends = rest
-    for first in range(0, TILE, ROWS):
-        rows = slice(first, first + ROWS)
+    mixed_ref, own_ref, twin_ref, store, ends = rest
+    half = own_ref.shape[0]
+    core = place_ref[0] % 2
+    for tile in range(mixed_ref.shape[0]):
+        rows = slice(tile * TILE, (tile + 1) * TILE)
+        groups = slice(tile * SUBS, (tile + 1) * SUBS)
         earlier = mm(twice(before_ref[rows]), tables[:, ODD])
         later = mm(twice(v_ref[rows]), tables[:, EVEN])
         short = apply_window(earlier, later, spec_ref[rows], tables)
-        put_mixed(store, first, 0, short, gate_ref[rows])
-    for mode, state in enumerate(end_states(store, mixed_ref, rates_ref)):
-        ends[mode] = jnp.exp(-float(inner) * rates_ref[mode]) * state + inner_ref[mode]
-    plane = len(piece_refs)
-    share = ends.shape[0] // plane
-    for ahead, piece in enumerate(piece_refs):
-        piece[...] = ends[pl.ds((place_ref[0] + ahead) % plane * share, share)]
+        put_mixed(store, 0, 0, short, gate_ref[rows])
+        rates = rates_ref.at[:, groups]
+        for mode, state in enumerate(end_states(store, mixed_ref.at[tile], rates)):
+            ends[mode] = jnp.exp(-float(inner) * rates[mode]) * state + inner_ref[mode, groups]
+        own_ref[:, groups] = ends[pl.ds(core * half, half)]
+        twin_ref[:, groups] = ends[pl.ds((1 - core) * half, half)]
 
 
 def decayed(rates, positions):
@@ -213,7 +243,8 @@
 
 SCALAR = pl.BlockSpec(memory_space=pltpu.SMEM)
 WHOLE = pl.BlockSpec(memory_space=pltpu.VMEM)
-RIM_ROOM = 40
+FAR = pl.BlockSpec(memory_space=pltpu.HBM)
+INNER_ROOM, RIM_ROOM = 32, 24
 
 
 def call(kernel, tiles, in_specs, out_specs, out_shape, scratch, flops, moved, room):
@@ -245,6 +276,10 @@
     return pltpu.VMEM((steps * SUBS, LANES), F32)
 
 
+def kept_far(array):
+    return pltpu.with_memory_space_constraint(array, pltpu.HBM)
+
+
 def on_device(v_stream, gate_one, gate_two, short_filter, decay_rates, residues, skip_bias):
     real_channels, tokens = v_stream.shape
     modes = decay_rates.shape[1]
@@ -262,7 +297,6 @@
     raw_rates, raw_weights = decay_rates.T, residues.T
     bias = skip_bias.reshape(groups, LANES)
     tables = jnp.asarray(window_tables())
-    tables_spec = pl.BlockSpec(tables.shape, lambda i: (0, 0))
     place = lax.axis_index("seq").astype(jnp.int32).reshape(1)
     inner = tokens - BLOCK
     shape = jax.ShapeDtypeStruct
@@ -271,29 +305,39 @@
     raw_spec = pl.BlockSpec((modes, TILE), lambda i: (0, i))
     rates_spec, half_spec = modes_spec(modes), modes_spec(modes // 2)
     laid = pltpu.VMEM((modes * SUBS, LANES), F32)
-    spectrum, inner_mixed, inner_state, rates = call(
+    tap_spectra = shape((channels, 2 * BLOCK), F32)
+    head = shape((channels, BLOCK), BF16)
+    spectrum, inner_mixed, inner_state, rates, v_first, gate_first, tables = pl.pallas_call(
         inner_kernel,
-        tiles,
-        [rows_spec(tokens), rows_spec(tokens), rows_spec(BLOCK), raw_spec, tables_spec],
-        [rows_spec(2 * BLOCK), steps_spec(inner), rates_spec, rates_spec],
-        [shape((channels, 2 * BLOCK), F32), shape((tiles, inner * SUBS, LANES), BF16), per_mode, per_mode],
-        [steps_scratch(inner), laid],
-        channels * inner * 2600,
-        channels * tokens * 8,
-        56,
-    )(v_stream, gate_one, short_filter, raw_rates, tables)
-    rim_mixed, own_end, twin_half = call(
+        in_specs=[FAR] * 5,
+        out_specs=[WHOLE] * 7,
+        out_shape=[tap_spectra, shape((tiles, inner * SUBS, LANES), BF16), per_mode, per_mode, head, head]
+        + [shape(tables.shape, BF16)],
+        scratch_shapes=[
+            pltpu.VMEM((channels, inner), BF16),
+            pltpu.VMEM((channels, inner), BF16),
+            pltpu.VMEM((channels, BLOCK), F32),
+            pltpu.VMEM((modes, channels), F32),
+            steps_scratch(inner),
+            laid,
+            pltpu.SemaphoreType.DMA((tiles * 5 + 2,)),
+        ],
+        compiler_params=pltpu.CompilerParams(vmem_limit_bytes=INNER_ROOM << 20),
+        cost_estimate=pl.CostEstimate(
+            flops=channels * inner * 2600, bytes_accessed=channels * tokens * 8, transcendentals=0
+        ),
+    )(*map(kept_far, (v_stream, gate_one, short_filter, raw_rates, tables)))
+    rim_mixed, own_end, twin_half = pl.pallas_call(
         functools.partial(rim_kernel, inner),
-        tiles,
-        [SCALAR, rows_spec(BLOCK), rows_spec(BLOCK), rows_spec(BLOCK), rows_spec(2 * BLOCK)]
-        + [rates_spec, rates_spec, tables_spec],
-        [steps_spec(BLOCK), half_spec, half_spec],
-        [shape((tiles, BLOCK * SUBS, LANES), BF16), half, half],
-        [steps_scratch(BLOCK), pltpu.VMEM((modes, SUBS, LANES), F32)],
-        channels * BLOCK * 2600,
-        channels * BLOCK * 16,
-        RIM_ROOM,
-    )(place, before, v_stream, gate_one, spectrum, rates, inner_state, tables)
+        in_specs=[SCALAR] + [WHOLE] * 7,
+        out_specs=[WHOLE] * 3,
+        out_shape=[shape((tiles, BLOCK * SUBS, LANES), BF16), half, half],
+        scratch_shapes=[steps_scratch(BLOCK), pltpu.VMEM((modes, SUBS, LANES), F32)],
+        compiler_params=pltpu.CompilerParams(vmem_limit_bytes=RIM_ROOM << 20),
+        cost_estimate=pl.CostEstimate(
+            flops=channels * BLOCK * 2600, bytes_accessed=channels * BLOCK * 16, transcendentals=0
+        ),
+    )(place, before, v_first, gate_first, spectrum, rates, inner_state, tables)
 
     def swap(array, distance):
         return lax.ppermute(array, "seq", [(i, i ^ distance) for i in range(shards)])
@@ -330,7 +374,7 @@
         [steps_scratch(tokens), pltpu.VMEM((modes, SUBS, LANES), F32), laid],
         channels * tokens * 70,
         channels * tokens * 6,
-        40,
+        32,
     )(place, rim_mixed, inner_mixed, gate_two, rates, raw_weights, bias, *starts)
     return hyena_out[:real_channels]
 

time: 52.9 us -> 47.9 us (0.905)
  local copies, waits for them, and re-layouts: 4.51 us -> 1.1 us
  Pallas kernels: 26.8 us -> 25.3 us
    unnamed x20 -> x6, local copies, waits for them, and re-layouts: 3.43 us -> 0.02 us
    pallas_call x2, Pallas kernels: 14.5 us -> 13 us  [the longest x1 10.1 us: on_device(): pl.pallas_call(inner_kernel, in_specs=[FAR] * 5, out_specs=[WHOLE] * 7, o...]
  transfers between devices with their start and end apart: 6 -> 6, of which waited for: 5 -> 5; matrix products, arithmetic and copies ran while one was open for 0% -> 0% of each run, Pallas kernels for 22% -> 21%
where the time goes in v5:
time: 47.9 us; the launch traced here: 47.7 us
  Pallas kernels  25.3 us (53%)
  starting transfers between devices  11 us (23%)
  waiting for transfers between devices  10.2 us (21%)
  local copies, waits for them, and re-layouts  1.1 us (2%)
    pallas_call x1, Pallas kernels, on_device(): call(functools.partial(outer_kernel, tokens * shards), tiles, [SCALAR, st...  12.1 us
    ppermute x5, waiting for transfers between devices, swap(): lax.ppermute(array, 'seq', [(i, i ^ distance) for i in range(shards)])  10.2 us
    pallas_call x1, Pallas kernels, on_device(): pl.pallas_call(inner_kernel, in_specs=[FAR] * 5, out_specs=[WHOLE] * 7, o...  10.1 us
    ppermute x5, starting transfers between devices, swap(): lax.ppermute(array, 'seq', [(i, i ^ distance) for i in range(shards)])  8.62 us
    pallas_call x1, Pallas kernels, on_device(): pl.pallas_call(functools.partial(rim_kernel, inner), in_specs=[SCALAR] +...  2.84 us
    ppermute x1, starting transfers between devices, on_device(): lax.ppermute(v_stream[:, tokens - BLOCK:], 'seq', [(i, i + 1) for i in ra...  2.39 us
    slice x1, local copies, waits for them, and re-layouts, on_device(): v_stream[:, tokens - BLOCK:]  1.08 us
  transfers between devices with their start and end apart: 6, of which 5 were waited for; matrix products, arithmetic and copies ran while one was open for 0% of the time, Pallas kernels for 21%

profile of v5, /device:TPU:0, one launch (start us, length us, event | category | flops | bytes accessed | tf_op | source)
XLA Modules:
  0.0 47.7 jit_solution(12428947493672211603)
XLA Ops:
  0.0 1.1 %slice.3 = bf16[2048,128]{1,0:T(8,128)(2,1)S(1)} slice(bf16[2048,512]{1,0:T(8,128)(2,1)} %v_hbm.1), slice={[0:2048], [384:512]} | slice | bytes 1048576 | tf_op jit(solution)/shard_map/slice | solution.py:287
  1.1 2.4 %collective-permute-start = (bf16[2048,128]{1,0:T(8,128)(2,1)S(1)}, bf16[2048,128]{1,0:T(8,128)(2,1)S(1)}, u32[]{:S(2)}, u32[]{:S(2)}) collective-permute-start(bf16[2048,128]{1,0:T(8,128)(2,1)S(1)} %slice.3), channel_id=1, source_target_pairs={{0,2},{2,4},{4,6},{6,8},{8,10},{10,12},{12,14},{14,16},{16,18},{18... | collective-permute-start | bytes 1572872 | tf_op jit(solution)/shard_map/ppermute | solution.py:287
  3.5 10.1 %shard_map.82 = (f32[2048,256]{1,0:T(8,128)S(1)}, bf16[2,3072,128]{2,1,0:T(8,128)(2,1)S(1)}, f32[16,16,128]{2,1,0:T(8,128)S(1)}, f32[16,16,128]{2,1,0:T(8,128)S(...) custom-call(bf16[2048,512]{1,0:T(8,128)(2,1)} %v_hbm.1, ...), custom_call_target="tpu_custom_call" | custom-call | flops 2044723200 | bytes 8388608 | tf_op jit(solution)/shard_map/pallas_call | solution.py:310
  13.6 0.0 collective-permute-done.before_ref
  13.6 0.0 copy-start
  13.6 0.0 copy-start.1
  13.6 0.0 copy-start.2
  13.7 2.8 %shard_map.83 = (bf16[2,1024,128]{2,1,0:T(8,128)(2,1)S(1)}, f32[8,16,128]{2,1,0:T(8,128)S(1)}, f32[8,16,128]{2,1,0:T(8,128)S(1)}) custom-call(s32[1]{0:T(128)} %bitcast.place_ref, bf16[2048,128]{1,0:T(8,128)(2,1)S(1)} %collective-permute-done.before_ref, bf16[2048,128]{1,0:T(8,128)(2,1)S(1)} %get-tuple-element.21.v_ref, ...), custom_call_target="tpu_custom_call" | custom-call | flops 681574400 | bytes 4194304 | tf_op jit(solution)/shard_map/pallas_call | solution.py:330
  16.5 2.7 %collective-permute-start.1 = (f32[8,16,128]{2,1,0:T(8,128)S(1)}, f32[8,16,128]{2,1,0:T(8,128)S(1)}, u32[]{:S(2)}, u32[]{:S(2)}) collective-permute-start(f32[8,16,128]{2,1,0:T(8,128)S(1)} %get-tuple-element.30), channel_id=1, source_target_pairs={{0,2},{2,0},{4,6},{6,4},{8,10},{10,8},{12,14},{14,12},{16,18},{18,... | collective-permute-start | bytes 196616 | tf_op jit(solution)/shard_map/ppermute | solution.py:343
  19.2 0.9 %collective-permute-done.1.other_ref.twin_ref = f32[8,16,128]{2,1,0:T(8,128)S(1)} collective-permute-done((f32[8,16,128]{2,1,0:T(8,128)S(1)}, f32[8,16,128]{2,1,0:T(8,128)S(1)}, u32[]{:S(2)}, u32[]{:S(2)}) %collective-permute-start.1) | collective-permute-done | bytes 65568 | tf_op jit(solution)/shard_map/ppermute | solution.py:343
  20.1 1.6 %collective-permute-start.2 = (f32[8,16,128]{2,1,0:T(8,128)S(1)}, f32[8,16,128]{2,1,0:T(8,128)S(1)}, u32[]{:S(2)}, u32[]{:S(2)}) collective-permute-start(f32[8,16,128]{2,1,0:T(8,128)S(1)} %shard_map.84.total_ref), channel_id=1, source_target_pairs={{0,4},{2,6},{4,0},{6,2},{8,12},{10,14},{12,8},{14,10},{16,20},{18,... | collective-permute-start | bytes 196616 | tf_op jit(solution)/shard_map/ppermute | solution.py:343
  21.7 2.8 %collective-permute-done.2.other_ref = f32[8,16,128]{2,1,0:T(8,128)S(1)} collective-permute-done((f32[8,16,128]{2,1,0:T(8,128)S(1)}, f32[8,16,128]{2,1,0:T(8,128)S(1)}, u32[]{:S(2)}, u32[]{:S(2)}) %collective-permute-start.2) | collective-permute-done | bytes 65568 | tf_op jit(solution)/shard_map/ppermute | solution.py:343
  24.6 1.6 %collective-permute-start.3 = (f32[8,16,128]{2,1,0:T(8,128)S(1)}, f32[8,16,128]{2,1,0:T(8,128)S(1)}, u32[]{:S(2)}, u32[]{:S(2)}) collective-permute-start(f32[8,16,128]{2,1,0:T(8,128)S(1)} %get-tuple-element.31.total_ref), channel_id=1, source_target_pairs={{0,8},{2,10},{4,12},{6,14},{8,0},{10,2},{12,4},{14,6},{16,24},{18,... | collective-permute-start | bytes 196616 | tf_op jit(solution)/shard_map/ppermute | solution.py:343
  26.2 2.7 %collective-permute-done.3.other_ref = f32[8,16,128]{2,1,0:T(8,128)S(1)} collective-permute-done((f32[8,16,128]{2,1,0:T(8,128)S(1)}, f32[8,16,128]{2,1,0:T(8,128)S(1)}, u32[]{:S(2)}, u32[]{:S(2)}) %collective-permute-start.3) | collective-permute-done | bytes 65568 | tf_op jit(solution)/shard_map/ppermute | solution.py:343
  29.0 2.7 %collective-permute-start.4 = (f32[8,16,128]{2,1,0:T(8,128)S(1)}, f32[8,16,128]{2,1,0:T(8,128)S(1)}, u32[]{:S(2)}, u32[]{:S(2)}) collective-permute-start(f32[8,16,128]{2,1,0:T(8,128)S(1)} %get-tuple-element.33), channel_id=1, source_target_pairs={{0,16},{2,18},{4,20},{6,22},{8,24},{10,26},{12,28},{14,30},{16,0},... | collective-permute-start | bytes 196616 | tf_op jit(solution)/shard_map/ppermute | solution.py:343
  31.6 2.6 %collective-permute-done.4.other_ref = f32[8,16,128]{2,1,0:T(8,128)S(1)} collective-permute-done((f32[8,16,128]{2,1,0:T(8,128)S(1)}, f32[8,16,128]{2,1,0:T(8,128)S(1)}, u32[]{:S(2)}, u32[]{:S(2)}) %collective-permute-start.4) | collective-permute-done | bytes 65568 | tf_op jit(solution)/shard_map/ppermute | solution.py:343
  34.2 0.1 collective-permute-start.5
  34.3 1.2 %collective-permute-done.5.rest_1_ = f32[8,16,128]{2,1,0:T(8,128)S(1)} collective-permute-done((f32[8,16,128]{2,1,0:T(8,128)S(1)}, f32[8,16,128]{2,1,0:T(8,128)S(1)}, u32[]{:S(2)}, u32[]{:S(2)}) %collective-permute-start.5) | collective-permute-done | bytes 65568 | tf_op jit(solution)/shard_map/ppermute | solution.py:343
  35.5 0.0 copy-done
  35.6 0.0 copy-done.1
  35.6 0.0 copy-done.2
  35.6 12.1 %shard_map.88 = bf16[2048,512]{1,0:T(8,128)(2,1)} custom-call(s32[1]{0:T(128)} %bitcast.place_ref, bf16[2,1024,128]{2,1,0:T(8,128)(2,1)S(1)} %get-tuple-element.27.rim_ref, bf16[2,3072,128]{2,1,0:T(8,128)(2,1)S(1)} %get-tuple-element.28.inner_ref, bf16[2048,512]{1,0:T(8,128)(2,1)S(1)} %copy-done, f32[16,16,128]{2,1,0:T(8,128)S(1)} %get-tuple-element.24.rates_ref, ...), custom_call_target="tpu_custom_call" | custom-call | flops 73400320 | bytes 6291456 | tf_op jit(solution)/shard_map/pallas_call | solution.py:366
  (5 shorter events, 0.2 us)
Async XLA Ops:
  1.1 12.5 %collective-permute-start = (bf16[2048,128]{1,0:T(8,128)(2,1)S(1)}, bf16[2048,128]{1,0:T(8,128)(2,1)S(1)}, u32[]{:S(2)}, u32[]{:S(2)}) collective-permute-start(bf16[2048,128]{1,0:T(8,128)(2,1)S(1)} %slice.3), channel_id=1, source_target_pairs={{0,2},{2,4},{4,6},{6,8},{8,10},{10,12},{12,14},{14,16},{16,18},{18... | collective-permute-start | bytes 1572872 | tf_op jit(solution)/shard_map/ppermute | solution.py:287
  13.6 21.9 %copy-start = (bf16[2048,512]{1,0:T(8,128)(2,1)S(1)}, bf16[2048,512]{1,0:T(8,128)(2,1)}, u32[]{:S(2)}) copy-start(bf16[2048,512]{1,0:T(8,128)(2,1)} %gate_ref.1) | copy-start | bytes 6291460
  13.6 21.9 %copy-start.1 = (f32[2048,16]{0,1:T(8,128)S(1)}, f32[2048,16]{0,1:T(8,128)}, u32[]{:S(2)}) copy-start(f32[2048,16]{0,1:T(8,128)} %param.13) | copy-start | bytes 393220
  13.6 21.9 %copy-start.2 = (f32[2048]{0:T(1024)S(1)}, f32[2048]{0:T(1024)}, u32[]{:S(2)}) copy-start(f32[2048]{0:T(1024)} %param.14) | copy-start | bytes 24580
  16.5 3.6 %collective-permute-start.1 = (f32[8,16,128]{2,1,0:T(8,128)S(1)}, f32[8,16,128]{2,1,0:T(8,128)S(1)}, u32[]{:S(2)}, u32[]{:S(2)}) collective-permute-start(f32[8,16,128]{2,1,0:T(8,128)S(1)} %get-tuple-element.30), channel_id=1, source_target_pairs={{0,2},{2,0},{4,6},{6,4},{8,10},{10,8},{12,14},{14,12},{16,18},{18,... | collective-permute-start | bytes 196616 | tf_op jit(solution)/shard_map/ppermute | solution.py:343
  20.1 4.4 %collective-permute-start.2 = (f32[8,16,128]{2,1,0:T(8,128)S(1)}, f32[8,16,128]{2,1,0:T(8,128)S(1)}, u32[]{:S(2)}, u32[]{:S(2)}) collective-permute-start(f32[8,16,128]{2,1,0:T(8,128)S(1)} %shard_map.84.total_ref), channel_id=1, source_target_pairs={{0,4},{2,6},{4,0},{6,2},{8,12},{10,14},{12,8},{14,10},{16,20},{18,... | collective-permute-start | bytes 196616 | tf_op jit(solution)/shard_map/ppermute | solution.py:343
  24.6 4.3 %collective-permute-start.3 = (f32[8,16,128]{2,1,0:T(8,128)S(1)}, f32[8,16,128]{2,1,0:T(8,128)S(1)}, u32[]{:S(2)}, u32[]{:S(2)}) collective-permute-start(f32[8,16,128]{2,1,0:T(8,128)S(1)} %get-tuple-element.31.total_ref), channel_id=1, source_target_pairs={{0,8},{2,10},{4,12},{6,14},{8,0},{10,2},{12,4},{14,6},{16,24},{18,... | collective-permute-start | bytes 196616 | tf_op jit(solution)/shard_map/ppermute | solution.py:343
  29.0 5.2 %collective-permute-start.4 = (f32[8,16,128]{2,1,0:T(8,128)S(1)}, f32[8,16,128]{2,1,0:T(8,128)S(1)}, u32[]{:S(2)}, u32[]{:S(2)}) collective-permute-start(f32[8,16,128]{2,1,0:T(8,128)S(1)} %get-tuple-element.33), channel_id=1, source_target_pairs={{0,16},{2,18},{4,20},{6,22},{8,24},{10,26},{12,28},{14,30},{16,0},... | collective-permute-start | bytes 196616 | tf_op jit(solution)/shard_map/ppermute | solution.py:343
  34.2 1.3 %collective-permute-start.5 = (f32[8,16,128]{2,1,0:T(8,128)S(1)}, f32[8,16,128]{2,1,0:T(8,128)S(1)}, u32[]{:S(2)}, u32[]{:S(2)}) collective-permute-start(f32[8,16,128]{2,1,0:T(8,128)S(1)} %get-tuple-element.36), channel_id=1, source_target_pairs={{0,2},{2,0},{4,6},{6,4},{8,10},{10,8},{12,14},{14,12},{16,18},{18,... | collective-permute-start | bytes 196616 | tf_op jit(solution)/shard_map/ppermute | solution.py:343

commit v6 on v5

--- a/solution.py
+++ b/solution.py
@@ -97,9 +97,10 @@
 
 
 def inner_kernel(
-    v_hbm, gate_hbm, taps_hbm, raw_hbm, tables_hbm,
-    spec_ref, mixed_ref, state_ref, rates_ref, v_first, gate_first, tables,
-    v_rest, gate_rest, taps, raw, store, laid, sems,
+    seq_total,
+    v_hbm, gate_hbm, taps_hbm, raw_hbm, raw_weights_hbm, tables_hbm,
+    spec_ref, mixed_ref, state_ref, rates_ref, scaled_ref, v_first, gate_first, tables,
+    v_rest, gate_rest, taps, raw, raw_weights, store, laid, sems,
 ):
     tiles, inner = mixed_ref.shape[0], v_rest.shape[1]
 
@@ -114,6 +115,7 @@
     small = [
         pltpu.make_async_copy(tables_hbm, tables, sems.at[tiles * 5]),
         pltpu.make_async_copy(raw_hbm, raw, sems.at[tiles * 5 + 1]),
+        pltpu.make_async_copy(raw_weights_hbm, raw_weights, sems.at[tiles * 5 + 2]),
     ]
     large = [copies(tile) for tile in range(tiles)]
     for copy in small + sum(large, []):
@@ -139,9 +141,13 @@
             earlier = later
         if tile == 0:
             small[1].wait()
+            small[2].wait()
         lay_out(raw.at[:, pl.ds(tile * TILE, TILE)], laid)
         modes = raw.shape[0]
-        rates_ref[:, groups] = laid[...].reshape(modes, SUBS, LANES)
+        rates = laid[...].reshape(modes, SUBS, LANES)
+        rates_ref[:, groups] = rates
+        lay_out(raw_weights.at[:, pl.ds(tile * TILE, TILE)], laid)
+        scaled_ref[:, groups] = laid[...].reshape(modes, SUBS, LANES) * jnp.sqrt(2.0 * rates + 2.0 / seq_total)
         for mode, state in enumerate(end_states(store, mixed_ref.at[tile], rates_ref.at[:, groups])):
             state_ref[mode, groups] = state
 
@@ -201,75 +207,92 @@
     twins_ref[...] = jnp.where(core == 0, second, first)
 
 
-def outer_kernel(seq_total, place_ref, rim_ref, inner_ref, gate_ref, rates_ref, raw_ref, bias_ref, *rest):
-    *start_refs, out_ref, store, begin, laid = rest
-    lay_out(raw_ref, laid)
-    modes, plane = rates_ref.shape[0], len(start_refs)
-    share = modes // plane
-    for behind, ref in enumerate(start_refs):
-        begin[pl.ds((place_ref[0] + behind) % plane * share, share)] = ref[...]
-    decay = [jnp.exp(-rates_ref[mode]) for mode in range(modes)]
-    weights = [laid[mode * SUBS : (mode + 1) * SUBS] for mode in range(modes)]
-    scaled = [weights[mode] * jnp.sqrt(2.0 * rates_ref[mode] + 2.0 / seq_total) for mode in range(modes)]
-    bias = bias_ref[...]
-    states = tuple(begin[mode] for mode in range(modes))
-    first = 0
-    for source in (rim_ref, inner_ref):
-
-        def turn(index, states, source=source, first=first):
-            at = pl.multiple_of(index * STEPS * SUBS, STEPS * SUBS)
-            values = source[pl.ds(at, STEPS * SUBS), :].astype(F32)
-            sums = []
-            for step in range(STEPS):
-                value = values[step * SUBS : (step + 1) * SUBS]
-                states = tuple(d * s + value for d, s in zip(decay, states))
-                terms = [c * s for c, s in zip(scaled, states)] + [bias * value]
-                while len(terms) > 1:
-                    terms = [sum(terms[i : i + 2][1:], terms[i]) for i in range(0, len(terms), 2)]
-                sums.append(terms[0])
-            store[pl.ds(first * SUBS + at, STEPS * SUBS), :] = jnp.concatenate(sums, axis=0)
-            return states
-
-        count = source.shape[0] // SUBS
-        states = lax.fori_loop(0, count // STEPS, turn, states)
-        first += count
-    for group in range(SUBS):
-        rows = slice(group * LANES, (group + 1) * LANES)
-        for block in range(first // BLOCK):
-            cols = slice(block * BLOCK, (block + 1) * BLOCK)
-            turned = store[pl.ds(block * BLOCK * SUBS + group, BLOCK, stride=SUBS), :].T
-            out_ref[rows, cols] = (gate_ref[rows, cols].astype(F32) * turned).astype(BF16)
+def added(terms):
+    while len(terms) > 1:
+        terms = [sum(terms[i : i + 2][1:], terms[i]) for i in range(0, len(terms), 2)]
+    return terms[0]
+
+
+def filtered(source, start, store, decay, scaled, bias, states):
+    def turn(index, states):
+        at = pl.multiple_of(index * STEPS * SUBS, STEPS * SUBS)
+        values = source[pl.ds(start * SUBS + at, STEPS * SUBS), :].astype(F32)
+        sums = []
+        for step in range(STEPS):
+            value = values[step * SUBS : (step + 1) * SUBS]
+            states = tuple(d * s + value for d, s in zip(decay, states))
+            sums.append(added([c * s for c, s in zip(scaled, states)] + [bias * value]))
+        store[pl.ds(at, STEPS * SUBS), :] = jnp.concatenate(sums, axis=0)
+        return states
+
+    return lax.fori_loop(0, BLOCK // STEPS, turn, states)
+
+
+def local_kernel(start, mixed_ref, rates_ref, scaled_ref, bias_ref, *rest):
+    *earlier, sums_ref, states_ref = rest
+    modes = rates_ref.shape[0]
+    for tile in range(sums_ref.shape[0]):
+        groups = slice(tile * SUBS, (tile + 1) * SUBS)
+        decay = [jnp.exp(-rates_ref[mode, groups]) for mode in range(modes)]
+        scaled = [scaled_ref[mode, groups] for mode in range(modes)]
+        states = tuple(earlier[0][m, groups] if earlier else jnp.zeros((SUBS, LANES), F32) for m in range(modes))
+        states = filtered(
+            mixed_ref.at[tile], start, sums_ref.at[tile], decay, scaled, bias_ref[groups], states
+        )
+        for mode in range(modes):
+            states_ref[mode, groups] = states[mode]
+
+
+def outer_kernel(place_ref, mixed_ref, gate_ref, rates_ref, scaled_ref, bias_ref, mine_ref, twins_ref, local_ref, *rest):
+    *sums_refs, out_hbm, store, begin, out, sems = rest
+    modes, half = rates_ref.shape[0], mine_ref.shape[0]
+    core = place_ref[0] % 2
+    begin[pl.ds(core * half, half)] = mine_ref[...]
+    begin[pl.ds((1 - core) * half, half)] = twins_ref[...]
+    blocks = len(sums_refs) + 1
+    copies = []
+    for tile in range(mixed_ref.shape[0]):
+        groups = slice(tile * SUBS, (tile + 1) * SUBS)
+        decay = [jnp.exp(-rates_ref[mode, groups]) for mode in range(modes)]
+        scaled = [scaled_ref[mode, groups] for mode in range(modes)]
+        states = tuple(c * begin[mode, groups] for mode, c in enumerate(scaled))
+        for block, sums_ref in enumerate(sums_refs):
+
+            def carry(index, states, sums_ref=sums_ref, block=block):
+                at = pl.multiple_of(index * STEPS * SUBS, STEPS * SUBS)
+                for step in range(STEPS):
+                    states = tuple(d * s for d, s in zip(decay, states))
+                    total = sums_ref[tile, pl.ds(at + step * SUBS, SUBS), :] + added(list(states))
+                    store[pl.ds(block * BLOCK * SUBS + at + step * SUBS, SUBS), :] = total
+                return states
+
+            states = lax.fori_loop(0, BLOCK // STEPS, carry, states)
+        past = float((blocks - 1) * BLOCK)
+        full = tuple(
+            local_ref[mode, groups] + jnp.exp(-past * rates_ref[mode, groups]) * begin[mode, groups]
+            for mode in range(modes)
+        )
+        last = (blocks - 1) * BLOCK
+        filtered(
+            mixed_ref.at[tile], last - BLOCK, store.at[pl.ds(last * SUBS, BLOCK * SUBS)], decay, scaled, bias_ref[groups], full
+        )
+        for group in range(SUBS):
+            rows = slice(tile * TILE + group * LANES, tile * TILE + (group + 1) * LANES)
+            for block in range(blocks):
+                cols = slice(block * BLOCK, (block + 1) * BLOCK)
+                turned = store[pl.ds(block * BLOCK * SUBS + group, BLOCK, stride=SUBS), :].T
+                out[rows, cols] = (gate_ref[rows, cols].astype(F32) * turned).astype(BF16)
+            copy = pltpu.make_async_copy(out.at[rows], out_hbm.at[rows], sems.at[tile * SUBS + group])
+            copy.start()
+            copies.append(copy)
+    for copy in copies:
+        copy.wait()
 
 
 SCALAR = pl.BlockSpec(memory_space=pltpu.SMEM)
 WHOLE = pl.BlockSpec(memory_space=pltpu.VMEM)
 FAR = pl.BlockSpec(memory_space=pltpu.HBM)
 INNER_ROOM, RIM_ROOM = 32, 24
-
-
-def call(kernel, tiles, in_specs, out_specs, out_shape, scratch, flops, moved, room):
-    return pl.pallas_call(
-        kernel,
-        grid=(tiles,),
-        in_specs=in_specs,
-        out_specs=out_specs,
-        out_shape=out_shape,
-        scratch_shapes=scratch,
-        compiler_params=pltpu.CompilerParams(vmem_limit_bytes=room << 20),
-        cost_estimate=pl.CostEstimate(flops=flops, bytes_accessed=moved, transcendentals=0),
-    )
-
-
-def rows_spec(width, column=0):
-    return pl.BlockSpec((TILE, width), lambda i: (i, column))
-
-
-def modes_spec(modes):
-    return pl.BlockSpec((modes, SUBS, LANES), lambda i: (0, i, 0))
-
-
-def steps_spec(steps):
-    return pl.BlockSpec((None, steps * SUBS, LANES), lambda i: (i, 0, 0))
 
 
 def steps_scratch(steps):
@@ -302,31 +325,30 @@
     shape = jax.ShapeDtypeStruct
     per_mode = shape((modes, groups, LANES), F32)
     half = shape((modes // 2, groups, LANES), F32)
-    raw_spec = pl.BlockSpec((modes, TILE), lambda i: (0, i))
-    rates_spec, half_spec = modes_spec(modes), modes_spec(modes // 2)
     laid = pltpu.VMEM((modes * SUBS, LANES), F32)
     tap_spectra = shape((channels, 2 * BLOCK), F32)
     head = shape((channels, BLOCK), BF16)
-    spectrum, inner_mixed, inner_state, rates, v_first, gate_first, tables = pl.pallas_call(
-        inner_kernel,
-        in_specs=[FAR] * 5,
-        out_specs=[WHOLE] * 7,
-        out_shape=[tap_spectra, shape((tiles, inner * SUBS, LANES), BF16), per_mode, per_mode, head, head]
+    spectrum, inner_mixed, inner_state, rates, scaled, v_first, gate_first, tables = pl.pallas_call(
+        functools.partial(inner_kernel, tokens * shards),
+        in_specs=[FAR] * 6,
+        out_specs=[WHOLE] * 8,
+        out_shape=[tap_spectra, shape((tiles, inner * SUBS, LANES), BF16)] + [per_mode] * 3 + [head, head]
         + [shape(tables.shape, BF16)],
         scratch_shapes=[
             pltpu.VMEM((channels, inner), BF16),
             pltpu.VMEM((channels, inner), BF16),
             pltpu.VMEM((channels, BLOCK), F32),
             pltpu.VMEM((modes, channels), F32),
+            pltpu.VMEM((modes, channels), F32),
             steps_scratch(inner),
             laid,
-            pltpu.SemaphoreType.DMA((tiles * 5 + 2,)),
+            pltpu.SemaphoreType.DMA((tiles * 5 + 3,)),
         ],
         compiler_params=pltpu.CompilerParams(vmem_limit_bytes=INNER_ROOM << 20),
         cost_estimate=pl.CostEstimate(
             flops=channels * inner * 2600, bytes_accessed=channels * tokens * 8, transcendentals=0
         ),
-    )(*map(kept_far, (v_stream, gate_one, short_filter, raw_rates, tables)))
+    )(*map(kept_far, (v_stream, gate_one, short_filter, raw_rates, raw_weights, tables)))
     rim_mixed, own_end, twin_half = pl.pallas_call(
         functools.partial(rim_kernel, inner),
         in_specs=[SCALAR] + [WHOLE] * 7,
@@ -351,31 +373,59 @@
             compiler_params=pltpu.CompilerParams(vmem_limit_bytes=8 << 20),
         )(place, rates, *arrays)
 
+    sums, states = [], []
+
+    def beside(arriving, sent):
+        block = len(sums)
+        if block >= tokens // BLOCK - 1:
+            return arriving
+        source, start = (inner_mixed, (block - 1) * BLOCK) if block else (rim_mixed, 0)
+        source, *earlier, _ = lax.optimization_barrier((source, *states[-1:], sent))
+        done = pl.pallas_call(
+            functools.partial(local_kernel, start),
+            in_specs=[WHOLE] * (4 + len(earlier)),
+            out_specs=[WHOLE] * 2,
+            out_shape=[shape((tiles, BLOCK * SUBS, LANES), F32), per_mode],
+            compiler_params=pltpu.CompilerParams(vmem_limit_bytes=8 << 20),
+            cost_estimate=pl.CostEstimate(
+                flops=channels * BLOCK * 2600, bytes_accessed=channels * BLOCK * 16, transcendentals=0
+            ),
+        )(source, rates, scaled, bias, *earlier)
+        arriving, total, state = lax.optimization_barrier((arriving, *done))
+        sums.append(total)
+        states.append(state)
+        return arriving
+
     twin_end = swap(twin_half, 1)
     (total,) = small(functools.partial(chip_kernel, tokens), 1, own_end, twin_end)
     ahead = jnp.zeros(half.shape, F32)
     size = 2
     while 2 * size < shards:
-        total, ahead = small(functools.partial(level_kernel, tokens, size), 2, total, swap(total, size), ahead)
+        other = beside(swap(total, size), total)
+        total, ahead = small(functools.partial(level_kernel, tokens, size), 2, total, other, ahead)
         size *= 2
-    mine, twins = small(
-        functools.partial(start_kernel, tokens, size), 2, swap(total, size), ahead, own_end, twin_end
-    )
-    starts = [mine, swap(twins, 1)]
-
-    hyena_out = call(
-        functools.partial(outer_kernel, tokens * shards),
-        tiles,
-        [SCALAR, steps_spec(BLOCK), steps_spec(inner), rows_spec(tokens), rates_spec, raw_spec]
-        + [pl.BlockSpec((SUBS, LANES), lambda i: (i, 0))]
-        + [half_spec] * 2,
-        rows_spec(tokens),
-        shape((channels, tokens), BF16),
-        [steps_scratch(tokens), pltpu.VMEM((modes, SUBS, LANES), F32), laid],
-        channels * tokens * 70,
-        channels * tokens * 6,
-        32,
-    )(place, rim_mixed, inner_mixed, gate_two, rates, raw_weights, bias, *starts)
+    other = beside(swap(total, size), total)
+    mine, twins = small(functools.partial(start_kernel, tokens, size), 2, other, ahead, own_end, twin_end)
+    twins = swap(twins, 1)
+    while len(sums) < tokens // BLOCK - 1:
+        beside(total, total)
+
+    hyena_out = pl.pallas_call(
+        outer_kernel,
+        in_specs=[SCALAR] + [WHOLE] * (8 + len(sums)),
+        out_specs=FAR,
+        out_shape=shape((channels, tokens), BF16),
+        scratch_shapes=[
+            steps_scratch(tokens),
+            pltpu.VMEM((modes, groups, LANES), F32),
+            pltpu.VMEM((channels, tokens), BF16),
+            pltpu.SemaphoreType.DMA((groups,)),
+        ],
+        compiler_params=pltpu.CompilerParams(vmem_limit_bytes=24 << 20),
+        cost_estimate=pl.CostEstimate(
+            flops=channels * tokens * 50, bytes_accessed=channels * tokens * 6, transcendentals=0
+        ),
+    )(place, inner_mixed, gate_two, rates, scaled, bias, mine, twins, states[-1], *sums)
     return hyena_out[:real_channels]
 
 

time: 47.9 us -> 44.1 us (0.921)
  waiting for transfers between devices: 10.2 us -> 2.6 us
  Pallas kernels: 25.3 us -> 29.1 us
    ppermute x5, waiting for transfers between devices: 10.2 us -> 2.6 us  [swap(): lax.ppermute(array, 'seq', [(i, i ^ distance) for i in range(shards)])]
    pallas_call x2 -> x5, Pallas kernels: 22.3 us -> 26.1 us  [the longest x1 10.2 us: on_device(): pl.pallas_call(functools.partial(inner_kernel, tokens * shards), in_specs...]
  transfers between devices with their start and end apart: 6 -> 6, of which waited for: 5 -> 4; matrix products, arithmetic and copies ran while one was open for 0% -> 0% of each run, Pallas kernels for 21% -> 41%
where the time goes in v6:
time: 44.1 us; the launch traced here: 43.9 us
  Pallas kernels  29.1 us (66%)
  starting transfers between devices  11 us (25%)
  waiting for transfers between devices  2.6 us (6%)
  local copies, waits for them, and re-layouts  1.09 us (2%)
    pallas_call x1, Pallas kernels, on_device(): pl.pallas_call(functools.partial(inner_kernel, tokens * shards), in_specs...  10.2 us
    ppermute x5, starting transfers between devices, swap(): lax.ppermute(array, 'seq', [(i, i ^ distance) for i in range(shards)])  8.62 us
    pallas_call x1, Pallas kernels, on_device(): pl.pallas_call(outer_kernel, in_specs=[SCALAR] + [WHOLE] * (8 + len(sums)...  8.31 us
    pallas_call x3, Pallas kernels, beside(): pl.pallas_call(functools.partial(local_kernel, start), in_specs=[WHOLE] *...  7.61 us
    pallas_call x1, Pallas kernels, on_device(): pl.pallas_call(functools.partial(rim_kernel, inner), in_specs=[SCALAR] +...  2.83 us
    ppermute x5, waiting for transfers between devices, swap(): lax.ppermute(array, 'seq', [(i, i ^ distance) for i in range(shards)])  2.6 us
    ppermute x1, starting transfers between devices, on_device(): lax.ppermute(v_stream[:, tokens - BLOCK:], 'seq', [(i, i + 1) for i in ra...  2.39 us
    slice x1, local copies, waits for them, and re-layouts, on_device(): v_stream[:, tokens - BLOCK:]  1.08 us
  transfers between devices with their start and end apart: 6, of which 4 were waited for; matrix products, arithmetic and copies ran while one was open for 0% of the time, Pallas kernels for 41%

profile of v6, /device:TPU:0, one launch (start us, length us, event | category | flops | bytes accessed | tf_op | source)
XLA Modules:
  0.0 43.9 jit_solution(13592157209192182876)
XLA Ops:
  0.0 1.1 %slice.3 = bf16[2048,128]{1,0:T(8,128)(2,1)S(1)} slice(bf16[2048,512]{1,0:T(8,128)(2,1)} %v_hbm.1), slice={[0:2048], [384:512]} | slice | bytes 1048576 | tf_op jit(solution)/shard_map/slice | solution.py:310
  1.1 2.4 %collective-permute-start = (bf16[2048,128]{1,0:T(8,128)(2,1)S(1)}, bf16[2048,128]{1,0:T(8,128)(2,1)S(1)}, u32[]{:S(2)}, u32[]{:S(2)}) collective-permute-start(bf16[2048,128]{1,0:T(8,128)(2,1)S(1)} %slice.3), channel_id=1, source_target_pairs={{0,2},{2,4},{4,6},{6,8},{8,10},{10,12},{12,14},{14,16},{16,18},{18... | collective-permute-start | bytes 1572872 | tf_op jit(solution)/shard_map/ppermute | solution.py:310
  3.5 10.2 %shard_map.82 = (f32[2048,256]{1,0:T(8,128)S(1)}, bf16[2,3072,128]{2,1,0:T(8,128)(2,1)S(1)}, f32[16,16,128]{2,1,0:T(8,128)S(1)}, f32[16,16,128]{2,1,0:T(8,128)S(...) custom-call(bf16[2048,512]{1,0:T(8,128)(2,1)} %v_hbm.1, ...), custom_call_target="tpu_custom_call" | custom-call | flops 2044723200 | bytes 8388608 | tf_op jit(solution)/shard_map/pallas_call | solution.py:331
  13.7 0.0 collective-permute-done.before_ref
  13.7 0.0 copy-start.1
  13.7 2.8 %shard_map.83 = (bf16[2,1024,128]{2,1,0:T(8,128)(2,1)S(1)}, f32[8,16,128]{2,1,0:T(8,128)S(1)}, f32[8,16,128]{2,1,0:T(8,128)S(1)}) custom-call(s32[1]{0:T(128)} %bitcast.place_ref, bf16[2048,128]{1,0:T(8,128)(2,1)S(1)} %collective-permute-done.before_ref, bf16[2048,128]{1,0:T(8,128)(2,1)S(1)} %get-tuple-element.45.v_ref, ...), custom_call_target="tpu_custom_call" | custom-call | flops 681574400 | bytes 4194304 | tf_op jit(solution)/shard_map/pallas_call | solution.py:352
  16.5 2.7 %collective-permute-start.1 = (f32[8,16,128]{2,1,0:T(8,128)S(1)}, f32[8,16,128]{2,1,0:T(8,128)S(1)}, u32[]{:S(2)}, u32[]{:S(2)}) collective-permute-start(f32[8,16,128]{2,1,0:T(8,128)S(1)} %get-tuple-element.51), channel_id=1, source_target_pairs={{0,2},{2,0},{4,6},{6,4},{8,10},{10,8},{12,14},{14,12},{16,18},{18,... | collective-permute-start | bytes 196616 | tf_op jit(solution)/shard_map/ppermute | solution.py:365
  19.2 0.9 %collective-permute-done.1.other_ref.twin_ref = f32[8,16,128]{2,1,0:T(8,128)S(1)} collective-permute-done((f32[8,16,128]{2,1,0:T(8,128)S(1)}, f32[8,16,128]{2,1,0:T(8,128)S(1)}, u32[]{:S(2)}, u32[]{:S(2)}) %collective-permute-start.1) | collective-permute-done | bytes 65568 | tf_op jit(solution)/shard_map/ppermute | solution.py:365
  20.1 1.6 %collective-permute-start.2 = (f32[8,16,128]{2,1,0:T(8,128)S(1)}, f32[8,16,128]{2,1,0:T(8,128)S(1)}, u32[]{:S(2)}, u32[]{:S(2)}) collective-permute-start(f32[8,16,128]{2,1,0:T(8,128)S(1)} %shard_map.84.total_ref), channel_id=1, source_target_pairs={{0,4},{2,6},{4,0},{6,2},{8,12},{10,14},{12,8},{14,10},{16,20},{18,... | collective-permute-start | bytes 196616 | tf_op jit(solution)/shard_map/ppermute | solution.py:365
  21.7 0.0 copy-done.1
  21.7 2.5 %shard_map.85 = (f32[2,1024,128]{2,1,0:T(8,128)S(1)}, f32[16,16,128]{2,1,0:T(8,128)S(1)}) custom-call(bf16[2,1024,128]{2,1,0:T(8,128)(2,1)S(1)} %get-tuple-element.53.mixed_ref, f32[16,16,128]{2,1,0:T(8,128)S(1)} %get-tuple-element.43.rates_ref, f32[16,16,128]{2,1,0:T(8,128)S(1)} %get-tuple-element.44.scaled_ref, f32[16,128]{1,0:T(8,128)S(1)} %bitcast.4), custom_call_target="tpu_custom_call" | custom-call | flops 681574400 | bytes 4194304 | tf_op jit(solution)/shard_map/pallas_call | solution.py:384
  24.3 0.3 collective-permute-done.2.other_ref
  24.6 1.6 %collective-permute-start.3 = (f32[8,16,128]{2,1,0:T(8,128)S(1)}, f32[8,16,128]{2,1,0:T(8,128)S(1)}, u32[]{:S(2)}, u32[]{:S(2)}) collective-permute-start(f32[8,16,128]{2,1,0:T(8,128)S(1)} %get-tuple-element.57.total_ref), channel_id=1, source_target_pairs={{0,8},{2,10},{4,12},{6,14},{8,0},{10,2},{12,4},{14,6},{16,24},{18,... | collective-permute-start | bytes 196616 | tf_op jit(solution)/shard_map/ppermute | solution.py:365
  26.3 2.5 %shard_map.87 = (f32[2,1024,128]{2,1,0:T(8,128)S(1)}, f32[16,16,128]{2,1,0:T(8,128)S(1)}) custom-call(bf16[2,3072,128]{2,1,0:T(8,128)(2,1)S(1)} %get-tuple-element.67.mixed_ref, f32[16,16,128]{2,1,0:T(8,128)S(1)} %get-tuple-element.43.rates_ref, f32[16,16,128]{2,1,0:T(8,128)S(1)} %get-tuple-element.44.scaled_ref, f32[16,128]{1,0:T(8,128)S(1)} %bitcast.5, ...), custom_call_target="tpu_custom_call" | custom-call | flops 681574400 | bytes 4194304 | tf_op jit(solution)/shard_map/pallas_call | solution.py:384
  28.8 0.0 copy-start
  28.8 0.1 collective-permute-done.3.other_ref
  29.0 2.7 %collective-permute-start.4 = (f32[8,16,128]{2,1,0:T(8,128)S(1)}, f32[8,16,128]{2,1,0:T(8,128)S(1)}, u32[]{:S(2)}, u32[]{:S(2)}) collective-permute-start(f32[8,16,128]{2,1,0:T(8,128)S(1)} %get-tuple-element.65), channel_id=1, source_target_pairs={{0,16},{2,18},{4,20},{6,22},{8,24},{10,26},{12,28},{14,30},{16,0},... | collective-permute-start | bytes 196616 | tf_op jit(solution)/shard_map/ppermute | solution.py:365
  31.6 2.5 %shard_map.89 = (f32[2,1024,128]{2,1,0:T(8,128)S(1)}, f32[16,16,128]{2,1,0:T(8,128)S(1)}) custom-call(bf16[2,3072,128]{2,1,0:T(8,128)(2,1)S(1)} %get-tuple-element.67.mixed_ref, f32[16,16,128]{2,1,0:T(8,128)S(1)} %get-tuple-element.43.rates_ref, f32[16,16,128]{2,1,0:T(8,128)S(1)} %get-tuple-element.44.scaled_ref, f32[16,128]{1,0:T(8,128)S(1)} %bitcast.6, ...), custom_call_target="tpu_custom_call" | custom-call | flops 681574400 | bytes 4194304 | tf_op jit(solution)/shard_map/pallas_call | solution.py:384
  34.2 0.0 collective-permute-done.4.other_ref
  34.3 0.1 collective-permute-start.5
  34.3 1.2 %collective-permute-done.5.twins_ref = f32[8,16,128]{2,1,0:T(8,128)S(1)} collective-permute-done((f32[8,16,128]{2,1,0:T(8,128)S(1)}, f32[8,16,128]{2,1,0:T(8,128)S(1)}, u32[]{:S(2)}, u32[]{:S(2)}) %collective-permute-start.5) | collective-permute-done | bytes 65568 | tf_op jit(solution)/shard_map/ppermute | solution.py:365
  35.6 0.0 copy-done
  35.6 8.3 %shard_map.91 = bf16[2048,512]{1,0:T(8,128)(2,1)} custom-call(s32[1]{0:T(128)} %bitcast.place_ref, bf16[2,3072,128]{2,1,0:T(8,128)(2,1)S(1)} %get-tuple-element.67.mixed_ref, bf16[2048,512]{1,0:T(8,128)(2,1)S(1)} %copy-done, f32[16,16,128]{2,1,0:T(8,128)S(1)} %get-tuple-element.43.rates_ref, f32[16,16,128]{2,1,0:T(8,128)S(1)} %get-tuple-element.44.scaled_ref, ...), custom_call_target="tpu_custom_call" | custom-call | flops 52428800 | bytes 6291456 | tf_op jit(solution)/shard_map/pallas_call | solution.py:413
  (5 shorter events, 0.2 us)
Async XLA Ops:
  1.1 12.6 %collective-permute-start = (bf16[2048,128]{1,0:T(8,128)(2,1)S(1)}, bf16[2048,128]{1,0:T(8,128)(2,1)S(1)}, u32[]{:S(2)}, u32[]{:S(2)}) collective-permute-start(bf16[2048,128]{1,0:T(8,128)(2,1)S(1)} %slice.3), channel_id=1, source_target_pairs={{0,2},{2,4},{4,6},{6,8},{8,10},{10,12},{12,14},{14,16},{16,18},{18... | collective-permute-start | bytes 1572872 | tf_op jit(solution)/shard_map/ppermute | solution.py:310
  13.7 8.0 %copy-start.1 = (f32[2048]{0:T(1024)S(1)}, f32[2048]{0:T(1024)}, u32[]{:S(2)}) copy-start(f32[2048]{0:T(1024)} %param.14) | copy-start | bytes 24580
  16.5 3.6 %collective-permute-start.1 = (f32[8,16,128]{2,1,0:T(8,128)S(1)}, f32[8,16,128]{2,1,0:T(8,128)S(1)}, u32[]{:S(2)}, u32[]{:S(2)}) collective-permute-start(f32[8,16,128]{2,1,0:T(8,128)S(1)} %get-tuple-element.51), channel_id=1, source_target_pairs={{0,2},{2,0},{4,6},{6,4},{8,10},{10,8},{12,14},{14,12},{16,18},{18,... | collective-permute-start | bytes 196616 | tf_op jit(solution)/shard_map/ppermute | solution.py:365
  20.1 4.4 %collective-permute-start.2 = (f32[8,16,128]{2,1,0:T(8,128)S(1)}, f32[8,16,128]{2,1,0:T(8,128)S(1)}, u32[]{:S(2)}, u32[]{:S(2)}) collective-permute-start(f32[8,16,128]{2,1,0:T(8,128)S(1)} %shard_map.84.total_ref), channel_id=1, source_target_pairs={{0,4},{2,6},{4,0},{6,2},{8,12},{10,14},{12,8},{14,10},{16,20},{18,... | collective-permute-start | bytes 196616 | tf_op jit(solution)/shard_map/ppermute | solution.py:365
  24.6 4.3 %collective-permute-start.3 = (f32[8,16,128]{2,1,0:T(8,128)S(1)}, f32[8,16,128]{2,1,0:T(8,128)S(1)}, u32[]{:S(2)}, u32[]{:S(2)}) collective-permute-start(f32[8,16,128]{2,1,0:T(8,128)S(1)} %get-tuple-element.57.total_ref), channel_id=1, source_target_pairs={{0,8},{2,10},{4,12},{6,14},{8,0},{10,2},{12,4},{14,6},{16,24},{18,... | collective-permute-start | bytes 196616 | tf_op jit(solution)/shard_map/ppermute | solution.py:365
  28.8 6.8 %copy-start = (bf16[2048,512]{1,0:T(8,128)(2,1)S(1)}, bf16[2048,512]{1,0:T(8,128)(2,1)}, u32[]{:S(2)}) copy-start(bf16[2048,512]{1,0:T(8,128)(2,1)} %gate_ref.1) | copy-start | bytes 6291460
  29.0 5.2 %collective-permute-start.4 = (f32[8,16,128]{2,1,0:T(8,128)S(1)}, f32[8,16,128]{2,1,0:T(8,128)S(1)}, u32[]{:S(2)}, u32[]{:S(2)}) collective-permute-start(f32[8,16,128]{2,1,0:T(8,128)S(1)} %get-tuple-element.65), channel_id=1, source_target_pairs={{0,16},{2,18},{4,20},{6,22},{8,24},{10,26},{12,28},{14,30},{16,0},... | collective-permute-start | bytes 196616 | tf_op jit(solution)/shard_map/ppermute | solution.py:365
  34.3 1.3 %collective-permute-start.5 = (f32[8,16,128]{2,1,0:T(8,128)S(1)}, f32[8,16,128]{2,1,0:T(8,128)S(1)}, u32[]{:S(2)}, u32[]{:S(2)}) collective-permute-start(f32[8,16,128]{2,1,0:T(8,128)S(1)} %get-tuple-element.74), channel_id=1, source_target_pairs={{0,2},{2,0},{4,6},{6,4},{8,10},{10,8},{12,14},{14,12},{16,18},{18,... | collective-permute-start | bytes 196616 | tf_op jit(solution)/shard_map/ppermute | solution.py:365

commit v7 on v6

--- a/solution.py
+++ b/solution.py
@@ -14,7 +14,8 @@
 TILE = LANES * SUBS
 BLOCK = 128
 ROWS = 1024
-STEPS = 8
+STEPS = 16
+LONG = 32
 F32, BF16 = jnp.float32, jnp.bfloat16
 
 
@@ -118,20 +119,24 @@
         pltpu.make_async_copy(raw_weights_hbm, raw_weights, sems.at[tiles * 5 + 2]),
     ]
     large = [copies(tile) for tile in range(tiles)]
-    for copy in small + sum(large, []):
+    for copy in small + large[0]:
         copy.start()
-    small[0].wait()
+    for copy in small + large[0]:
+        copy.wait()
     sign = 1.0 - 2.0 * (lax.broadcasted_iota(jnp.int32, (1, 2 * BLOCK), 1) % 2).astype(F32)
     for tile in range(tiles):
         rows = slice(tile * TILE, (tile + 1) * TILE)
         groups = slice(tile * SUBS, (tile + 1) * SUBS)
-        large[tile][0].wait()
+        if tile:
+            for copy in large[tile]:
+                copy.wait()
+        if tile + 1 < tiles:
+            for copy in large[tile + 1]:
+                copy.start()
         tap_hi, tap_lo = split(taps[rows])
         spectrum = mm(twice(tap_hi), tables[:, EVEN]) + mm(tap_lo, tables[:BLOCK, EVEN])
         turned = spectrum * sign
         spec_ref[rows] = turned
-        for copy in large[tile][1:]:
-            copy.wait()
         earlier = mm(twice(v_first[rows]), tables[:, EVEN])
         for block in range(1, inner // BLOCK + 1):
             at = slice((block - 1) * BLOCK, block * BLOCK)
@@ -139,9 +144,6 @@
             short = apply_window(earlier, later, spectrum if block % 2 else turned, tables)
             put_mixed(store, 0, block - 1, short, gate_rest[rows, at])
             earlier = later
-        if tile == 0:
-            small[1].wait()
-            small[2].wait()
         lay_out(raw.at[:, pl.ds(tile * TILE, TILE)], laid)
         modes = raw.shape[0]
         rates = laid[...].reshape(modes, SUBS, LANES)
@@ -215,17 +217,17 @@
 
 def filtered(source, start, store, decay, scaled, bias, states):
     def turn(index, states):
-        at = pl.multiple_of(index * STEPS * SUBS, STEPS * SUBS)
-        values = source[pl.ds(start * SUBS + at, STEPS * SUBS), :].astype(F32)
+        at = pl.multiple_of(index * LONG * SUBS, LONG * SUBS)
+        values = source[pl.ds(start * SUBS + at, LONG * SUBS), :].astype(F32)
         sums = []
-        for step in range(STEPS):
+        for step in range(LONG):
             value = values[step * SUBS : (step + 1) * SUBS]
             states = tuple(d * s + value for d, s in zip(decay, states))
             sums.append(added([c * s for c, s in zip(scaled, states)] + [bias * value]))
-        store[pl.ds(at, STEPS * SUBS), :] = jnp.concatenate(sums, axis=0)
+        store[pl.ds(at, LONG * SUBS), :] = jnp.concatenate(sums, axis=0)
         return states
 
-    return lax.fori_loop(0, BLOCK // STEPS, turn, states)
+    return lax.fori_loop(0, BLOCK // LONG, turn, states)
 
 
 def local_kernel(start, mixed_ref, rates_ref, scaled_ref, bias_ref, *rest):
@@ -259,14 +261,14 @@
         for block, sums_ref in enumerate(sums_refs):
 
             def carry(index, states, sums_ref=sums_ref, block=block):
-                at = pl.multiple_of(index * STEPS * SUBS, STEPS * SUBS)
-                for step in range(STEPS):
+                at = pl.multiple_of(index * LONG * SUBS, LONG * SUBS)
+                for step in range(LONG):
                     states = tuple(d * s for d, s in zip(decay, states))
                     total = sums_ref[tile, pl.ds(at + step * SUBS, SUBS), :] + added(list(states))
                     store[pl.ds(block * BLOCK * SUBS + at + step * SUBS, SUBS), :] = total
                 return states
 
-            states = lax.fori_loop(0, BLOCK // STEPS, carry, states)
+            states = lax.fori_loop(0, BLOCK // LONG, carry, states)
         past = float((blocks - 1) * BLOCK)
         full = tuple(
             local_ref[mode, groups] + jnp.exp(-past * rates_ref[mode, groups]) * begin[mode, groups]

time: 44.1 us -> 43 us (0.975)
  Pallas kernels: 29.1 us -> 27.4 us
  waiting for transfers between devices: 2.6 us -> 3.23 us
    pallas_call x3, Pallas kernels: 7.61 us -> 6.98 us  [beside(): pl.pallas_call(functools.partial(local_kernel, start), in_specs=[WHOLE] *...]
    ppermute x5, waiting for transfers between devices: 2.6 us -> 3.23 us  [swap(): lax.ppermute(array, 'seq', [(i, i ^ distance) for i in range(shards)])]
    pallas_call x1, Pallas kernels: 8.31 us -> 7.76 us  [on_device(): pl.pallas_call(outer_kernel, in_specs=[SCALAR] + [WHOLE] * (8 + len(sums)...]
    pallas_call x1, Pallas kernels: 10.2 us -> 9.7 us  [on_device(): pl.pallas_call(functools.partial(inner_kernel, tokens * shards), in_specs...]
  transfers between devices with their start and end apart: 6 -> 6, of which waited for: 4 -> 5; matrix products, arithmetic and copies ran while one was open for 0% -> 0% of each run, Pallas kernels for 41% -> 39%
where the time goes in v7:
time: 43 us; the launch traced here: 42.8 us
  Pallas kernels  27.4 us (64%)
  starting transfers between devices  11 us (26%)
  waiting for transfers between devices  3.23 us (8%)
  local copies, waits for them, and re-layouts  1.09 us (3%)
    pallas_call x1, Pallas kernels, on_device(): pl.pallas_call(functools.partial(inner_kernel, tokens * shards), in_specs...  9.7 us
    ppermute x5, starting transfers between devices, swap(): lax.ppermute(array, 'seq', [(i, i ^ distance) for i in range(shards)])  8.62 us
    pallas_call x1, Pallas kernels, on_device(): pl.pallas_call(outer_kernel, in_specs=[SCALAR] + [WHOLE] * (8 + len(sums)...  7.76 us
    pallas_call x3, Pallas kernels, beside(): pl.pallas_call(functools.partial(local_kernel, start), in_specs=[WHOLE] *...  6.98 us
    ppermute x5, waiting for transfers between devices, swap(): lax.ppermute(array, 'seq', [(i, i ^ distance) for i in range(shards)])  3.23 us
    pallas_call x1, Pallas kernels, on_device(): pl.pallas_call(functools.partial(rim_kernel, inner), in_specs=[SCALAR] +...  2.78 us
    ppermute x1, starting transfers between devices, on_device(): lax.ppermute(v_stream[:, tokens - BLOCK:], 'seq', [(i, i + 1) for i in ra...  2.39 us
    slice x1, local copies, waits for them, and re-layouts, on_device(): v_stream[:, tokens - BLOCK:]  1.08 us
  transfers between devices with their start and end apart: 6, of which 5 were waited for; matrix products, arithmetic and copies ran while one was open for 0% of the time, Pallas kernels for 39%

profile of v7, /device:TPU:0, one launch (start us, length us, event | category | flops | bytes accessed | tf_op | source)
XLA Modules:
  0.0 42.8 jit_solution(5049099673048658681)
XLA Ops:
  0.0 1.1 %slice.3 = bf16[2048,128]{1,0:T(8,128)(2,1)S(1)} slice(bf16[2048,512]{1,0:T(8,128)(2,1)} %v_hbm.1), slice={[0:2048], [384:512]} | slice | bytes 1048576 | tf_op jit(solution)/shard_map/slice | solution.py:312
  1.1 2.4 %collective-permute-start = (bf16[2048,128]{1,0:T(8,128)(2,1)S(1)}, bf16[2048,128]{1,0:T(8,128)(2,1)S(1)}, u32[]{:S(2)}, u32[]{:S(2)}) collective-permute-start(bf16[2048,128]{1,0:T(8,128)(2,1)S(1)} %slice.3), channel_id=1, source_target_pairs={{0,2},{2,4},{4,6},{6,8},{8,10},{10,12},{12,14},{14,16},{16,18},{18... | collective-permute-start | bytes 1572872 | tf_op jit(solution)/shard_map/ppermute | solution.py:312
  3.5 9.7 %shard_map.82 = (f32[2048,256]{1,0:T(8,128)S(1)}, bf16[2,3072,128]{2,1,0:T(8,128)(2,1)S(1)}, f32[16,16,128]{2,1,0:T(8,128)S(1)}, f32[16,16,128]{2,1,0:T(8,128)S(...) custom-call(bf16[2048,512]{1,0:T(8,128)(2,1)} %v_hbm.1, ...), custom_call_target="tpu_custom_call" | custom-call | flops 2044723200 | bytes 8388608 | tf_op jit(solution)/shard_map/pallas_call | solution.py:333
  13.2 0.0 collective-permute-done.before_ref
  13.2 0.0 copy-start.1
  13.2 2.8 %shard_map.83 = (bf16[2,1024,128]{2,1,0:T(8,128)(2,1)S(1)}, f32[8,16,128]{2,1,0:T(8,128)S(1)}, f32[8,16,128]{2,1,0:T(8,128)S(1)}) custom-call(s32[1]{0:T(128)} %bitcast.place_ref, bf16[2048,128]{1,0:T(8,128)(2,1)S(1)} %collective-permute-done.before_ref, bf16[2048,128]{1,0:T(8,128)(2,1)S(1)} %get-tuple-element.45.v_ref, ...), custom_call_target="tpu_custom_call" | custom-call | flops 681574400 | bytes 4194304 | tf_op jit(solution)/shard_map/pallas_call | solution.py:354
  16.0 2.7 %collective-permute-start.1 = (f32[8,16,128]{2,1,0:T(8,128)S(1)}, f32[8,16,128]{2,1,0:T(8,128)S(1)}, u32[]{:S(2)}, u32[]{:S(2)}) collective-permute-start(f32[8,16,128]{2,1,0:T(8,128)S(1)} %get-tuple-element.51), channel_id=1, source_target_pairs={{0,2},{2,0},{4,6},{6,4},{8,10},{10,8},{12,14},{14,12},{16,18},{18,... | collective-permute-start | bytes 196616 | tf_op jit(solution)/shard_map/ppermute | solution.py:367
  18.7 0.9 %collective-permute-done.1.other_ref.twin_ref = f32[8,16,128]{2,1,0:T(8,128)S(1)} collective-permute-done((f32[8,16,128]{2,1,0:T(8,128)S(1)}, f32[8,16,128]{2,1,0:T(8,128)S(1)}, u32[]{:S(2)}, u32[]{:S(2)}) %collective-permute-start.1) | collective-permute-done | bytes 65568 | tf_op jit(solution)/shard_map/ppermute | solution.py:367
  19.6 1.6 %collective-permute-start.2 = (f32[8,16,128]{2,1,0:T(8,128)S(1)}, f32[8,16,128]{2,1,0:T(8,128)S(1)}, u32[]{:S(2)}, u32[]{:S(2)}) collective-permute-start(f32[8,16,128]{2,1,0:T(8,128)S(1)} %shard_map.84.total_ref), channel_id=1, source_target_pairs={{0,4},{2,6},{4,0},{6,2},{8,12},{10,14},{12,8},{14,10},{16,20},{18,... | collective-permute-start | bytes 196616 | tf_op jit(solution)/shard_map/ppermute | solution.py:367
  21.2 0.0 copy-done.1
  21.2 2.3 %shard_map.85 = (f32[2,1024,128]{2,1,0:T(8,128)S(1)}, f32[16,16,128]{2,1,0:T(8,128)S(1)}) custom-call(bf16[2,1024,128]{2,1,0:T(8,128)(2,1)S(1)} %get-tuple-element.53.mixed_ref, f32[16,16,128]{2,1,0:T(8,128)S(1)} %get-tuple-element.43.rates_ref, f32[16,16,128]{2,1,0:T(8,128)S(1)} %get-tuple-element.44.scaled_ref, f32[16,128]{1,0:T(8,128)S(1)} %bitcast.4), custom_call_target="tpu_custom_call" | custom-call | flops 681574400 | bytes 4194304 | tf_op jit(solution)/shard_map/pallas_call | solution.py:386
  23.5 0.5 %collective-permute-done.2.other_ref = f32[8,16,128]{2,1,0:T(8,128)S(1)} collective-permute-done((f32[8,16,128]{2,1,0:T(8,128)S(1)}, f32[8,16,128]{2,1,0:T(8,128)S(1)}, u32[]{:S(2)}, u32[]{:S(2)}) %collective-permute-start.2) | collective-permute-done | bytes 65568 | tf_op jit(solution)/shard_map/ppermute | solution.py:367
  24.1 1.6 %collective-permute-start.3 = (f32[8,16,128]{2,1,0:T(8,128)S(1)}, f32[8,16,128]{2,1,0:T(8,128)S(1)}, u32[]{:S(2)}, u32[]{:S(2)}) collective-permute-start(f32[8,16,128]{2,1,0:T(8,128)S(1)} %get-tuple-element.57.total_ref), channel_id=1, source_target_pairs={{0,8},{2,10},{4,12},{6,14},{8,0},{10,2},{12,4},{14,6},{16,24},{18,... | collective-permute-start | bytes 196616 | tf_op jit(solution)/shard_map/ppermute | solution.py:367
  25.7 2.3 %shard_map.87 = (f32[2,1024,128]{2,1,0:T(8,128)S(1)}, f32[16,16,128]{2,1,0:T(8,128)S(1)}) custom-call(bf16[2,3072,128]{2,1,0:T(8,128)(2,1)S(1)} %get-tuple-element.67.mixed_ref, f32[16,16,128]{2,1,0:T(8,128)S(1)} %get-tuple-element.43.rates_ref, f32[16,16,128]{2,1,0:T(8,128)S(1)} %get-tuple-element.44.scaled_ref, f32[16,128]{1,0:T(8,128)S(1)} %bitcast.5, ...), custom_call_target="tpu_custom_call" | custom-call | flops 681574400 | bytes 4194304 | tf_op jit(solution)/shard_map/pallas_call | solution.py:386
  28.0 0.0 copy-start
  28.1 0.3 collective-permute-done.3.other_ref
  28.5 2.7 %collective-permute-start.4 = (f32[8,16,128]{2,1,0:T(8,128)S(1)}, f32[8,16,128]{2,1,0:T(8,128)S(1)}, u32[]{:S(2)}, u32[]{:S(2)}) collective-permute-start(f32[8,16,128]{2,1,0:T(8,128)S(1)} %get-tuple-element.65), channel_id=1, source_target_pairs={{0,16},{2,18},{4,20},{6,22},{8,24},{10,26},{12,28},{14,30},{16,0},... | collective-permute-start | bytes 196616 | tf_op jit(solution)/shard_map/ppermute | solution.py:367
  31.1 2.3 %shard_map.89 = (f32[2,1024,128]{2,1,0:T(8,128)S(1)}, f32[16,16,128]{2,1,0:T(8,128)S(1)}) custom-call(bf16[2,3072,128]{2,1,0:T(8,128)(2,1)S(1)} %get-tuple-element.67.mixed_ref, f32[16,16,128]{2,1,0:T(8,128)S(1)} %get-tuple-element.43.rates_ref, f32[16,16,128]{2,1,0:T(8,128)S(1)} %get-tuple-element.44.scaled_ref, f32[16,128]{1,0:T(8,128)S(1)} %bitcast.6, ...), custom_call_target="tpu_custom_call" | custom-call | flops 681574400 | bytes 4194304 | tf_op jit(solution)/shard_map/pallas_call | solution.py:386
  33.4 0.2 collective-permute-done.4.other_ref
  33.7 0.1 collective-permute-start.5
  33.8 1.2 %collective-permute-done.5.twins_ref = f32[8,16,128]{2,1,0:T(8,128)S(1)} collective-permute-done((f32[8,16,128]{2,1,0:T(8,128)S(1)}, f32[8,16,128]{2,1,0:T(8,128)S(1)}, u32[]{:S(2)}, u32[]{:S(2)}) %collective-permute-start.5) | collective-permute-done | bytes 65568 | tf_op jit(solution)/shard_map/ppermute | solution.py:367
  35.0 0.0 copy-done
  35.1 7.8 %shard_map.91 = bf16[2048,512]{1,0:T(8,128)(2,1)} custom-call(s32[1]{0:T(128)} %bitcast.place_ref, bf16[2,3072,128]{2,1,0:T(8,128)(2,1)S(1)} %get-tuple-element.67.mixed_ref, bf16[2048,512]{1,0:T(8,128)(2,1)S(1)} %copy-done, f32[16,16,128]{2,1,0:T(8,128)S(1)} %get-tuple-element.43.rates_ref, f32[16,16,128]{2,1,0:T(8,128)S(1)} %get-tuple-element.44.scaled_ref, ...), custom_call_target="tpu_custom_call" | custom-call | flops 52428800 | bytes 6291456 | tf_op jit(solution)/shard_map/pallas_call | solution.py:415
  (5 shorter events, 0.2 us)
Async XLA Ops:
  1.1 12.1 %collective-permute-start = (bf16[2048,128]{1,0:T(8,128)(2,1)S(1)}, bf16[2048,128]{1,0:T(8,128)(2,1)S(1)}, u32[]{:S(2)}, u32[]{:S(2)}) collective-permute-start(bf16[2048,128]{1,0:T(8,128)(2,1)S(1)} %slice.3), channel_id=1, source_target_pairs={{0,2},{2,4},{4,6},{6,8},{8,10},{10,12},{12,14},{14,16},{16,18},{18... | collective-permute-start | bytes 1572872 | tf_op jit(solution)/shard_map/ppermute | solution.py:312
  13.2 8.0 %copy-start.1 = (f32[2048]{0:T(1024)S(1)}, f32[2048]{0:T(1024)}, u32[]{:S(2)}) copy-start(f32[2048]{0:T(1024)} %param.14) | copy-start | bytes 24580
  16.0 3.6 %collective-permute-start.1 = (f32[8,16,128]{2,1,0:T(8,128)S(1)}, f32[8,16,128]{2,1,0:T(8,128)S(1)}, u32[]{:S(2)}, u32[]{:S(2)}) collective-permute-start(f32[8,16,128]{2,1,0:T(8,128)S(1)} %get-tuple-element.51), channel_id=1, source_target_pairs={{0,2},{2,0},{4,6},{6,4},{8,10},{10,8},{12,14},{14,12},{16,18},{18,... | collective-permute-start | bytes 196616 | tf_op jit(solution)/shard_map/ppermute | solution.py:367
  19.6 4.4 %collective-permute-start.2 = (f32[8,16,128]{2,1,0:T(8,128)S(1)}, f32[8,16,128]{2,1,0:T(8,128)S(1)}, u32[]{:S(2)}, u32[]{:S(2)}) collective-permute-start(f32[8,16,128]{2,1,0:T(8,128)S(1)} %shard_map.84.total_ref), channel_id=1, source_target_pairs={{0,4},{2,6},{4,0},{6,2},{8,12},{10,14},{12,8},{14,10},{16,20},{18,... | collective-permute-start | bytes 196616 | tf_op jit(solution)/shard_map/ppermute | solution.py:367
  24.1 4.3 %collective-permute-start.3 = (f32[8,16,128]{2,1,0:T(8,128)S(1)}, f32[8,16,128]{2,1,0:T(8,128)S(1)}, u32[]{:S(2)}, u32[]{:S(2)}) collective-permute-start(f32[8,16,128]{2,1,0:T(8,128)S(1)} %get-tuple-element.57.total_ref), channel_id=1, source_target_pairs={{0,8},{2,10},{4,12},{6,14},{8,0},{10,2},{12,4},{14,6},{16,24},{18,... | collective-permute-start | bytes 196616 | tf_op jit(solution)/shard_map/ppermute | solution.py:367
  28.0 7.0 %copy-start = (bf16[2048,512]{1,0:T(8,128)(2,1)S(1)}, bf16[2048,512]{1,0:T(8,128)(2,1)}, u32[]{:S(2)}) copy-start(bf16[2048,512]{1,0:T(8,128)(2,1)} %gate_ref.1) | copy-start | bytes 6291460
  28.5 5.2 %collective-permute-start.4 = (f32[8,16,128]{2,1,0:T(8,128)S(1)}, f32[8,16,128]{2,1,0:T(8,128)S(1)}, u32[]{:S(2)}, u32[]{:S(2)}) collective-permute-start(f32[8,16,128]{2,1,0:T(8,128)S(1)} %get-tuple-element.65), channel_id=1, source_target_pairs={{0,16},{2,18},{4,20},{6,22},{8,24},{10,26},{12,28},{14,30},{16,0},... | collective-permute-start | bytes 196616 | tf_op jit(solution)/shard_map/ppermute | solution.py:367
  33.7 1.3 %collective-permute-start.5 = (f32[8,16,128]{2,1,0:T(8,128)S(1)}, f32[8,16,128]{2,1,0:T(8,128)S(1)}, u32[]{:S(2)}, u32[]{:S(2)}) collective-permute-start(f32[8,16,128]{2,1,0:T(8,128)S(1)} %get-tuple-element.74), channel_id=1, source_target_pairs={{0,2},{2,0},{4,6},{6,4},{8,10},{10,8},{12,14},{14,12},{16,18},{18,... | collective-permute-start | bytes 196616 | tf_op jit(solution)/shard_map/ppermute | solution.py:367

commit v8 on v7

--- a/solution.py
+++ b/solution.py
@@ -245,39 +245,65 @@
             states_ref[mode, groups] = states[mode]
 
 
-def outer_kernel(place_ref, mixed_ref, gate_ref, rates_ref, scaled_ref, bias_ref, mine_ref, twins_ref, local_ref, *rest):
+def half_modes(which, start_ref, rates_ref, scaled_ref, groups, past):
+    half = start_ref.shape[0]
+    rates = rates_ref[pl.ds(which * half, half), groups]
+    states = scaled_ref[pl.ds(which * half, half), groups] * start_ref[:, groups]
+    if past:
+        states = states * jnp.exp(-float(past) * rates)
+    decay = jnp.exp(-rates)
+    return [decay[mode] for mode in range(half)], tuple(states[mode] for mode in range(half))
+
+
+def add_carry(sums, into, decay, states):
+    def turn(index, states):
+        at = pl.multiple_of(index * LONG * SUBS, LONG * SUBS)
+        for step in range(LONG):
+            states = tuple(d * s for d, s in zip(decay, states))
+            where = pl.ds(at + step * SUBS, SUBS)
+            into[where, :] = sums[where, :] + added(list(states))
+        return states
+
+    return lax.fori_loop(0, BLOCK // LONG, turn, states)
+
+
+def own_carry_kernel(place_ref, rates_ref, scaled_ref, mine_ref, *sums_refs):
+    count = len(sums_refs) // 2
+    for tile in range(sums_refs[0].shape[0]):
+        groups = slice(tile * SUBS, (tile + 1) * SUBS)
+        decay, states = half_modes(place_ref[0] % 2, mine_ref, rates_ref, scaled_ref, groups, 0)
+        for before, after in zip(sums_refs[:count], sums_refs[count:]):
+            states = add_carry(before.at[tile], after.at[tile], decay, states)
+
+
+def outer_kernel(
+    own_done, place_ref, mixed_ref, gate_ref, rates_ref, scaled_ref, bias_ref, mine_ref, twins_ref, local_ref, *rest
+):
     *sums_refs, out_hbm, store, begin, out, sems = rest
     modes, half = rates_ref.shape[0], mine_ref.shape[0]
     core = place_ref[0] % 2
     begin[pl.ds(core * half, half)] = mine_ref[...]
     begin[pl.ds((1 - core) * half, half)] = twins_ref[...]
     blocks = len(sums_refs) + 1
+    last = (blocks - 1) * BLOCK
     copies = []
     for tile in range(mixed_ref.shape[0]):
         groups = slice(tile * SUBS, (tile + 1) * SUBS)
+        decay, states = half_modes(1 - core, twins_ref, rates_ref, scaled_ref, groups, 0)
+        for block, sums_ref in enumerate(sums_refs):
+            if block == own_done:
+                more = half_modes(core, mine_ref, rates_ref, scaled_ref, groups, own_done * BLOCK)
+                decay, states = decay + more[0], states + more[1]
+            into = store.at[pl.ds(block * BLOCK * SUBS, BLOCK * SUBS)]
+            states = add_carry(sums_ref.at[tile], into, decay, states)
         decay = [jnp.exp(-rates_ref[mode, groups]) for mode in range(modes)]
         scaled = [scaled_ref[mode, groups] for mode in range(modes)]
-        states = tuple(c * begin[mode, groups] for mode, c in enumerate(scaled))
-        for block, sums_ref in enumerate(sums_refs):
-
-            def carry(index, states, sums_ref=sums_ref, block=block):
-                at = pl.multiple_of(index * LONG * SUBS, LONG * SUBS)
-                for step in range(LONG):
-                    states = tuple(d * s for d, s in zip(decay, states))
-                    total = sums_ref[tile, pl.ds(at + step * SUBS, SUBS), :] + added(list(states))
-                    store[pl.ds(block * BLOCK * SUBS + at + step * SUBS, SUBS), :] = total
-                return states
-
-            states = lax.fori_loop(0, BLOCK // LONG, carry, states)
-        past = float((blocks - 1) * BLOCK)
         full = tuple(
-            local_ref[mode, groups] + jnp.exp(-past * rates_ref[mode, groups]) * begin[mode, groups]
+            local_ref[mode, groups] + jnp.exp(-float(last) * rates_ref[mode, groups]) * begin[mode, groups]
             for mode in range(modes)
         )
-        last = (blocks - 1) * BLOCK
-        filtered(
-            mixed_ref.at[tile], last - BLOCK, store.at[pl.ds(last * SUBS, BLOCK * SUBS)], decay, scaled, bias_ref[groups], full
-        )
+        into = store.at[pl.ds(last * SUBS, BLOCK * SUBS)]
+        filtered(mixed_ref.at[tile], last - BLOCK, into, decay, scaled, bias_ref[groups], full)
         for group in range(SUBS):
             rows = slice(tile * TILE + group * LANES, tile * TILE + (group + 1) * LANES)
             for block in range(blocks):
@@ -294,6 +320,7 @@
 SCALAR = pl.BlockSpec(memory_space=pltpu.SMEM)
 WHOLE = pl.BlockSpec(memory_space=pltpu.VMEM)
 FAR = pl.BlockSpec(memory_space=pltpu.HBM)
+OWN = 2
 INNER_ROOM, RIM_ROOM = 32, 24
 
 
@@ -408,12 +435,22 @@
         size *= 2
     other = beside(swap(total, size), total)
     mine, twins = small(functools.partial(start_kernel, tokens, size), 2, other, ahead, own_end, twin_end)
-    twins = swap(twins, 1)
     while len(sums) < tokens // BLOCK - 1:
         beside(total, total)
+    twins = swap(twins, 1)
+    sums[:OWN] = pl.pallas_call(
+        own_carry_kernel,
+        in_specs=[SCALAR] + [WHOLE] * (3 + OWN),
+        out_specs=[WHOLE] * OWN,
+        out_shape=[shape(sums[0].shape, F32)] * OWN,
+        compiler_params=pltpu.CompilerParams(vmem_limit_bytes=8 << 20),
+        cost_estimate=pl.CostEstimate(
+            flops=channels * OWN * BLOCK * 600, bytes_accessed=channels * BLOCK * 16, transcendentals=0
+        ),
+    )(place, rates, scaled, mine, *sums[:OWN])
 
     hyena_out = pl.pallas_call(
-        outer_kernel,
+        functools.partial(outer_kernel, OWN),
         in_specs=[SCALAR] + [WHOLE] * (8 + len(sums)),
         out_specs=FAR,
         out_shape=shape((channels, tokens), BF16),

time: 43 us -> 42 us (0.977)
  waiting for transfers between devices: 3.23 us -> 2.05 us
    ppermute x5, waiting for transfers between devices: 3.23 us -> 2.05 us  [swap(): lax.ppermute(array, 'seq', [(i, i ^ distance) for i in range(shards)])]
    pallas_call x1 -> x2, Pallas kernels: 7.76 us -> 7.89 us  [the longest x1 6.7 us: on_device(): pl.pallas_call(functools.partial(outer_kernel, OWN), in_specs=[SCALAR] +...]
  transfers between devices with their start and end apart: 6 -> 6, of which waited for: 5 -> 4; matrix products, arithmetic and copies ran while one was open for 0% -> 0% of each run, Pallas kernels for 39% -> 43%
where the time goes in v8:
time: 42 us; the launch traced here: 41.8 us
  Pallas kernels  27.5 us (65%)
  starting transfers between devices  11 us (26%)
  waiting for transfers between devices  2.05 us (5%)
  local copies, waits for them, and re-layouts  1.09 us (3%)
    pallas_call x1, Pallas kernels, on_device(): pl.pallas_call(functools.partial(inner_kernel, tokens * shards), in_specs...  9.7 us
    ppermute x5, starting transfers between devices, swap(): lax.ppermute(array, 'seq', [(i, i ^ distance) for i in range(shards)])  8.62 us
    pallas_call x3, Pallas kernels, beside(): pl.pallas_call(functools.partial(local_kernel, start), in_specs=[WHOLE] *...  6.98 us
    pallas_call x1, Pallas kernels, on_device(): pl.pallas_call(functools.partial(outer_kernel, OWN), in_specs=[SCALAR] +...  6.7 us
    pallas_call x1, Pallas kernels, on_device(): pl.pallas_call(functools.partial(rim_kernel, inner), in_specs=[SCALAR] +...  2.78 us
    ppermute x1, starting transfers between devices, on_device(): lax.ppermute(v_stream[:, tokens - BLOCK:], 'seq', [(i, i + 1) for i in ra...  2.39 us
    ppermute x5, waiting for transfers between devices, swap(): lax.ppermute(array, 'seq', [(i, i ^ distance) for i in range(shards)])  2.05 us
    pallas_call x1, Pallas kernels, on_device(): pl.pallas_call(own_carry_kernel, in_specs=[SCALAR] + [WHOLE] * (3 + OWN),...  1.19 us
  transfers between devices with their start and end apart: 6, of which 4 were waited for; matrix products, arithmetic and copies ran while one was open for 0% of the time, Pallas kernels for 43%

profile of v8, /device:TPU:0, one launch (start us, length us, event | category | flops | bytes accessed | tf_op | source)
XLA Modules:
  0.0 41.8 jit_solution(7825619427694439085)
XLA Ops:
  0.0 1.1 %slice.3 = bf16[2048,128]{1,0:T(8,128)(2,1)S(1)} slice(bf16[2048,512]{1,0:T(8,128)(2,1)} %v_hbm.1), slice={[0:2048], [384:512]} | slice | bytes 1048576 | tf_op jit(solution)/shard_map/slice | solution.py:339
  1.1 2.4 %collective-permute-start = (bf16[2048,128]{1,0:T(8,128)(2,1)S(1)}, bf16[2048,128]{1,0:T(8,128)(2,1)S(1)}, u32[]{:S(2)}, u32[]{:S(2)}) collective-permute-start(bf16[2048,128]{1,0:T(8,128)(2,1)S(1)} %slice.3), channel_id=1, source_target_pairs={{0,2},{2,4},{4,6},{6,8},{8,10},{10,12},{12,14},{14,16},{16,18},{18... | collective-permute-start | bytes 1572872 | tf_op jit(solution)/shard_map/ppermute | solution.py:339
  3.5 9.7 %shard_map.82 = (f32[2048,256]{1,0:T(8,128)S(1)}, bf16[2,3072,128]{2,1,0:T(8,128)(2,1)S(1)}, f32[16,16,128]{2,1,0:T(8,128)S(1)}, f32[16,16,128]{2,1,0:T(8,128)S(...) custom-call(bf16[2048,512]{1,0:T(8,128)(2,1)} %v_hbm.1, ...), custom_call_target="tpu_custom_call" | custom-call | flops 2044723200 | bytes 8388608 | tf_op jit(solution)/shard_map/pallas_call | solution.py:360
  13.2 0.0 collective-permute-done.before_ref
  13.2 0.0 copy-start.1
  13.2 2.8 %shard_map.83 = (bf16[2,1024,128]{2,1,0:T(8,128)(2,1)S(1)}, f32[8,16,128]{2,1,0:T(8,128)S(1)}, f32[8,16,128]{2,1,0:T(8,128)S(1)}) custom-call(s32[1]{0:T(128)} %bitcast.place_ref, bf16[2048,128]{1,0:T(8,128)(2,1)S(1)} %collective-permute-done.before_ref, bf16[2048,128]{1,0:T(8,128)(2,1)S(1)} %get-tuple-element.47.v_ref, ...), custom_call_target="tpu_custom_call" | custom-call | flops 681574400 | bytes 4194304 | tf_op jit(solution)/shard_map/pallas_call | solution.py:381
  16.0 2.7 %collective-permute-start.1 = (f32[8,16,128]{2,1,0:T(8,128)S(1)}, f32[8,16,128]{2,1,0:T(8,128)S(1)}, u32[]{:S(2)}, u32[]{:S(2)}) collective-permute-start(f32[8,16,128]{2,1,0:T(8,128)S(1)} %get-tuple-element.53), channel_id=1, source_target_pairs={{0,2},{2,0},{4,6},{6,4},{8,10},{10,8},{12,14},{14,12},{16,18},{18,... | collective-permute-start | bytes 196616 | tf_op jit(solution)/shard_map/ppermute | solution.py:394
  18.7 0.9 %collective-permute-done.1.other_ref.twin_ref = f32[8,16,128]{2,1,0:T(8,128)S(1)} collective-permute-done((f32[8,16,128]{2,1,0:T(8,128)S(1)}, f32[8,16,128]{2,1,0:T(8,128)S(1)}, u32[]{:S(2)}, u32[]{:S(2)}) %collective-permute-start.1) | collective-permute-done | bytes 65568 | tf_op jit(solution)/shard_map/ppermute | solution.py:394
  19.6 1.6 %collective-permute-start.2 = (f32[8,16,128]{2,1,0:T(8,128)S(1)}, f32[8,16,128]{2,1,0:T(8,128)S(1)}, u32[]{:S(2)}, u32[]{:S(2)}) collective-permute-start(f32[8,16,128]{2,1,0:T(8,128)S(1)} %shard_map.84.total_ref), channel_id=1, source_target_pairs={{0,4},{2,6},{4,0},{6,2},{8,12},{10,14},{12,8},{14,10},{16,20},{18,... | collective-permute-start | bytes 196616 | tf_op jit(solution)/shard_map/ppermute | solution.py:394
  21.2 0.0 copy-done.1
  21.2 2.3 %shard_map.85 = (f32[2,1024,128]{2,1,0:T(8,128)S(1)}, f32[16,16,128]{2,1,0:T(8,128)S(1)}) custom-call(bf16[2,1024,128]{2,1,0:T(8,128)(2,1)S(1)} %get-tuple-element.55.mixed_ref, f32[16,16,128]{2,1,0:T(8,128)S(1)} %get-tuple-element.45.rates_ref, f32[16,16,128]{2,1,0:T(8,128)S(1)} %get-tuple-element.46.scaled_ref, f32[16,128]{1,0:T(8,128)S(1)} %bitcast.4), custom_call_target="tpu_custom_call" | custom-call | flops 681574400 | bytes 4194304 | tf_op jit(solution)/shard_map/pallas_call | solution.py:413
  23.5 0.5 %collective-permute-done.2.other_ref = f32[8,16,128]{2,1,0:T(8,128)S(1)} collective-permute-done((f32[8,16,128]{2,1,0:T(8,128)S(1)}, f32[8,16,128]{2,1,0:T(8,128)S(1)}, u32[]{:S(2)}, u32[]{:S(2)}) %collective-permute-start.2) | collective-permute-done | bytes 65568 | tf_op jit(solution)/shard_map/ppermute | solution.py:394
  24.1 1.6 %collective-permute-start.3 = (f32[8,16,128]{2,1,0:T(8,128)S(1)}, f32[8,16,128]{2,1,0:T(8,128)S(1)}, u32[]{:S(2)}, u32[]{:S(2)}) collective-permute-start(f32[8,16,128]{2,1,0:T(8,128)S(1)} %get-tuple-element.59.total_ref), channel_id=1, source_target_pairs={{0,8},{2,10},{4,12},{6,14},{8,0},{10,2},{12,4},{14,6},{16,24},{18,... | collective-permute-start | bytes 196616 | tf_op jit(solution)/shard_map/ppermute | solution.py:394
  25.7 2.3 %shard_map.87 = (f32[2,1024,128]{2,1,0:T(8,128)S(1)}, f32[16,16,128]{2,1,0:T(8,128)S(1)}) custom-call(bf16[2,3072,128]{2,1,0:T(8,128)(2,1)S(1)} %get-tuple-element.69.mixed_ref, f32[16,16,128]{2,1,0:T(8,128)S(1)} %get-tuple-element.45.rates_ref, f32[16,16,128]{2,1,0:T(8,128)S(1)} %get-tuple-element.46.scaled_ref, f32[16,128]{1,0:T(8,128)S(1)} %bitcast.5, ...), custom_call_target="tpu_custom_call" | custom-call | flops 681574400 | bytes 4194304 | tf_op jit(solution)/shard_map/pallas_call | solution.py:413
  28.0 0.4 collective-permute-done.3.other_ref
  28.4 0.0 copy-start
  28.5 2.7 %collective-permute-start.4 = (f32[8,16,128]{2,1,0:T(8,128)S(1)}, f32[8,16,128]{2,1,0:T(8,128)S(1)}, u32[]{:S(2)}, u32[]{:S(2)}) collective-permute-start(f32[8,16,128]{2,1,0:T(8,128)S(1)} %get-tuple-element.67), channel_id=1, source_target_pairs={{0,16},{2,18},{4,20},{6,22},{8,24},{10,26},{12,28},{14,30},{16,0},... | collective-permute-start | bytes 196616 | tf_op jit(solution)/shard_map/ppermute | solution.py:394
  31.1 2.3 %shard_map.89 = (f32[2,1024,128]{2,1,0:T(8,128)S(1)}, f32[16,16,128]{2,1,0:T(8,128)S(1)}) custom-call(bf16[2,3072,128]{2,1,0:T(8,128)(2,1)S(1)} %get-tuple-element.69.mixed_ref, f32[16,16,128]{2,1,0:T(8,128)S(1)} %get-tuple-element.45.rates_ref, f32[16,16,128]{2,1,0:T(8,128)S(1)} %get-tuple-element.46.scaled_ref, f32[16,128]{1,0:T(8,128)S(1)} %bitcast.6, ...), custom_call_target="tpu_custom_call" | custom-call | flops 681574400 | bytes 4194304 | tf_op jit(solution)/shard_map/pallas_call | solution.py:413
  33.4 0.2 collective-permute-done.4.other_ref
  33.7 0.1 collective-permute-start.5
  33.8 1.2 %shard_map.91 = (f32[2,1024,128]{2,1,0:T(8,128)S(1)}, f32[2,1024,128]{2,1,0:T(8,128)S(1)}) custom-call(s32[1]{0:T(128)} %bitcast.place_ref, f32[16,16,128]{2,1,0:T(8,128)S(1)} %get-tuple-element.45.rates_ref, f32[16,16,128]{2,1,0:T(8,128)S(1)} %get-tuple-element.46.scaled_ref, f32[8,16,128]{2,1,0:T(8,128)S(1)} %get-tuple-element.75.mine_ref, ...), custom_call_target="tpu_custom_call" | custom-call | flops 314572800 | bytes 4194304 | tf_op jit(solution)/shard_map/pallas_call | solution.py:441
  35.0 0.0 collective-permute-done.5.twins_ref
  35.1 0.0 copy-done
  35.1 6.7 %shard_map.92 = bf16[2048,512]{1,0:T(8,128)(2,1)} custom-call(s32[1]{0:T(128)} %bitcast.place_ref, bf16[2,3072,128]{2,1,0:T(8,128)(2,1)S(1)} %get-tuple-element.69.mixed_ref, bf16[2048,512]{1,0:T(8,128)(2,1)S(1)} %copy-done, f32[16,16,128]{2,1,0:T(8,128)S(1)} %get-tuple-element.45.rates_ref, f32[16,16,128]{2,1,0:T(8,128)S(1)} %get-tuple-element.46.scaled_ref, ...), custom_call_target="tpu_custom_call" | custom-call | flops 52428800 | bytes 6291456 | tf_op jit(solution)/shard_map/pallas_call | solution.py:452
  (5 shorter events, 0.2 us)
Async XLA Ops:
  1.1 12.1 %collective-permute-start = (bf16[2048,128]{1,0:T(8,128)(2,1)S(1)}, bf16[2048,128]{1,0:T(8,128)(2,1)S(1)}, u32[]{:S(2)}, u32[]{:S(2)}) collective-permute-start(bf16[2048,128]{1,0:T(8,128)(2,1)S(1)} %slice.3), channel_id=1, source_target_pairs={{0,2},{2,4},{4,6},{6,8},{8,10},{10,12},{12,14},{14,16},{16,18},{18... | collective-permute-start | bytes 1572872 | tf_op jit(solution)/shard_map/ppermute | solution.py:339
  13.2 8.0 %copy-start.1 = (f32[2048]{0:T(1024)S(1)}, f32[2048]{0:T(1024)}, u32[]{:S(2)}) copy-start(f32[2048]{0:T(1024)} %param.14) | copy-start | bytes 24580
  16.0 3.6 %collective-permute-start.1 = (f32[8,16,128]{2,1,0:T(8,128)S(1)}, f32[8,16,128]{2,1,0:T(8,128)S(1)}, u32[]{:S(2)}, u32[]{:S(2)}) collective-permute-start(f32[8,16,128]{2,1,0:T(8,128)S(1)} %get-tuple-element.53), channel_id=1, source_target_pairs={{0,2},{2,0},{4,6},{6,4},{8,10},{10,8},{12,14},{14,12},{16,18},{18,... | collective-permute-start | bytes 196616 | tf_op jit(solution)/shard_map/ppermute | solution.py:394
  19.6 4.4 %collective-permute-start.2 = (f32[8,16,128]{2,1,0:T(8,128)S(1)}, f32[8,16,128]{2,1,0:T(8,128)S(1)}, u32[]{:S(2)}, u32[]{:S(2)}) collective-permute-start(f32[8,16,128]{2,1,0:T(8,128)S(1)} %shard_map.84.total_ref), channel_id=1, source_target_pairs={{0,4},{2,6},{4,0},{6,2},{8,12},{10,14},{12,8},{14,10},{16,20},{18,... | collective-permute-start | bytes 196616 | tf_op jit(solution)/shard_map/ppermute | solution.py:394
  24.1 4.3 %collective-permute-start.3 = (f32[8,16,128]{2,1,0:T(8,128)S(1)}, f32[8,16,128]{2,1,0:T(8,128)S(1)}, u32[]{:S(2)}, u32[]{:S(2)}) collective-permute-start(f32[8,16,128]{2,1,0:T(8,128)S(1)} %get-tuple-element.59.total_ref), channel_id=1, source_target_pairs={{0,8},{2,10},{4,12},{6,14},{8,0},{10,2},{12,4},{14,6},{16,24},{18,... | collective-permute-start | bytes 196616 | tf_op jit(solution)/shard_map/ppermute | solution.py:394
  28.4 6.6 %copy-start = (bf16[2048,512]{1,0:T(8,128)(2,1)S(1)}, bf16[2048,512]{1,0:T(8,128)(2,1)}, u32[]{:S(2)}) copy-start(bf16[2048,512]{1,0:T(8,128)(2,1)} %gate_ref.1) | copy-start | bytes 6291460
  28.5 5.2 %collective-permute-start.4 = (f32[8,16,128]{2,1,0:T(8,128)S(1)}, f32[8,16,128]{2,1,0:T(8,128)S(1)}, u32[]{:S(2)}, u32[]{:S(2)}) collective-permute-start(f32[8,16,128]{2,1,0:T(8,128)S(1)} %get-tuple-element.67), channel_id=1, source_target_pairs={{0,16},{2,18},{4,20},{6,22},{8,24},{10,26},{12,28},{14,30},{16,0},... | collective-permute-start | bytes 196616 | tf_op jit(solution)/shard_map/ppermute | solution.py:394
  33.7 1.3 %collective-permute-start.5 = (f32[8,16,128]{2,1,0:T(8,128)S(1)}, f32[8,16,128]{2,1,0:T(8,128)S(1)}, u32[]{:S(2)}, u32[]{:S(2)}) collective-permute-start(f32[8,16,128]{2,1,0:T(8,128)S(1)} %get-tuple-element.76), channel_id=1, source_target_pairs={{0,2},{2,0},{4,6},{6,4},{8,10},{10,8},{12,14},{14,12},{16,18},{18,... | collective-permute-start | bytes 196616 | tf_op jit(solution)/shard_map/ppermute | solution.py:394

commit v9 on v8

--- a/solution.py
+++ b/solution.py
@@ -230,19 +230,20 @@
     return lax.fori_loop(0, BLOCK // LONG, turn, states)
 
 
-def local_kernel(start, mixed_ref, rates_ref, scaled_ref, bias_ref, *rest):
-    *earlier, sums_ref, states_ref = rest
+def local_kernel(units, known, kept, rim_ref, inner_ref, rates_ref, scaled_ref, bias_ref, *rest):
+    earlier, sums_refs, states_refs = rest[: len(known)], rest[len(known) :][: len(units)], rest[len(known) + len(units) :]
     modes = rates_ref.shape[0]
-    for tile in range(sums_ref.shape[0]):
+    held = {tile: tuple(ref[mode] for mode in range(modes)) for tile, ref in zip(known, earlier)}
+    for (block, tile), sums_ref in zip(units, sums_refs):
         groups = slice(tile * SUBS, (tile + 1) * SUBS)
         decay = [jnp.exp(-rates_ref[mode, groups]) for mode in range(modes)]
         scaled = [scaled_ref[mode, groups] for mode in range(modes)]
-        states = tuple(earlier[0][m, groups] if earlier else jnp.zeros((SUBS, LANES), F32) for m in range(modes))
-        states = filtered(
-            mixed_ref.at[tile], start, sums_ref.at[tile], decay, scaled, bias_ref[groups], states
-        )
+        states = held.get(tile, tuple(jnp.zeros((SUBS, LANES), F32) for _ in range(modes)))
+        source, start = (inner_ref, (block - 1) * BLOCK) if block else (rim_ref, 0)
+        held[tile] = filtered(source.at[tile], start, sums_ref, decay, scaled, bias_ref[groups], states)
+    for tile, states_ref in zip(kept, states_refs):
         for mode in range(modes):
-            states_ref[mode, groups] = states[mode]
+            states_ref[mode] = held[tile][mode]
 
 
 def half_modes(which, start_ref, rates_ref, scaled_ref, groups, past):
@@ -267,43 +268,29 @@
     return lax.fori_loop(0, BLOCK // LONG, turn, states)
 
 
-def own_carry_kernel(place_ref, rates_ref, scaled_ref, mine_ref, *sums_refs):
+def own_carry_kernel(tiles, place_ref, rates_ref, scaled_ref, mine_ref, *sums_refs):
     count = len(sums_refs) // 2
-    for tile in range(sums_refs[0].shape[0]):
+    for tile in range(tiles):
         groups = slice(tile * SUBS, (tile + 1) * SUBS)
         decay, states = half_modes(place_ref[0] % 2, mine_ref, rates_ref, scaled_ref, groups, 0)
-        for before, after in zip(sums_refs[:count], sums_refs[count:]):
-            states = add_carry(before.at[tile], after.at[tile], decay, states)
-
-
-def outer_kernel(
-    own_done, place_ref, mixed_ref, gate_ref, rates_ref, scaled_ref, bias_ref, mine_ref, twins_ref, local_ref, *rest
-):
-    *sums_refs, out_hbm, store, begin, out, sems = rest
-    modes, half = rates_ref.shape[0], mine_ref.shape[0]
+        for unit in range(tile, count, tiles):
+            states = add_carry(sums_refs[unit], sums_refs[count + unit], decay, states)
+
+
+def outer_kernel(tiles, own_done, place_ref, gate_ref, rates_ref, scaled_ref, mine_ref, twins_ref, *rest):
+    *sums_refs, out_hbm, store, out, sems = rest
     core = place_ref[0] % 2
-    begin[pl.ds(core * half, half)] = mine_ref[...]
-    begin[pl.ds((1 - core) * half, half)] = twins_ref[...]
-    blocks = len(sums_refs) + 1
-    last = (blocks - 1) * BLOCK
+    blocks = len(sums_refs) // tiles
     copies = []
-    for tile in range(mixed_ref.shape[0]):
+    for tile in range(tiles):
         groups = slice(tile * SUBS, (tile + 1) * SUBS)
         decay, states = half_modes(1 - core, twins_ref, rates_ref, scaled_ref, groups, 0)
-        for block, sums_ref in enumerate(sums_refs):
+        for block in range(blocks):
             if block == own_done:
                 more = half_modes(core, mine_ref, rates_ref, scaled_ref, groups, own_done * BLOCK)
                 decay, states = decay + more[0], states + more[1]
             into = store.at[pl.ds(block * BLOCK * SUBS, BLOCK * SUBS)]
-            states = add_carry(sums_ref.at[tile], into, decay, states)
-        decay = [jnp.exp(-rates_ref[mode, groups]) for mode in range(modes)]
-        scaled = [scaled_ref[mode, groups] for mode in range(modes)]
-        full = tuple(
-            local_ref[mode, groups] + jnp.exp(-float(last) * rates_ref[mode, groups]) * begin[mode, groups]
-            for mode in range(modes)
-        )
-        into = store.at[pl.ds(last * SUBS, BLOCK * SUBS)]
-        filtered(mixed_ref.at[tile], last - BLOCK, into, decay, scaled, bias_ref[groups], full)
+            states = add_carry(sums_refs[block * tiles + tile], into, decay, states)
         for group in range(SUBS):
             rows = slice(tile * TILE + group * LANES, tile * TILE + (group + 1) * LANES)
             for block in range(blocks):
@@ -402,61 +389,66 @@
             compiler_params=pltpu.CompilerParams(vmem_limit_bytes=8 << 20),
         )(place, rates, *arrays)
 
-    sums, states = [], []
-
-    def beside(arriving, sent):
-        block = len(sums)
-        if block >= tokens // BLOCK - 1:
+    blocks = tokens // BLOCK
+    sums, states = [], {}
+    one_tile = shape((modes, SUBS, LANES), F32)
+
+    def beside(arriving, sent, count):
+        units = [divmod(len(sums) + i, tiles) for i in range(count) if len(sums) + i < blocks * tiles]
+        if not units:
             return arriving
-        source, start = (inner_mixed, (block - 1) * BLOCK) if block else (rim_mixed, 0)
-        source, *earlier, _ = lax.optimization_barrier((source, *states[-1:], sent))
+        touched = sorted({tile for _, tile in units})
+        known = [tile for tile in touched if tile in states]
+        kept = [tile for tile in touched if (blocks - 1, tile) not in units]
+        rim, *earlier, _ = lax.optimization_barrier((rim_mixed, *(states[tile] for tile in known), sent))
         done = pl.pallas_call(
-            functools.partial(local_kernel, start),
-            in_specs=[WHOLE] * (4 + len(earlier)),
-            out_specs=[WHOLE] * 2,
-            out_shape=[shape((tiles, BLOCK * SUBS, LANES), F32), per_mode],
+            functools.partial(local_kernel, units, known, kept),
+            in_specs=[WHOLE] * (5 + len(known)),
+            out_specs=[WHOLE] * (len(units) + len(kept)),
+            out_shape=[shape((BLOCK * SUBS, LANES), F32)] * len(units) + [one_tile] * len(kept),
             compiler_params=pltpu.CompilerParams(vmem_limit_bytes=8 << 20),
             cost_estimate=pl.CostEstimate(
-                flops=channels * BLOCK * 2600, bytes_accessed=channels * BLOCK * 16, transcendentals=0
+                flops=len(units) * TILE * BLOCK * 2600, bytes_accessed=TILE * BLOCK * 16, transcendentals=0
             ),
-        )(source, rates, scaled, bias, *earlier)
-        arriving, total, state = lax.optimization_barrier((arriving, *done))
-        sums.append(total)
-        states.append(state)
+        )(rim, inner_mixed, rates, scaled, bias, *earlier)
+        arriving, *done = lax.optimization_barrier((arriving, *done))
+        sums.extend(done[: len(units)])
+        states.update(zip(kept, done[len(units) :]))
         return arriving
 
-    twin_end = swap(twin_half, 1)
+    levels = shards.bit_length() - 2
+    early = blocks * tiles // 8
+    quotas = [(blocks * tiles - early + levels - 1 - i) // levels for i in range(levels)]
+    twin_end = beside(swap(twin_half, 1), twin_half, early)
     (total,) = small(functools.partial(chip_kernel, tokens), 1, own_end, twin_end)
     ahead = jnp.zeros(half.shape, F32)
     size = 2
-    while 2 * size < shards:
-        other = beside(swap(total, size), total)
+    for quota in quotas[:-1]:
+        other = beside(swap(total, size), total, quota)
         total, ahead = small(functools.partial(level_kernel, tokens, size), 2, total, other, ahead)
         size *= 2
-    other = beside(swap(total, size), total)
+    other = beside(swap(total, size), total, quotas[-1])
     mine, twins = small(functools.partial(start_kernel, tokens, size), 2, other, ahead, own_end, twin_end)
-    while len(sums) < tokens // BLOCK - 1:
-        beside(total, total)
     twins = swap(twins, 1)
-    sums[:OWN] = pl.pallas_call(
-        own_carry_kernel,
-        in_specs=[SCALAR] + [WHOLE] * (3 + OWN),
-        out_specs=[WHOLE] * OWN,
-        out_shape=[shape(sums[0].shape, F32)] * OWN,
+    own = OWN * tiles
+    sums[:own] = pl.pallas_call(
+        functools.partial(own_carry_kernel, tiles),
+        in_specs=[SCALAR] + [WHOLE] * (3 + own),
+        out_specs=[WHOLE] * own,
+        out_shape=[shape(sums[0].shape, F32)] * own,
         compiler_params=pltpu.CompilerParams(vmem_limit_bytes=8 << 20),
         cost_estimate=pl.CostEstimate(
             flops=channels * OWN * BLOCK * 600, bytes_accessed=channels * BLOCK * 16, transcendentals=0
         ),
-    )(place, rates, scaled, mine, *sums[:OWN])
+    )(place, rates, scaled, mine, *sums[:own])
 
     hyena_out = pl.pallas_call(
-        functools.partial(outer_kernel, OWN),
-        in_specs=[SCALAR] + [WHOLE] * (8 + len(sums)),
+        functools.partial(outer_kernel, tiles, OWN),
+        in_specs=[SCALAR] + [WHOLE] * (5 + len(sums)),
         out_specs=FAR,
         out_shape=shape((channels, tokens), BF16),
         scratch_shapes=[
             steps_scratch(tokens),
-            pltpu.VMEM((modes, groups, LANES), F32),
             pltpu.VMEM((channels, tokens), BF16),
             pltpu.SemaphoreType.DMA((groups,)),
         ],
@@ -464,7 +456,7 @@
         cost_estimate=pl.CostEstimate(
             flops=channels * tokens * 50, bytes_accessed=channels * tokens * 6, transcendentals=0
         ),
-    )(place, inner_mixed, gate_two, rates, scaled, bias, mine, twins, states[-1], *sums)
+    )(place, gate_two, rates, scaled, mine, twins, *sums)
     return hyena_out[:real_channels]
 
 

time: 42 us -> 41.7 us (level)
  waiting for transfers between devices: 2.05 us -> 0.65 us
  Pallas kernels: 27.5 us -> 28.7 us
    ppermute x5, waiting for transfers between devices: 2.05 us -> 0.65 us  [swap(): lax.ppermute(array, 'seq', [(i, i ^ distance) for i in range(shards)])]
    pallas_call x5 -> x6, Pallas kernels: 14.9 us -> 16 us  [the longest x4 9.31 us: beside(): pl.pallas_call(functools.partial(local_kernel, units, known, kept), in_sp...]
  transfers between devices with their start and end apart: 6 -> 6, of which waited for: 4 -> 2; matrix products, arithmetic and copies ran while one was open for 0% -> 0% of each run, Pallas kernels for 43% -> 49%
where the time goes in v9:
time: 41.7 us; the launch traced here: 41.5 us
  Pallas kernels  28.7 us (69%)
  starting transfers between devices  11 us (26%)
  local copies, waits for them, and re-layouts  1.09 us (3%)
  waiting for transfers between devices  0.65 us (2%)
    pallas_call x1, Pallas kernels, on_device(): pl.pallas_call(functools.partial(inner_kernel, tokens * shards), in_specs...  9.7 us
    pallas_call x4, Pallas kernels, beside(): pl.pallas_call(functools.partial(local_kernel, units, known, kept), in_sp...  9.31 us
    ppermute x5, starting transfers between devices, swap(): lax.ppermute(array, 'seq', [(i, i ^ distance) for i in range(shards)])  8.62 us
    pallas_call x1, Pallas kernels, on_device(): pl.pallas_call(functools.partial(outer_kernel, tiles, OWN), in_specs=[SCA...  5.49 us
    pallas_call x1, Pallas kernels, on_device(): pl.pallas_call(functools.partial(rim_kernel, inner), in_specs=[SCALAR] +...  2.78 us
    ppermute x1, starting transfers between devices, on_device(): lax.ppermute(v_stream[:, tokens - BLOCK:], 'seq', [(i, i + 1) for i in ra...  2.39 us
    pallas_call x1, Pallas kernels, on_device(): pl.pallas_call(functools.partial(own_carry_kernel, tiles), in_specs=[SCAL...  1.19 us
    slice x1, local copies, waits for them, and re-layouts, on_device(): v_stream[:, tokens - BLOCK:]  1.08 us
  transfers between devices with their start and end apart: 6, of which 2 were waited for; matrix products, arithmetic and copies ran while one was open for 0% of the time, Pallas kernels for 49%

profile of v9, /device:TPU:0, one launch (start us, length us, event | category | flops | bytes accessed | tf_op | source)
XLA Modules:
  0.0 41.5 jit_solution(2517733108309359849)
XLA Ops:
  0.0 1.1 %slice.3 = bf16[2048,128]{1,0:T(8,128)(2,1)S(1)} slice(bf16[2048,512]{1,0:T(8,128)(2,1)} %v_hbm.1), slice={[0:2048], [384:512]} | slice | bytes 1048576 | tf_op jit(solution)/shard_map/slice | solution.py:326
  1.1 2.4 %collective-permute-start = (bf16[2048,128]{1,0:T(8,128)(2,1)S(1)}, bf16[2048,128]{1,0:T(8,128)(2,1)S(1)}, u32[]{:S(2)}, u32[]{:S(2)}) collective-permute-start(bf16[2048,128]{1,0:T(8,128)(2,1)S(1)} %slice.3), channel_id=1, source_target_pairs={{0,2},{2,4},{4,6},{6,8},{8,10},{10,12},{12,14},{14,16},{16,18},{18... | collective-permute-start | bytes 1572872 | tf_op jit(solution)/shard_map/ppermute | solution.py:326
  3.5 9.7 %shard_map.82 = (f32[2048,256]{1,0:T(8,128)S(1)}, bf16[2,3072,128]{2,1,0:T(8,128)(2,1)S(1)}, f32[16,16,128]{2,1,0:T(8,128)S(1)}, f32[16,16,128]{2,1,0:T(8,128)S(...) custom-call(bf16[2048,512]{1,0:T(8,128)(2,1)} %v_hbm.1, ...), custom_call_target="tpu_custom_call" | custom-call | flops 2044723200 | bytes 8388608 | tf_op jit(solution)/shard_map/pallas_call | solution.py:347
  13.2 0.0 collective-permute-done.before_ref
  13.2 0.0 copy-start.1
  13.2 2.8 %shard_map.83 = (bf16[2,1024,128]{2,1,0:T(8,128)(2,1)S(1)}, f32[8,16,128]{2,1,0:T(8,128)S(1)}, f32[8,16,128]{2,1,0:T(8,128)S(1)}) custom-call(s32[1]{0:T(128)} %bitcast.place_ref, bf16[2048,128]{1,0:T(8,128)(2,1)S(1)} %collective-permute-done.before_ref, bf16[2048,128]{1,0:T(8,128)(2,1)S(1)} %get-tuple-element.67.v_ref, ...), custom_call_target="tpu_custom_call" | custom-call | flops 681574400 | bytes 4194304 | tf_op jit(solution)/shard_map/pallas_call | solution.py:368
  16.0 2.7 %collective-permute-start.1 = (f32[8,16,128]{2,1,0:T(8,128)S(1)}, f32[8,16,128]{2,1,0:T(8,128)S(1)}, u32[]{:S(2)}, u32[]{:S(2)}) collective-permute-start(f32[8,16,128]{2,1,0:T(8,128)S(1)} %get-tuple-element.73), channel_id=1, source_target_pairs={{0,2},{2,0},{4,6},{6,4},{8,10},{10,8},{12,14},{14,12},{16,18},{18,... | collective-permute-start | bytes 196616 | tf_op jit(solution)/shard_map/ppermute | solution.py:381
  18.7 1.2 %shard_map.84 = (f32[1024,128]{1,0:T(8,128)S(1)}, f32[16,8,128]{2,1,0:T(8,128)S(1)}) custom-call(bf16[2,1024,128]{2,1,0:T(8,128)(2,1)S(1)} %get-tuple-element.104.rim_ref, bf16[2,3072,128]{2,1,0:T(8,128)(2,1)S(1)} %get-tuple-element.76.inner_ref, f32[16,16,128]{2,1,0:T(8,128)S(1)} %get-tuple-element.65.rates_ref, ...), custom_call_target="tpu_custom_call" | custom-call | flops 340787200 | bytes 2097152 | tf_op jit(solution)/shard_map/pallas_call | solution.py:404
  19.8 0.0 collective-permute-done.1.other_ref.twin_ref
  19.9 1.6 %collective-permute-start.2 = (f32[8,16,128]{2,1,0:T(8,128)S(1)}, f32[8,16,128]{2,1,0:T(8,128)S(1)}, u32[]{:S(2)}, u32[]{:S(2)}) collective-permute-start(f32[8,16,128]{2,1,0:T(8,128)S(1)} %shard_map.85.total_ref), channel_id=1, source_target_pairs={{0,4},{2,6},{4,0},{6,2},{8,12},{10,14},{12,8},{14,10},{16,20},{18,... | collective-permute-start | bytes 196616 | tf_op jit(solution)/shard_map/ppermute | solution.py:381
  21.5 3.5 %shard_map.86 = (f32[1024,128]{1,0:T(8,128)S(1)}, f32[1024,128]{1,0:T(8,128)S(1)}, f32[1024,128]{1,0:T(8,128)S(1)}, f32[16,8,128]{2,1,0:T(8,128)S(1)}, f32[16,8,128]{2,1,0:T(8,128)S(1)}) custom-call(bf16[2,1024,128]{2,1,0:T(8,128)(2,1)S(1)} %get-tuple-element.104.rim_ref, bf16[2,3072,128]{2,1,0:T(8,128)(2,1)S(1)} %get-tuple-element.76.inner_ref, ...), custom_call_target="tpu_custom_call" | custom-call | flops 1022361600 | bytes 2097152 | tf_op jit(solution)/shard_map/pallas_call | solution.py:404
  25.0 0.0 collective-permute-done.2.other_ref
  25.0 0.1 shard_map.87
  25.1 1.6 %collective-permute-start.3 = (f32[8,16,128]{2,1,0:T(8,128)S(1)}, f32[8,16,128]{2,1,0:T(8,128)S(1)}, u32[]{:S(2)}, u32[]{:S(2)}) collective-permute-start(f32[8,16,128]{2,1,0:T(8,128)S(1)} %get-tuple-element.89.total_ref), channel_id=1, source_target_pairs={{0,8},{2,10},{4,12},{6,14},{8,0},{10,2},{12,4},{14,6},{16,24},{18,... | collective-permute-start | bytes 196616 | tf_op jit(solution)/shard_map/ppermute | solution.py:381
  26.7 2.3 %shard_map.88 = (f32[1024,128]{1,0:T(8,128)S(1)}, f32[1024,128]{1,0:T(8,128)S(1)}, f32[16,8,128]{2,1,0:T(8,128)S(1)}, f32[16,8,128]{2,1,0:T(8,128)S(1)}) custom-call(bf16[2,1024,128]{2,1,0:T(8,128)(2,1)S(1)} %get-tuple-element.104.rim_ref, bf16[2,3072,128]{2,1,0:T(8,128)(2,1)S(1)} %get-tuple-element.76.inner_ref, ...), custom_call_target="tpu_custom_call" | custom-call | flops 681574400 | bytes 2097152 | tf_op jit(solution)/shard_map/pallas_call | solution.py:404
  29.0 0.3 collective-permute-done.3.other_ref
  29.4 0.0 copy-start
  29.4 2.7 %collective-permute-start.4 = (f32[8,16,128]{2,1,0:T(8,128)S(1)}, f32[8,16,128]{2,1,0:T(8,128)S(1)}, u32[]{:S(2)}, u32[]{:S(2)}) collective-permute-start(f32[8,16,128]{2,1,0:T(8,128)S(1)} %get-tuple-element.101), channel_id=1, source_target_pairs={{0,16},{2,18},{4,20},{6,22},{8,24},{10,26},{12,28},{14,30},{16,0},... | collective-permute-start | bytes 196616 | tf_op jit(solution)/shard_map/ppermute | solution.py:381
  32.1 2.3 %shard_map.90 = (f32[1024,128]{1,0:T(8,128)S(1)}, f32[1024,128]{1,0:T(8,128)S(1)}) custom-call(bf16[2,1024,128]{2,1,0:T(8,128)(2,1)S(1)} %get-tuple-element.104.rim_ref, bf16[2,3072,128]{2,1,0:T(8,128)(2,1)S(1)} %get-tuple-element.76.inner_ref, f32[16,16,128]{2,1,0:T(8,128)S(1)} %get-tuple-element.65.rates_ref, ...), custom_call_target="tpu_custom_call" | custom-call | flops 681574400 | bytes 2097152 | tf_op jit(solution)/shard_map/pallas_call | solution.py:404
  34.4 0.2 collective-permute-done.4.other_ref
  34.7 0.1 collective-permute-start.5
  34.8 1.2 %shard_map.92 = (f32[1024,128]{1,0:T(8,128)S(1)}, f32[1024,128]{1,0:T(8,128)S(1)}, f32[1024,128]{1,0:T(8,128)S(1)}, f32[1024,128]{1,0:T(8,128)S(1)}) custom-call(s32[1]{0:T(128)} %bitcast.place_ref, f32[16,16,128]{2,1,0:T(8,128)S(1)} %get-tuple-element.65.rates_ref, f32[16,16,128]{2,1,0:T(8,128)S(1)} %get-tuple-element.66.scaled_ref, ...), custom_call_target="tpu_custom_call" | custom-call | flops 314572800 | bytes 4194304 | tf_op jit(solution)/shard_map/pallas_call | solution.py:434
  36.0 0.0 collective-permute-done.5.twins_ref
  36.0 5.5 %shard_map.93 = bf16[2048,512]{1,0:T(8,128)(2,1)} custom-call(s32[1]{0:T(128)} %bitcast.place_ref, bf16[2048,512]{1,0:T(8,128)(2,1)S(1)} %copy-done, f32[16,16,128]{2,1,0:T(8,128)S(1)} %get-tuple-element.65.rates_ref, f32[16,16,128]{2,1,0:T(8,128)S(1)} %get-tuple-element.66.scaled_ref, f32[8,16,128]{2,1,0:T(8,128)S(1)} %get-tuple-element.111.mine_ref, ...), custom_call_target="tpu_custom_call" | custom-call | flops 52428800 | bytes 6291456 | tf_op jit(solution)/shard_map/pallas_call | solution.py:445
  (6 shorter events, 0.1 us)
Async XLA Ops:
  1.1 12.1 %collective-permute-start = (bf16[2048,128]{1,0:T(8,128)(2,1)S(1)}, bf16[2048,128]{1,0:T(8,128)(2,1)S(1)}, u32[]{:S(2)}, u32[]{:S(2)}) collective-permute-start(bf16[2048,128]{1,0:T(8,128)(2,1)S(1)} %slice.3), channel_id=1, source_target_pairs={{0,2},{2,4},{4,6},{6,8},{8,10},{10,12},{12,14},{14,16},{16,18},{18... | collective-permute-start | bytes 1572872 | tf_op jit(solution)/shard_map/ppermute | solution.py:326
  13.2 5.5 %copy-start.1 = (f32[2048]{0:T(1024)S(1)}, f32[2048]{0:T(1024)}, u32[]{:S(2)}) copy-start(f32[2048]{0:T(1024)} %param.14) | copy-start | bytes 24580
  16.0 3.8 %collective-permute-start.1 = (f32[8,16,128]{2,1,0:T(8,128)S(1)}, f32[8,16,128]{2,1,0:T(8,128)S(1)}, u32[]{:S(2)}, u32[]{:S(2)}) collective-permute-start(f32[8,16,128]{2,1,0:T(8,128)S(1)} %get-tuple-element.73), channel_id=1, source_target_pairs={{0,2},{2,0},{4,6},{6,4},{8,10},{10,8},{12,14},{14,12},{16,18},{18,... | collective-permute-start | bytes 196616 | tf_op jit(solution)/shard_map/ppermute | solution.py:381
  19.9 5.1 %collective-permute-start.2 = (f32[8,16,128]{2,1,0:T(8,128)S(1)}, f32[8,16,128]{2,1,0:T(8,128)S(1)}, u32[]{:S(2)}, u32[]{:S(2)}) collective-permute-start(f32[8,16,128]{2,1,0:T(8,128)S(1)} %shard_map.85.total_ref), channel_id=1, source_target_pairs={{0,4},{2,6},{4,0},{6,2},{8,12},{10,14},{12,8},{14,10},{16,20},{18,... | collective-permute-start | bytes 196616 | tf_op jit(solution)/shard_map/ppermute | solution.py:381
  25.1 4.3 %collective-permute-start.3 = (f32[8,16,128]{2,1,0:T(8,128)S(1)}, f32[8,16,128]{2,1,0:T(8,128)S(1)}, u32[]{:S(2)}, u32[]{:S(2)}) collective-permute-start(f32[8,16,128]{2,1,0:T(8,128)S(1)} %get-tuple-element.89.total_ref), channel_id=1, source_target_pairs={{0,8},{2,10},{4,12},{6,14},{8,0},{10,2},{12,4},{14,6},{16,24},{18,... | collective-permute-start | bytes 196616 | tf_op jit(solution)/shard_map/ppermute | solution.py:381
  29.4 6.6 %copy-start = (bf16[2048,512]{1,0:T(8,128)(2,1)S(1)}, bf16[2048,512]{1,0:T(8,128)(2,1)}, u32[]{:S(2)}) copy-start(bf16[2048,512]{1,0:T(8,128)(2,1)} %gate_ref.1) | copy-start | bytes 6291460
  29.4 5.2 %collective-permute-start.4 = (f32[8,16,128]{2,1,0:T(8,128)S(1)}, f32[8,16,128]{2,1,0:T(8,128)S(1)}, u32[]{:S(2)}, u32[]{:S(2)}) collective-permute-start(f32[8,16,128]{2,1,0:T(8,128)S(1)} %get-tuple-element.101), channel_id=1, source_target_pairs={{0,16},{2,18},{4,20},{6,22},{8,24},{10,26},{12,28},{14,30},{16,0},... | collective-permute-start | bytes 196616 | tf_op jit(solution)/shard_map/ppermute | solution.py:381
  34.7 1.3 %collective-permute-start.5 = (f32[8,16,128]{2,1,0:T(8,128)S(1)}, f32[8,16,128]{2,1,0:T(8,128)S(1)}, u32[]{:S(2)}, u32[]{:S(2)}) collective-permute-start(f32[8,16,128]{2,1,0:T(8,128)S(1)} %get-tuple-element.112), channel_id=1, source_target_pairs={{0,2},{2,0},{4,6},{6,4},{8,10},{10,8},{12,14},{14,12},{16,18},{18,... | collective-permute-start | bytes 196616 | tf_op jit(solution)/shard_map/ppermute | solution.py:381

commit v10 on v9

--- a/solution.py
+++ b/solution.py
@@ -60,9 +60,9 @@
 def apply_window(earlier, later, spectrum, tables):
     (e_re, e_im), (l_re, l_im), (h_re, h_im) = parts(earlier), parts(later), parts(spectrum)
     re, im = e_re + l_im, e_im - l_re
-    high, low = split(jnp.concatenate([re * h_re - im * h_im, re * h_im + im * h_re], axis=1))
-    both = mm(high, tables[:, BACK])
-    return both[:, :BLOCK] + both[:, BLOCK:] + mm(low, tables[:, BACK][:, :BLOCK])
+    product = jnp.concatenate([re * h_re - im * h_im, re * h_im + im * h_re], axis=1)
+    both = mm(product.astype(BF16), tables[:, BACK])
+    return both[:, :BLOCK] + both[:, BLOCK:]
 
 
 def put_mixed(store, first_row, block_at, short, gate):

time: 41.7 us -> 40.8 us (0.978)
  Pallas kernels: 28.7 us -> 27.7 us
    pallas_call x1, Pallas kernels: 9.7 us -> 8.79 us  [on_device(): pl.pallas_call(functools.partial(inner_kernel, tokens * shards), in_specs...]
  transfers between devices with their start and end apart: 6 -> 6, of which waited for: 2 -> 2; matrix products, arithmetic and copies ran while one was open for 0% -> 0% of each run, Pallas kernels for 49% -> 48%
where the time goes in v10:
time: 40.8 us; the launch traced here: 40.6 us
  Pallas kernels  27.7 us (68%)
  starting transfers between devices  11 us (27%)
  local copies, waits for them, and re-layouts  1.09 us (3%)
  waiting for transfers between devices  0.65 us (2%)
    pallas_call x4, Pallas kernels, beside(): pl.pallas_call(functools.partial(local_kernel, units, known, kept), in_sp...  9.31 us
    pallas_call x1, Pallas kernels, on_device(): pl.pallas_call(functools.partial(inner_kernel, tokens * shards), in_specs...  8.79 us
    ppermute x5, starting transfers between devices, swap(): lax.ppermute(array, 'seq', [(i, i ^ distance) for i in range(shards)])  8.62 us
    pallas_call x1, Pallas kernels, on_device(): pl.pallas_call(functools.partial(outer_kernel, tiles, OWN), in_specs=[SCA...  5.49 us
    pallas_call x1, Pallas kernels, on_device(): pl.pallas_call(functools.partial(rim_kernel, inner), in_specs=[SCALAR] +...  2.78 us
    ppermute x1, starting transfers between devices, on_device(): lax.ppermute(v_stream[:, tokens - BLOCK:], 'seq', [(i, i + 1) for i in ra...  2.39 us
    pallas_call x1, Pallas kernels, on_device(): pl.pallas_call(functools.partial(own_carry_kernel, tiles), in_specs=[SCAL...  1.19 us
    slice x1, local copies, waits for them, and re-layouts, on_device(): v_stream[:, tokens - BLOCK:]  1.08 us
  transfers between devices with their start and end apart: 6, of which 2 were waited for; matrix products, arithmetic and copies ran while one was open for 0% of the time, Pallas kernels for 48%

profile of v10, /device:TPU:0, one launch (start us, length us, event | category | flops | bytes accessed | tf_op | source)
XLA Modules:
  0.0 40.6 jit_solution(6910750061400116861)
XLA Ops:
  0.0 1.1 %slice.3 = bf16[2048,128]{1,0:T(8,128)(2,1)S(1)} slice(bf16[2048,512]{1,0:T(8,128)(2,1)} %v_hbm.1), slice={[0:2048], [384:512]} | slice | bytes 1048576 | tf_op jit(solution)/shard_map/slice | solution.py:326
  1.1 2.4 %collective-permute-start = (bf16[2048,128]{1,0:T(8,128)(2,1)S(1)}, bf16[2048,128]{1,0:T(8,128)(2,1)S(1)}, u32[]{:S(2)}, u32[]{:S(2)}) collective-permute-start(bf16[2048,128]{1,0:T(8,128)(2,1)S(1)} %slice.3), channel_id=1, source_target_pairs={{0,2},{2,4},{4,6},{6,8},{8,10},{10,12},{12,14},{14,16},{16,18},{18... | collective-permute-start | bytes 1572872 | tf_op jit(solution)/shard_map/ppermute | solution.py:326
  3.5 8.8 %shard_map.82 = (f32[2048,256]{1,0:T(8,128)S(1)}, bf16[2,3072,128]{2,1,0:T(8,128)(2,1)S(1)}, f32[16,16,128]{2,1,0:T(8,128)S(1)}, f32[16,16,128]{2,1,0:T(8,128)S(...) custom-call(bf16[2048,512]{1,0:T(8,128)(2,1)} %v_hbm.1, ...), custom_call_target="tpu_custom_call" | custom-call | flops 2044723200 | bytes 8388608 | tf_op jit(solution)/shard_map/pallas_call | solution.py:347
  12.3 0.0 collective-permute-done.before_ref
  12.3 0.0 copy-start.1
  12.3 2.8 %shard_map.83 = (bf16[2,1024,128]{2,1,0:T(8,128)(2,1)S(1)}, f32[8,16,128]{2,1,0:T(8,128)S(1)}, f32[8,16,128]{2,1,0:T(8,128)S(1)}) custom-call(s32[1]{0:T(128)} %bitcast.place_ref, bf16[2048,128]{1,0:T(8,128)(2,1)S(1)} %collective-permute-done.before_ref, bf16[2048,128]{1,0:T(8,128)(2,1)S(1)} %get-tuple-element.67.v_ref, ...), custom_call_target="tpu_custom_call" | custom-call | flops 681574400 | bytes 4194304 | tf_op jit(solution)/shard_map/pallas_call | solution.py:368
  15.1 2.7 %collective-permute-start.1 = (f32[8,16,128]{2,1,0:T(8,128)S(1)}, f32[8,16,128]{2,1,0:T(8,128)S(1)}, u32[]{:S(2)}, u32[]{:S(2)}) collective-permute-start(f32[8,16,128]{2,1,0:T(8,128)S(1)} %get-tuple-element.73), channel_id=1, source_target_pairs={{0,2},{2,0},{4,6},{6,4},{8,10},{10,8},{12,14},{14,12},{16,18},{18,... | collective-permute-start | bytes 196616 | tf_op jit(solution)/shard_map/ppermute | solution.py:381
  17.8 1.2 %shard_map.84 = (f32[1024,128]{1,0:T(8,128)S(1)}, f32[16,8,128]{2,1,0:T(8,128)S(1)}) custom-call(bf16[2,1024,128]{2,1,0:T(8,128)(2,1)S(1)} %get-tuple-element.104.rim_ref, bf16[2,3072,128]{2,1,0:T(8,128)(2,1)S(1)} %get-tuple-element.76.inner_ref, f32[16,16,128]{2,1,0:T(8,128)S(1)} %get-tuple-element.65.rates_ref, ...), custom_call_target="tpu_custom_call" | custom-call | flops 340787200 | bytes 2097152 | tf_op jit(solution)/shard_map/pallas_call | solution.py:404
  18.9 0.0 collective-permute-done.1.other_ref.twin_ref
  19.0 1.6 %collective-permute-start.2 = (f32[8,16,128]{2,1,0:T(8,128)S(1)}, f32[8,16,128]{2,1,0:T(8,128)S(1)}, u32[]{:S(2)}, u32[]{:S(2)}) collective-permute-start(f32[8,16,128]{2,1,0:T(8,128)S(1)} %shard_map.85.total_ref), channel_id=1, source_target_pairs={{0,4},{2,6},{4,0},{6,2},{8,12},{10,14},{12,8},{14,10},{16,20},{18,... | collective-permute-start | bytes 196616 | tf_op jit(solution)/shard_map/ppermute | solution.py:381
  20.6 3.5 %shard_map.86 = (f32[1024,128]{1,0:T(8,128)S(1)}, f32[1024,128]{1,0:T(8,128)S(1)}, f32[1024,128]{1,0:T(8,128)S(1)}, f32[16,8,128]{2,1,0:T(8,128)S(1)}, f32[16,8,128]{2,1,0:T(8,128)S(1)}) custom-call(bf16[2,1024,128]{2,1,0:T(8,128)(2,1)S(1)} %get-tuple-element.104.rim_ref, bf16[2,3072,128]{2,1,0:T(8,128)(2,1)S(1)} %get-tuple-element.76.inner_ref, ...), custom_call_target="tpu_custom_call" | custom-call | flops 1022361600 | bytes 2097152 | tf_op jit(solution)/shard_map/pallas_call | solution.py:404
  24.1 0.0 collective-permute-done.2.other_ref
  24.1 0.1 shard_map.87
  24.1 1.6 %collective-permute-start.3 = (f32[8,16,128]{2,1,0:T(8,128)S(1)}, f32[8,16,128]{2,1,0:T(8,128)S(1)}, u32[]{:S(2)}, u32[]{:S(2)}) collective-permute-start(f32[8,16,128]{2,1,0:T(8,128)S(1)} %get-tuple-element.89.total_ref), channel_id=1, source_target_pairs={{0,8},{2,10},{4,12},{6,14},{8,0},{10,2},{12,4},{14,6},{16,24},{18,... | collective-permute-start | bytes 196616 | tf_op jit(solution)/shard_map/ppermute | solution.py:381
  25.8 2.3 %shard_map.88 = (f32[1024,128]{1,0:T(8,128)S(1)}, f32[1024,128]{1,0:T(8,128)S(1)}, f32[16,8,128]{2,1,0:T(8,128)S(1)}, f32[16,8,128]{2,1,0:T(8,128)S(1)}) custom-call(bf16[2,1024,128]{2,1,0:T(8,128)(2,1)S(1)} %get-tuple-element.104.rim_ref, bf16[2,3072,128]{2,1,0:T(8,128)(2,1)S(1)} %get-tuple-element.76.inner_ref, ...), custom_call_target="tpu_custom_call" | custom-call | flops 681574400 | bytes 2097152 | tf_op jit(solution)/shard_map/pallas_call | solution.py:404
  28.1 0.3 collective-permute-done.3.other_ref
  28.5 0.0 copy-start
  28.5 2.7 %collective-permute-start.4 = (f32[8,16,128]{2,1,0:T(8,128)S(1)}, f32[8,16,128]{2,1,0:T(8,128)S(1)}, u32[]{:S(2)}, u32[]{:S(2)}) collective-permute-start(f32[8,16,128]{2,1,0:T(8,128)S(1)} %get-tuple-element.101), channel_id=1, source_target_pairs={{0,16},{2,18},{4,20},{6,22},{8,24},{10,26},{12,28},{14,30},{16,0},... | collective-permute-start | bytes 196616 | tf_op jit(solution)/shard_map/ppermute | solution.py:381
  31.2 2.3 %shard_map.90 = (f32[1024,128]{1,0:T(8,128)S(1)}, f32[1024,128]{1,0:T(8,128)S(1)}) custom-call(bf16[2,1024,128]{2,1,0:T(8,128)(2,1)S(1)} %get-tuple-element.104.rim_ref, bf16[2,3072,128]{2,1,0:T(8,128)(2,1)S(1)} %get-tuple-element.76.inner_ref, f32[16,16,128]{2,1,0:T(8,128)S(1)} %get-tuple-element.65.rates_ref, ...), custom_call_target="tpu_custom_call" | custom-call | flops 681574400 | bytes 2097152 | tf_op jit(solution)/shard_map/pallas_call | solution.py:404
  33.5 0.2 collective-permute-done.4.other_ref
  33.8 0.1 collective-permute-start.5
  33.9 1.2 %shard_map.92 = (f32[1024,128]{1,0:T(8,128)S(1)}, f32[1024,128]{1,0:T(8,128)S(1)}, f32[1024,128]{1,0:T(8,128)S(1)}, f32[1024,128]{1,0:T(8,128)S(1)}) custom-call(s32[1]{0:T(128)} %bitcast.place_ref, f32[16,16,128]{2,1,0:T(8,128)S(1)} %get-tuple-element.65.rates_ref, f32[16,16,128]{2,1,0:T(8,128)S(1)} %get-tuple-element.66.scaled_ref, ...), custom_call_target="tpu_custom_call" | custom-call | flops 314572800 | bytes 4194304 | tf_op jit(solution)/shard_map/pallas_call | solution.py:434
  35.1 0.0 collective-permute-done.5.twins_ref
  35.1 5.5 %shard_map.93 = bf16[2048,512]{1,0:T(8,128)(2,1)} custom-call(s32[1]{0:T(128)} %bitcast.place_ref, bf16[2048,512]{1,0:T(8,128)(2,1)S(1)} %copy-done, f32[16,16,128]{2,1,0:T(8,128)S(1)} %get-tuple-element.65.rates_ref, f32[16,16,128]{2,1,0:T(8,128)S(1)} %get-tuple-element.66.scaled_ref, f32[8,16,128]{2,1,0:T(8,128)S(1)} %get-tuple-element.111.mine_ref, ...), custom_call_target="tpu_custom_call" | custom-call | flops 52428800 | bytes 6291456 | tf_op jit(solution)/shard_map/pallas_call | solution.py:445
  (6 shorter events, 0.1 us)
Async XLA Ops:
  1.1 11.2 %collective-permute-start = (bf16[2048,128]{1,0:T(8,128)(2,1)S(1)}, bf16[2048,128]{1,0:T(8,128)(2,1)S(1)}, u32[]{:S(2)}, u32[]{:S(2)}) collective-permute-start(bf16[2048,128]{1,0:T(8,128)(2,1)S(1)} %slice.3), channel_id=1, source_target_pairs={{0,2},{2,4},{4,6},{6,8},{8,10},{10,12},{12,14},{14,16},{16,18},{18... | collective-permute-start | bytes 1572872 | tf_op jit(solution)/shard_map/ppermute | solution.py:326
  12.3 5.5 %copy-start.1 = (f32[2048]{0:T(1024)S(1)}, f32[2048]{0:T(1024)}, u32[]{:S(2)}) copy-start(f32[2048]{0:T(1024)} %param.14) | copy-start | bytes 24580
  15.1 3.8 %collective-permute-start.1 = (f32[8,16,128]{2,1,0:T(8,128)S(1)}, f32[8,16,128]{2,1,0:T(8,128)S(1)}, u32[]{:S(2)}, u32[]{:S(2)}) collective-permute-start(f32[8,16,128]{2,1,0:T(8,128)S(1)} %get-tuple-element.73), channel_id=1, source_target_pairs={{0,2},{2,0},{4,6},{6,4},{8,10},{10,8},{12,14},{14,12},{16,18},{18,... | collective-permute-start | bytes 196616 | tf_op jit(solution)/shard_map/ppermute | solution.py:381
  19.0 5.1 %collective-permute-start.2 = (f32[8,16,128]{2,1,0:T(8,128)S(1)}, f32[8,16,128]{2,1,0:T(8,128)S(1)}, u32[]{:S(2)}, u32[]{:S(2)}) collective-permute-start(f32[8,16,128]{2,1,0:T(8,128)S(1)} %shard_map.85.total_ref), channel_id=1, source_target_pairs={{0,4},{2,6},{4,0},{6,2},{8,12},{10,14},{12,8},{14,10},{16,20},{18,... | collective-permute-start | bytes 196616 | tf_op jit(solution)/shard_map/ppermute | solution.py:381
  24.1 4.3 %collective-permute-start.3 = (f32[8,16,128]{2,1,0:T(8,128)S(1)}, f32[8,16,128]{2,1,0:T(8,128)S(1)}, u32[]{:S(2)}, u32[]{:S(2)}) collective-permute-start(f32[8,16,128]{2,1,0:T(8,128)S(1)} %get-tuple-element.89.total_ref), channel_id=1, source_target_pairs={{0,8},{2,10},{4,12},{6,14},{8,0},{10,2},{12,4},{14,6},{16,24},{18,... | collective-permute-start | bytes 196616 | tf_op jit(solution)/shard_map/ppermute | solution.py:381
  28.5 6.6 %copy-start = (bf16[2048,512]{1,0:T(8,128)(2,1)S(1)}, bf16[2048,512]{1,0:T(8,128)(2,1)}, u32[]{:S(2)}) copy-start(bf16[2048,512]{1,0:T(8,128)(2,1)} %gate_ref.1) | copy-start | bytes 6291460
  28.5 5.2 %collective-permute-start.4 = (f32[8,16,128]{2,1,0:T(8,128)S(1)}, f32[8,16,128]{2,1,0:T(8,128)S(1)}, u32[]{:S(2)}, u32[]{:S(2)}) collective-permute-start(f32[8,16,128]{2,1,0:T(8,128)S(1)} %get-tuple-element.101), channel_id=1, source_target_pairs={{0,16},{2,18},{4,20},{6,22},{8,24},{10,26},{12,28},{14,30},{16,0},... | collective-permute-start | bytes 196616 | tf_op jit(solution)/shard_map/ppermute | solution.py:381
  33.8 1.3 %collective-permute-start.5 = (f32[8,16,128]{2,1,0:T(8,128)S(1)}, f32[8,16,128]{2,1,0:T(8,128)S(1)}, u32[]{:S(2)}, u32[]{:S(2)}) collective-permute-start(f32[8,16,128]{2,1,0:T(8,128)S(1)} %get-tuple-element.112), channel_id=1, source_target_pairs={{0,2},{2,0},{4,6},{6,4},{8,10},{10,8},{12,14},{14,12},{16,18},{18,... | collective-permute-start | bytes 196616 | tf_op jit(solution)/shard_map/ppermute | solution.py:381

commit v11 on v10

--- a/solution.py
+++ b/solution.py
@@ -57,12 +57,14 @@
     return image[:, :BLOCK], image[:, BLOCK:]
 
 
-def apply_window(earlier, later, spectrum, tables):
+def apply_window(earlier, later, spectrum, tables, fine=False):
     (e_re, e_im), (l_re, l_im), (h_re, h_im) = parts(earlier), parts(later), parts(spectrum)
     re, im = e_re + l_im, e_im - l_re
     product = jnp.concatenate([re * h_re - im * h_im, re * h_im + im * h_re], axis=1)
-    both = mm(product.astype(BF16), tables[:, BACK])
-    return both[:, :BLOCK] + both[:, BLOCK:]
+    high, low = split(product)
+    both = mm(high, tables[:, BACK])
+    result = both[:, :BLOCK] + both[:, BLOCK:]
+    return result + mm(low, tables[:, BACK][:, :BLOCK]) if fine else result
 
 
 def put_mixed(store, first_row, block_at, short, gate):
@@ -163,7 +165,7 @@
         groups = slice(tile * SUBS, (tile + 1) * SUBS)
         earlier = mm(twice(before_ref[rows]), tables[:, ODD])
         later = mm(twice(v_ref[rows]), tables[:, EVEN])
-        short = apply_window(earlier, later, spec_ref[rows], tables)
+        short = apply_window(earlier, later, spec_ref[rows], tables, fine=True)
         put_mixed(store, 0, 0, short, gate_ref[rows])
         rates = rates_ref.at[:, groups]
         for mode, state in enumerate(end_states(store, mixed_ref.at[tile], rates)):

time: 40.8 us -> 40.8 us (level)
  no operation moved by 1% of the time
where the time goes in v11:
time: 40.8 us; the launch traced here: 40.6 us
  Pallas kernels  27.7 us (68%)
  starting transfers between devices  11 us (27%)
  local copies, waits for them, and re-layouts  1.09 us (3%)
  waiting for transfers between devices  0.65 us (2%)
    pallas_call x4, Pallas kernels, beside(): pl.pallas_call(functools.partial(local_kernel, units, known, kept), in_sp...  9.31 us
    pallas_call x1, Pallas kernels, on_device(): pl.pallas_call(functools.partial(inner_kernel, tokens * shards), in_specs...  8.79 us
    ppermute x5, starting transfers between devices, swap(): lax.ppermute(array, 'seq', [(i, i ^ distance) for i in range(shards)])  8.62 us
    pallas_call x1, Pallas kernels, on_device(): pl.pallas_call(functools.partial(outer_kernel, tiles, OWN), in_specs=[SCA...  5.49 us
    pallas_call x1, Pallas kernels, on_device(): pl.pallas_call(functools.partial(rim_kernel, inner), in_specs=[SCALAR] +...  2.78 us
    ppermute x1, starting transfers between devices, on_device(): lax.ppermute(v_stream[:, tokens - BLOCK:], 'seq', [(i, i + 1) for i in ra...  2.39 us
    pallas_call x1, Pallas kernels, on_device(): pl.pallas_call(functools.partial(own_carry_kernel, tiles), in_specs=[SCAL...  1.19 us
    slice x1, local copies, waits for them, and re-layouts, on_device(): v_stream[:, tokens - BLOCK:]  1.08 us
  transfers between devices with their start and end apart: 6, of which 2 were waited for; matrix products, arithmetic and copies ran while one was open for 0% of the time, Pallas kernels for 48%

profile of v11, /device:TPU:0, one launch (start us, length us, event | category | flops | bytes accessed | tf_op | source)
XLA Modules:
  0.0 40.6 jit_solution(7115309961923376591)
XLA Ops:
  0.0 1.1 %slice.3 = bf16[2048,128]{1,0:T(8,128)(2,1)S(1)} slice(bf16[2048,512]{1,0:T(8,128)(2,1)} %v_hbm.1), slice={[0:2048], [384:512]} | slice | bytes 1048576 | tf_op jit(solution)/shard_map/slice | solution.py:328
  1.1 2.4 %collective-permute-start = (bf16[2048,128]{1,0:T(8,128)(2,1)S(1)}, bf16[2048,128]{1,0:T(8,128)(2,1)S(1)}, u32[]{:S(2)}, u32[]{:S(2)}) collective-permute-start(bf16[2048,128]{1,0:T(8,128)(2,1)S(1)} %slice.3), channel_id=1, source_target_pairs={{0,2},{2,4},{4,6},{6,8},{8,10},{10,12},{12,14},{14,16},{16,18},{18... | collective-permute-start | bytes 1572872 | tf_op jit(solution)/shard_map/ppermute | solution.py:328
  3.5 8.8 %shard_map.82 = (f32[2048,256]{1,0:T(8,128)S(1)}, bf16[2,3072,128]{2,1,0:T(8,128)(2,1)S(1)}, f32[16,16,128]{2,1,0:T(8,128)S(1)}, f32[16,16,128]{2,1,0:T(8,128)S(...) custom-call(bf16[2048,512]{1,0:T(8,128)(2,1)} %v_hbm.1, ...), custom_call_target="tpu_custom_call" | custom-call | flops 2044723200 | bytes 8388608 | tf_op jit(solution)/shard_map/pallas_call | solution.py:349
  12.3 0.0 collective-permute-done.before_ref
  12.3 0.0 copy-start.1
  12.3 2.8 %shard_map.83 = (bf16[2,1024,128]{2,1,0:T(8,128)(2,1)S(1)}, f32[8,16,128]{2,1,0:T(8,128)S(1)}, f32[8,16,128]{2,1,0:T(8,128)S(1)}) custom-call(s32[1]{0:T(128)} %bitcast.place_ref, bf16[2048,128]{1,0:T(8,128)(2,1)S(1)} %collective-permute-done.before_ref, bf16[2048,128]{1,0:T(8,128)(2,1)S(1)} %get-tuple-element.67.v_ref, ...), custom_call_target="tpu_custom_call" | custom-call | flops 681574400 | bytes 4194304 | tf_op jit(solution)/shard_map/pallas_call | solution.py:370
  15.1 2.7 %collective-permute-start.1 = (f32[8,16,128]{2,1,0:T(8,128)S(1)}, f32[8,16,128]{2,1,0:T(8,128)S(1)}, u32[]{:S(2)}, u32[]{:S(2)}) collective-permute-start(f32[8,16,128]{2,1,0:T(8,128)S(1)} %get-tuple-element.73), channel_id=1, source_target_pairs={{0,2},{2,0},{4,6},{6,4},{8,10},{10,8},{12,14},{14,12},{16,18},{18,... | collective-permute-start | bytes 196616 | tf_op jit(solution)/shard_map/ppermute | solution.py:383
  17.8 1.2 %shard_map.84 = (f32[1024,128]{1,0:T(8,128)S(1)}, f32[16,8,128]{2,1,0:T(8,128)S(1)}) custom-call(bf16[2,1024,128]{2,1,0:T(8,128)(2,1)S(1)} %get-tuple-element.104.rim_ref, bf16[2,3072,128]{2,1,0:T(8,128)(2,1)S(1)} %get-tuple-element.76.inner_ref, f32[16,16,128]{2,1,0:T(8,128)S(1)} %get-tuple-element.65.rates_ref, ...), custom_call_target="tpu_custom_call" | custom-call | flops 340787200 | bytes 2097152 | tf_op jit(solution)/shard_map/pallas_call | solution.py:406
  18.9 0.0 collective-permute-done.1.other_ref.twin_ref
  19.0 1.6 %collective-permute-start.2 = (f32[8,16,128]{2,1,0:T(8,128)S(1)}, f32[8,16,128]{2,1,0:T(8,128)S(1)}, u32[]{:S(2)}, u32[]{:S(2)}) collective-permute-start(f32[8,16,128]{2,1,0:T(8,128)S(1)} %shard_map.85.total_ref), channel_id=1, source_target_pairs={{0,4},{2,6},{4,0},{6,2},{8,12},{10,14},{12,8},{14,10},{16,20},{18,... | collective-permute-start | bytes 196616 | tf_op jit(solution)/shard_map/ppermute | solution.py:383
  20.6 3.5 %shard_map.86 = (f32[1024,128]{1,0:T(8,128)S(1)}, f32[1024,128]{1,0:T(8,128)S(1)}, f32[1024,128]{1,0:T(8,128)S(1)}, f32[16,8,128]{2,1,0:T(8,128)S(1)}, f32[16,8,128]{2,1,0:T(8,128)S(1)}) custom-call(bf16[2,1024,128]{2,1,0:T(8,128)(2,1)S(1)} %get-tuple-element.104.rim_ref, bf16[2,3072,128]{2,1,0:T(8,128)(2,1)S(1)} %get-tuple-element.76.inner_ref, ...), custom_call_target="tpu_custom_call" | custom-call | flops 1022361600 | bytes 2097152 | tf_op jit(solution)/shard_map/pallas_call | solution.py:406
  24.1 0.0 collective-permute-done.2.other_ref
  24.1 0.1 shard_map.87
  24.1 1.6 %collective-permute-start.3 = (f32[8,16,128]{2,1,0:T(8,128)S(1)}, f32[8,16,128]{2,1,0:T(8,128)S(1)}, u32[]{:S(2)}, u32[]{:S(2)}) collective-permute-start(f32[8,16,128]{2,1,0:T(8,128)S(1)} %get-tuple-element.89.total_ref), channel_id=1, source_target_pairs={{0,8},{2,10},{4,12},{6,14},{8,0},{10,2},{12,4},{14,6},{16,24},{18,... | collective-permute-start | bytes 196616 | tf_op jit(solution)/shard_map/ppermute | solution.py:383
  25.8 2.3 %shard_map.88 = (f32[1024,128]{1,0:T(8,128)S(1)}, f32[1024,128]{1,0:T(8,128)S(1)}, f32[16,8,128]{2,1,0:T(8,128)S(1)}, f32[16,8,128]{2,1,0:T(8,128)S(1)}) custom-call(bf16[2,1024,128]{2,1,0:T(8,128)(2,1)S(1)} %get-tuple-element.104.rim_ref, bf16[2,3072,128]{2,1,0:T(8,128)(2,1)S(1)} %get-tuple-element.76.inner_ref, ...), custom_call_target="tpu_custom_call" | custom-call | flops 681574400 | bytes 2097152 | tf_op jit(solution)/shard_map/pallas_call | solution.py:406
  28.1 0.3 collective-permute-done.3.other_ref
  28.5 0.0 copy-start
  28.5 2.7 %collective-permute-start.4 = (f32[8,16,128]{2,1,0:T(8,128)S(1)}, f32[8,16,128]{2,1,0:T(8,128)S(1)}, u32[]{:S(2)}, u32[]{:S(2)}) collective-permute-start(f32[8,16,128]{2,1,0:T(8,128)S(1)} %get-tuple-element.101), channel_id=1, source_target_pairs={{0,16},{2,18},{4,20},{6,22},{8,24},{10,26},{12,28},{14,30},{16,0},... | collective-permute-start | bytes 196616 | tf_op jit(solution)/shard_map/ppermute | solution.py:383
  31.2 2.3 %shard_map.90 = (f32[1024,128]{1,0:T(8,128)S(1)}, f32[1024,128]{1,0:T(8,128)S(1)}) custom-call(bf16[2,1024,128]{2,1,0:T(8,128)(2,1)S(1)} %get-tuple-element.104.rim_ref, bf16[2,3072,128]{2,1,0:T(8,128)(2,1)S(1)} %get-tuple-element.76.inner_ref, f32[16,16,128]{2,1,0:T(8,128)S(1)} %get-tuple-element.65.rates_ref, ...), custom_call_target="tpu_custom_call" | custom-call | flops 681574400 | bytes 2097152 | tf_op jit(solution)/shard_map/pallas_call | solution.py:406
  33.5 0.2 collective-permute-done.4.other_ref
  33.8 0.1 collective-permute-start.5
  33.9 1.2 %shard_map.92 = (f32[1024,128]{1,0:T(8,128)S(1)}, f32[1024,128]{1,0:T(8,128)S(1)}, f32[1024,128]{1,0:T(8,128)S(1)}, f32[1024,128]{1,0:T(8,128)S(1)}) custom-call(s32[1]{0:T(128)} %bitcast.place_ref, f32[16,16,128]{2,1,0:T(8,128)S(1)} %get-tuple-element.65.rates_ref, f32[16,16,128]{2,1,0:T(8,128)S(1)} %get-tuple-element.66.scaled_ref, ...), custom_call_target="tpu_custom_call" | custom-call | flops 314572800 | bytes 4194304 | tf_op jit(solution)/shard_map/pallas_call | solution.py:436
  35.1 0.0 collective-permute-done.5.twins_ref
  35.1 5.5 %shard_map.93 = bf16[2048,512]{1,0:T(8,128)(2,1)} custom-call(s32[1]{0:T(128)} %bitcast.place_ref, bf16[2048,512]{1,0:T(8,128)(2,1)S(1)} %copy-done, f32[16,16,128]{2,1,0:T(8,128)S(1)} %get-tuple-element.65.rates_ref, f32[16,16,128]{2,1,0:T(8,128)S(1)} %get-tuple-element.66.scaled_ref, f32[8,16,128]{2,1,0:T(8,128)S(1)} %get-tuple-element.111.mine_ref, ...), custom_call_target="tpu_custom_call" | custom-call | flops 52428800 | bytes 6291456 | tf_op jit(solution)/shard_map/pallas_call | solution.py:447
  (6 shorter events, 0.1 us)
Async XLA Ops:
  1.1 11.2 %collective-permute-start = (bf16[2048,128]{1,0:T(8,128)(2,1)S(1)}, bf16[2048,128]{1,0:T(8,128)(2,1)S(1)}, u32[]{:S(2)}, u32[]{:S(2)}) collective-permute-start(bf16[2048,128]{1,0:T(8,128)(2,1)S(1)} %slice.3), channel_id=1, source_target_pairs={{0,2},{2,4},{4,6},{6,8},{8,10},{10,12},{12,14},{14,16},{16,18},{18... | collective-permute-start | bytes 1572872 | tf_op jit(solution)/shard_map/ppermute | solution.py:328
  12.3 5.5 %copy-start.1 = (f32[2048]{0:T(1024)S(1)}, f32[2048]{0:T(1024)}, u32[]{:S(2)}) copy-start(f32[2048]{0:T(1024)} %param.14) | copy-start | bytes 24580
  15.1 3.8 %collective-permute-start.1 = (f32[8,16,128]{2,1,0:T(8,128)S(1)}, f32[8,16,128]{2,1,0:T(8,128)S(1)}, u32[]{:S(2)}, u32[]{:S(2)}) collective-permute-start(f32[8,16,128]{2,1,0:T(8,128)S(1)} %get-tuple-element.73), channel_id=1, source_target_pairs={{0,2},{2,0},{4,6},{6,4},{8,10},{10,8},{12,14},{14,12},{16,18},{18,... | collective-permute-start | bytes 196616 | tf_op jit(solution)/shard_map/ppermute | solution.py:383
  19.0 5.1 %collective-permute-start.2 = (f32[8,16,128]{2,1,0:T(8,128)S(1)}, f32[8,16,128]{2,1,0:T(8,128)S(1)}, u32[]{:S(2)}, u32[]{:S(2)}) collective-permute-start(f32[8,16,128]{2,1,0:T(8,128)S(1)} %shard_map.85.total_ref), channel_id=1, source_target_pairs={{0,4},{2,6},{4,0},{6,2},{8,12},{10,14},{12,8},{14,10},{16,20},{18,... | collective-permute-start | bytes 196616 | tf_op jit(solution)/shard_map/ppermute | solution.py:383
  24.1 4.3 %collective-permute-start.3 = (f32[8,16,128]{2,1,0:T(8,128)S(1)}, f32[8,16,128]{2,1,0:T(8,128)S(1)}, u32[]{:S(2)}, u32[]{:S(2)}) collective-permute-start(f32[8,16,128]{2,1,0:T(8,128)S(1)} %get-tuple-element.89.total_ref), channel_id=1, source_target_pairs={{0,8},{2,10},{4,12},{6,14},{8,0},{10,2},{12,4},{14,6},{16,24},{18,... | collective-permute-start | bytes 196616 | tf_op jit(solution)/shard_map/ppermute | solution.py:383
  28.5 6.6 %copy-start = (bf16[2048,512]{1,0:T(8,128)(2,1)S(1)}, bf16[2048,512]{1,0:T(8,128)(2,1)}, u32[]{:S(2)}) copy-start(bf16[2048,512]{1,0:T(8,128)(2,1)} %gate_ref.1) | copy-start | bytes 6291460
  28.5 5.2 %collective-permute-start.4 = (f32[8,16,128]{2,1,0:T(8,128)S(1)}, f32[8,16,128]{2,1,0:T(8,128)S(1)}, u32[]{:S(2)}, u32[]{:S(2)}) collective-permute-start(f32[8,16,128]{2,1,0:T(8,128)S(1)} %get-tuple-element.101), channel_id=1, source_target_pairs={{0,16},{2,18},{4,20},{6,22},{8,24},{10,26},{12,28},{14,30},{16,0},... | collective-permute-start | bytes 196616 | tf_op jit(solution)/shard_map/ppermute | solution.py:383
  33.8 1.3 %collective-permute-start.5 = (f32[8,16,128]{2,1,0:T(8,128)S(1)}, f32[8,16,128]{2,1,0:T(8,128)S(1)}, u32[]{:S(2)}, u32[]{:S(2)}) collective-permute-start(f32[8,16,128]{2,1,0:T(8,128)S(1)} %get-tuple-element.112), channel_id=1, source_target_pairs={{0,2},{2,0},{4,6},{6,4},{8,10},{10,8},{12,14},{14,12},{16,18},{18,... | collective-permute-start | bytes 196616 | tf_op jit(solution)/shard_map/ppermute | solution.py:383
